TPU v7x, 512 devices: a whole 4x8x8 slice. The times are simulated.
512 devices in a mesh: grp: 32 (over x, z), vocab: 16 (over y, core).
Axes of the slice: x: 4, y: 8, z: 8, core: 2. Of those that a mesh axis runs over, the one named last changes fastest.
Arguments:
- inner_x: bfloat16 [8192, 4096], P('grp', 'vocab'), may hold values from -6 to 6
- gate_z: bfloat16 [8192, 4096], P('grp', 'vocab'), may hold values from -6 to 6
- state_b: bfloat16 [8192, 128], P('grp'), may hold values from -6 to 6
- state_c: bfloat16 [8192, 128], P('grp'), may hold values from -6 to 6
- step_raw: float32 [64, 8192], P('vocab', 'grp'), may hold values from -6 to 6
- decay_log: float32 [64], P('vocab'), may hold values from 0 to 2.77
- step_bias: float32 [64], P('vocab'), may hold values from -7 to -2.3
- skip_gain: float32 [64], P('vocab'), may hold values from 0.5 to 1.5
- norm_gain: float32 [4096], P('vocab'), may hold values from 0.5 to 1.5
- out_weight: bfloat16 [4096, 2048], P('vocab'), may hold values from -0.09375 to 0.09375
- residual: bfloat16 [8192, 2048], P('grp'), may hold values from -6 to 6
- ref_hidden: bfloat16 [8192, 2048], P('grp'), may hold values from -6 to 6
- policy_gain: float32 [2048], replicated, may hold values from 0.5 to 1.5
- ref_gain: float32 [2048], replicated, may hold values from 0.5 to 1.5
- policy_head: bfloat16 [2048, 25216], P('grp', 'vocab')
- ref_head: bfloat16 [2048, 25216], P('grp', 'vocab')
- saved_pages: bfloat16 [128, 4096, 128], P('grp', 'vocab'), may hold values from -0.5 to 0.5
- lengths: int32 [32, 16], P('grp'), may hold values from 1 to 96, 256 in all within a row
- page_owner: int32 [32, 16], replicated, may hold values from 0 to 31, as said below
- page_slot: int32 [32, 16], replicated, may hold values from 0 to 3
- resumed: int32 [32, 16], P('grp'), may hold values 0 or 1
- targets: int32 [8192], P('grp'), may hold values from 0 to 25215
Outputs:
- logprobs: float32 [2, 8192], P(None, 'grp')
- request_sums: float32 [2, 512], P(None, 'grp')
Inputs may be any that keep to these rules, and one draw needn't show every extreme that they name: Each group's lengths sum to 256, and its largest is 96. `page_owner`: the 16 requests of one group name 16 different owner groups.
All inputs are finite; a program needn't handle non-finite values. No bound on the sum of `resumed` on one device may be relied on, other than what follows from the above.
Results may differ from a plain program's by a relative error of at most 0.0011.
Values may be sent and summed in bfloat16 or wider, within the bound.
No kernel may reach another device: no remote copies, remote signals or barrier semaphores. Data moves between devices by JAX's collectives and lax.ppermute only.
A program may use at most 64 MiB of HBM per device.

v0:
```python
import jax
import jax.numpy as jnp
from jax import lax
from jax.sharding import PartitionSpec as P

INNER = 4096


precise = lax.Precision.HIGHEST
epsilon = 1e-05


def from_behind(x, axis, by):
    count = lax.axis_size(axis)
    pairs = [(i, i + by) for i in range(count) if 0 <= i + by < count]
    return lax.ppermute(x, axis, pairs)


def prepare(step_raw, decay_log, step_bias, length_row):
    tok_count = step_raw.shape[1]
    step_size = jax.nn.softplus(step_raw + step_bias[:, None])
    log_decay = -jnp.exp(decay_log)[:, None] * step_size
    cumulative = jnp.cumsum(log_decay, axis=1)
    before = cumulative - log_decay
    ends = jnp.cumsum(length_row)
    starts = ends - length_row
    position = jnp.arange(tok_count, dtype=jnp.int32)
    member = jnp.logical_and(
        position[:, None] >= starts[None, :], position[:, None] < ends[None, :]
    ).astype(jnp.float32)
    at_start = jnp.take(before, starts, axis=1)
    start_tok = jnp.dot(at_start, member.T, precision=precise)
    same_req = jnp.dot(member, member.T, precision=precise) > 0.5
    causal = jnp.logical_and(position[:, None] >= position[None, :], same_req)
    return (step_size, cumulative, before, member, start_tok, causal, starts)


def intra_outputs(inner_x, state_b, state_c, step_size, cumulative, causal, head_count):
    tok_count = inner_x.shape[0]
    scores = jnp.dot(state_c, state_b.T, preferred_element_type=jnp.float32)
    gap_val = jnp.where(causal[None], cumulative[:, :, None] - cumulative[:, None, :], 0.0)
    mixing = jnp.where(causal[None], jnp.exp(gap_val), 0.0) * scores[None] * step_size[:, None, :]
    mixing = mixing.astype(jnp.bfloat16)
    values = inner_x.reshape(tok_count, head_count, -1)
    return jnp.einsum("hts,shp->thp", mixing, values, preferred_element_type=jnp.float32)


def final_state(
    inner_x, state_b, step_size, cumulative, before, member, starts, init_last, head_count
):
    tok_count = inner_x.shape[0]
    last_col = member[:, -1]
    final_cum = cumulative[:, -1]
    inside = last_col[None, :] > 0.5
    weight = jnp.where(
        inside, jnp.exp(jnp.where(inside, final_cum[:, None] - cumulative, 0.0)) * step_size, 0.0
    )
    scaled = inner_x.astype(jnp.float32).reshape(tok_count, head_count, -1) * weight.T[:, :, None]
    summed = jnp.dot(
        scaled.reshape(tok_count, -1).T, state_b.astype(jnp.float32), precision=precise
    )
    kept = jnp.exp(final_cum - before[:, starts[-1]])
    return summed.reshape(init_last.shape) + kept[:, None, None] * init_last


def start_outputs(state_c, init_states, member, cumulative, start_tok):
    requests, head_count, head_width, state_width = init_states.shape
    tok_count = state_c.shape[0]
    flat_init = init_states.reshape(-1, state_width)
    project = jnp.einsum("tn,kn->tk", state_c.astype(jnp.float32), flat_init, precision=precise)
    project = project.reshape(tok_count, requests, head_count * head_width)
    picked = jnp.einsum("trk,tr->tk", project, member, precision=precise)
    decay_tok = jnp.exp(cumulative - start_tok).T
    return picked.reshape(tok_count, head_count, head_width) * decay_tok[:, :, None]


def gate_terms(inner_x, gate_z, skip_gain, norm_gain, intra_out, start_out, head_count):
    tok_count = inner_x.shape[0]
    values = inner_x.astype(jnp.float32).reshape(tok_count, head_count, -1)
    mixed = intra_out + start_out + skip_gain[None, :, None] * values
    gated = mixed.reshape(tok_count, -1) * jax.nn.silu(gate_z.astype(jnp.float32))
    squares = jnp.sum(gated * gated, axis=1)
    weighted = (gated * norm_gain[None, :]).astype(jnp.bfloat16)
    return (weighted, squares)


def final_norm(hidden, gain_row):
    factor = lax.rsqrt(jnp.mean(hidden * hidden, axis=1) + epsilon)
    return (hidden * factor[:, None] * gain_row[None, :]).astype(jnp.bfloat16)


def add_rows(normed, piece):
    return jnp.dot(normed, piece, preferred_element_type=jnp.float32)


def body(
    inner_x,
    gate_z,
    state_b,
    state_c,
    step_raw,
    decay_log,
    step_bias,
    skip_gain,
    norm_gain,
    out_weight,
    residual,
    ref_hidden,
    policy_gain,
    ref_gain,
    policy_head,
    ref_head,
    saved_pages,
    lengths,
    page_owner,
    page_slot,
    resumed,
    targets,
):
    head_count = step_raw.shape[0]
    my_group = lax.axis_index("grp")
    length_row = lengths[0]
    resume_row = resumed[0].astype(jnp.float32)
    matched = page_owner == my_group
    send_slot = jnp.sum(jnp.where(matched, page_slot, 0), axis=1)
    outgoing = jnp.take(saved_pages, send_slot, axis=0)
    incoming = lax.all_to_all(outgoing, "grp", split_axis=0, concat_axis=0, tiled=True)
    own_owner = lax.dynamic_index_in_dim(page_owner, my_group, 0, keepdims=False)
    fetched = jnp.take(incoming, own_owner, axis=0).astype(jnp.float32)
    requests = fetched.shape[0]
    fetched = (
        fetched.reshape(requests, head_count, -1, fetched.shape[-1])
        * resume_row[:, None, None, None]
    )
    step_size, cumulative, before, member, start_tok, causal, starts = prepare(
        step_raw, decay_log, step_bias, length_row
    )
    intra_out = intra_outputs(inner_x, state_b, state_c, step_size, cumulative, causal, head_count)
    ending = final_state(
        inner_x, state_b, step_size, cumulative, before, member, starts, fetched[-1], head_count
    )
    carried = from_behind(ending, "grp", 1)
    has_carry = my_group >= 1
    first_state = jnp.where(has_carry, carried, fetched[0])
    init_states = jnp.concatenate([first_state[None], fetched[1:]], axis=0)
    start_out = start_outputs(state_c, init_states, member, cumulative, start_tok)
    weighted, squares = gate_terms(
        inner_x, gate_z, skip_gain, norm_gain, intra_out, start_out, head_count
    )
    partial_value = jnp.dot(weighted, out_weight, preferred_element_type=jnp.float32)
    partial_value, squares = lax.psum((partial_value, squares), "vocab")
    hidden = (
        residual.astype(jnp.float32) + partial_value * lax.rsqrt(squares / INNER + epsilon)[:, None]
    )
    policy_normed = final_norm(hidden, policy_gain)
    ref_normed = final_norm(ref_hidden.astype(jnp.float32), ref_gain)
    vocab_local = policy_head.shape[1]
    policy_logits = add_rows(policy_normed, lax.all_gather(policy_head, "grp", axis=0, tiled=True))
    ref_logits = add_rows(ref_normed, lax.all_gather(ref_head, "grp", axis=0, tiled=True))
    vocab_start = lax.axis_index("vocab") * vocab_local
    columns_id = jnp.arange(vocab_local, dtype=jnp.int32)[None, :] + vocab_start
    hit_mask = columns_id == targets[:, None]
    policy_top = jnp.max(policy_logits, axis=1)
    ref_top = jnp.max(ref_logits, axis=1)
    policy_top, ref_top = lax.pmax((policy_top, ref_top), "vocab")
    policy_total = jnp.sum(jnp.exp(policy_logits - policy_top[:, None]), axis=1)
    ref_total = jnp.sum(jnp.exp(ref_logits - ref_top[:, None]), axis=1)
    policy_pick = jnp.sum(jnp.where(hit_mask, policy_logits, 0.0), axis=1)
    ref_pick = jnp.sum(jnp.where(hit_mask, ref_logits, 0.0), axis=1)
    policy_total, ref_total, policy_pick, ref_pick = lax.psum(
        (policy_total, ref_total, policy_pick, ref_pick), "vocab"
    )
    policy_lp = policy_pick - (policy_top + jnp.log(policy_total))
    ref_lp = ref_pick - (ref_top + jnp.log(ref_total))
    logprobs = jnp.stack([policy_lp, ref_lp])
    paired = jnp.stack([policy_lp, policy_lp - ref_lp])
    request_sums = jnp.dot(paired, member, precision=precise)
    return (logprobs, request_sums)


def solution(mesh):
    in_specs = (
        P("grp", "vocab"),
        P("grp", "vocab"),
        P("grp", None),
        P("grp", None),
        P("vocab", "grp"),
        P("vocab"),
        P("vocab"),
        P("vocab"),
        P("vocab"),
        P("vocab", None),
        P("grp", None),
        P("grp", None),
        P(),
        P(),
        P("grp", "vocab"),
        P("grp", "vocab"),
        P("grp", "vocab", None),
        P("grp", None),
        P(),
        P(),
        P("grp", None),
        P("grp"),
    )
    out_specs = (P(None, "grp"), P(None, "grp"))
    return jax.shard_map(body, mesh=mesh, in_specs=in_specs, out_specs=out_specs, check_vma=False)
```

profile of v0, /device:TPU:1, one launch (start us, length us, event | category | flops | bytes accessed | tf_op | source)
XLA Modules:
  0.0 356.1 jit_solution(7010211466037685944)
XLA Ops:
  8.9 1.9 gather_fusion
  10.8 1.6 broadcast_select_fusion
  12.4 13.9 %all-to-all-start = ((bf16[32,256,128]{2,1,0:T(8,128)(2,1)}), bf16[32,256,128]{2,1,0:T(8,128)(2,1)S(1)}, u32[]{:S(2)}, u32[]{:S(2)}) async-start(bf16[32,256,128]{2,1,0:T(8,128)(2,1)} %broadcast_select_fusion), calls=%async_computation | async-start | bytes 4194304 | tf_op jit(solution)/shard_map/all_to_all | solution.py:127
  26.6 1.2 reduce-window.11
  35.1 2.0 gather_fusion.2
  38.2 1.2 subtract_exponential_fusion
  39.4 1.7 fusion.7
  41.1 1.8 fusion.55
  42.9 32.3 %all-to-all-done = bf16[32,256,128]{2,1,0:T(8,128)(2,1)S(1)} async-done(((bf16[32,256,128]{2,1,0:T(8,128)(2,1)}), bf16[32,256,128]{2,1,0:T(8,128)(2,1)S(1)}, u32[]{:S(2)}, u32[]{:S(2)}) %all-to-all-start) | async-done | bytes 2097184 | tf_op jit(solution)/shard_map/all_to_all | solution.py:127
  75.2 1.7 gather_fusion.1
  76.9 1.7 convert_multiply_fusion.2
  78.9 4.0 %collective-permute-start = (f32[4,64,128]{2,1,0:T(8,128)S(1)}, f32[4,64,128]{2,1,0:T(8,128)S(1)}, u32[]{:S(2)}, u32[]{:S(2)}) collective-permute-start(f32[4,64,128]{2,1,0:T(8,128)S(1)} %convolution_add_fusion), channel_id=1, source_target_pairs={{0,16},{16,32},{32,48},{48,64},{64,80},{80,96},{96,112},{112,128},... | collective-permute-start | bytes 393224 | tf_op jit(solution)/shard_map/ppermute | solution.py:16
  83.4 1.8 collective-permute-done
  86.1 1.8 fusion.56
  89.5 1.8 fusion.28
  93.0 25.1 %psum.43 = f32[256]{0:T(256)S(1)} all-reduce(f32[256]{0:T(256)S(1)} %multiply_reduce_fusion.2), channel_id=1, replica_groups=mesh['grp'=32,'vocab'=16] {'vocab'}, use_global_device_ids=true, to_apply=%region_6.7 | all-reduce | flops 256 | bytes 2048 | tf_op jit(solution)/shard_map/psum | solution.py:151
  118.1 95.6 %all-reduce.4.cloned.1.call-done = f32[256,2048]{1,0:T(8,128)} async-done(((f32[256,2048]{1,0:T(8,128)}), f32[256,2048]{1,0:T(8,128)}) %all-reduce.4.cloned.1.call-update) | async-done | bytes 2097168 | tf_op jit(solution)/shard_map/psum | solution.py:151
  213.7 2.5 multiply_reduce_fusion.1
  216.3 7.3 %fusion.53 = (f32[256]{0:T(256)S(1)}, f32[256,1576]{0,1:T(8,128)}) fusion(bf16[2048,1576]{1,0:T(8,128)(2,1)} %all-gather.3.cloned.1.call-done, f32[256,2048]{1,0:T(8,128)S(1)} %copy-done.1, bf16[256,2048]{1,0:T(8,128)(2,1)} %param.32, f32[2048]{0:T(1024)S(1)} %copy-done.29, f32[256]{0:T(256)S(1)} %add_rsqrt_fusion.1, f32[256]{0:T(256)S(1)} %add_rsqrt_fusion.2), kind=kOutput, calls=%fused_computation.115 | convolution fusion | flops 1656104704 | bytes 11226112 | tf_op jit(solution)/shard_map/dot_general | solution.py:93
  223.6 64.9 %all-gather.5.cloned.1.call-done = bf16[2048,1576]{1,0:T(8,128)(2,1)} async-done(((bf16[64,1576]{1,0:T(8,128)(2,1)}), bf16[2048,1576]{1,0:T(8,128)(2,1)}) %all-gather.5.cloned.1.call-update) | async-done | bytes 6455312 | tf_op jit(solution)/shard_map/all_gather | solution.py:159
  288.5 7.2 %fusion.54 = (f32[256]{0:T(256)S(1)}, f32[256,1576]{0,1:T(8,128)}) fusion(bf16[2048,1576]{1,0:T(8,128)(2,1)} %all-gather.5.cloned.1.call-done, bf16[256,2048]{1,0:T(8,128)(2,1)} %param.33, f32[2048]{0:T(1024)S(1)} %copy-done.30, f32[256]{0:T(256)S(1)} %add_rsqrt_fusion), kind=kOutput, calls=%fused_computation.116 | convolution fusion | flops 1655056128 | bytes 9127936 | tf_op jit(solution)/shard_map/dot_general | solution.py:93
  295.7 23.9 %all-reduce.1 = (f32[256]{0:T(256)S(1)}, f32[256]{0:T(256)S(1)}) all-reduce(f32[256]{0:T(256)S(1)} %get-tuple-element.27, f32[256]{0:T(256)S(1)} %get-tuple-element.29), channel_id=1, replica_groups=mesh['grp'=32,'vocab'=16] {'vocab'}, use_global_device_ids=true, to_apply=%region_11.12 | all-reduce | flops 512 | bytes 4096 | tf_op jit(solution)/shard_map/pmax | solution.py:165
  319.6 2.2 exponential_reduce_fusion
  321.9 25.5 %all-reduce = (f32[256]{0:T(256)S(1)}, f32[256]{0:T(256)S(1)}, f32[256]{0:T(256)S(1)}, f32[256]{0:T(256)S(1)}) all-reduce(f32[256]{0:T(256)S(1)} %get-tuple-element.21, f32[256]{0:T(256)S(1)} %get-tuple-element.22, f32[256]{0:T(256)S(1)} %get-tuple-element.3, f32[256]{0:T(256)S(1)} %get-tuple-element.2), channel_id=1, replica_groups=mesh['grp'=32,'vocab'=16] {'vocab'}, use_global_device_ids=true, to_apply=%region_9.10 | all-reduce | flops 1024 | bytes 8192 | tf_op jit(solution)/shard_map/psum | solution.py:170
  (126 shorter events, 13.9 us)
Async XLA Ops:
  8.0 81.5 %copy-start = (bf16[256,2048]{1,0:T(8,128)(2,1)S(1)}, bf16[256,2048]{1,0:T(8,128)(2,1)}, u32[]{:S(2)}) copy-start(bf16[256,2048]{1,0:T(8,128)(2,1)} %param.31) | copy-start | bytes 3145732
  12.4 14.0 %copy-start.19 = (s32[1,16]{1,0:T(1,128)S(1)}, s32[1,16]{1,0:T(1,128)}, u32[]{:S(2)}) copy-start(s32[1,16]{1,0:T(1,128)} %param.39) | copy-start | bytes 196
  12.4 14.1 %copy-start.31 = (f32[4]{0:T(128)S(1)}, f32[4]{0:T(128)}, u32[]{:S(2)}) copy-start(f32[4]{0:T(128)} %param.27) | copy-start | bytes 52
  12.4 14.1 %copy-start.17 = (f32[4,256]{1,0:T(4,128)S(1)}, f32[4,256]{1,0:T(4,128)}, u32[]{:S(2)}) copy-start(f32[4,256]{1,0:T(4,128)} %param.26) | copy-start | bytes 12292
  12.4 14.1 %copy-start.27 = (f32[4]{0:T(128)S(1)}, f32[4]{0:T(128)}, u32[]{:S(2)}) copy-start(f32[4]{0:T(128)} %param.28) | copy-start | bytes 52
  12.4 21.9 %copy-start.8 = (bf16[256,256]{1,0:T(8,128)(2,1)S(1)}, bf16[256,256]{1,0:T(8,128)(2,1)}, u32[]{:S(2)}) copy-start(bf16[256,256]{1,0:T(8,128)(2,1)} %param.22) | copy-start | bytes 393220
  12.4 24.8 %copy-start.9 = (s32[32,16]{0,1:T(8,128)S(1)}, s32[32,16]{0,1:T(8,128)}, u32[]{:S(2)}) copy-start(s32[32,16]{0,1:T(8,128)} %param.40) | copy-start | bytes 6148
  12.4 62.8 %all-to-all-start = ((bf16[32,256,128]{2,1,0:T(8,128)(2,1)}), bf16[32,256,128]{2,1,0:T(8,128)(2,1)S(1)}, u32[]{:S(2)}, u32[]{:S(2)}) async-start(bf16[32,256,128]{2,1,0:T(8,128)(2,1)} %broadcast_select_fusion), calls=%async_computation | async-start | bytes 4194304 | tf_op jit(solution)/shard_map/all_to_all | solution.py:127
  26.3 187.4 %all-reduce.4.cloned.1.call-start = ((), (), s32[]{:S(2)}) async-start(), calls=%async_computation.1 | async-start | bytes 4194304 | tf_op jit(solution)/shard_map/psum | solution.py:151
  26.6 7.8 %copy-start.11 = (f32[4,256]{1,0:T(4,128)}, f32[4,256]{1,0:T(4,128)S(1)}, u32[]{:S(2)}) copy-start(f32[4,256]{1,0:T(4,128)S(1)} %get-tuple-element.20) | copy-start | bytes 12292
  28.2 6.2 %copy-start.13 = (f32[1,4,2,128]{3,1,2,0:T(4,128)}, f32[1,4,2,128]{3,1,2,0:T(4,128)S(1)}, u32[]{:S(2)}) copy-start(f32[1,4,2,128]{3,1,2,0:T(4,128)S(1)} %copy.61) | copy-start | bytes 12292
  28.9 5.5 %copy-start.15 = (s32[16]{0:T(128)}, s32[16]{0:T(128)S(1)}, u32[]{:S(2)}) copy-start(s32[16]{0:T(128)S(1)} %get-tuple-element.7) | copy-start | bytes 196
  76.9 6.0 %copy-start.16 = (s32[16]{0:T(128)S(1)}, s32[16]{0:T(128)}, u32[]{:S(2)}) copy-start(s32[16]{0:T(128)} %copy-done.15) | copy-start | bytes 196
  76.9 6.0 %copy-start.22 = (f32[16,4]{1,0:T(8,128)S(1)}, f32[16,4]{1,0:T(8,128)}, u32[]{:S(2)}) copy-start(f32[16,4]{1,0:T(8,128)} %gather_fusion.2) | copy-start | bytes 772
  76.9 6.0 %copy-start.24 = (s32[16]{0:T(128)S(1)}, s32[16]{0:T(128)}, u32[]{:S(2)}) copy-start(s32[16]{0:T(128)} %copy-done.23) | copy-start | bytes 196
  76.9 6.0 %copy-start.26 = (pred[16]{0:T(512)(128)(4,1)S(1)}, pred[16]{0:T(512)(128)(4,1)}, u32[]{:S(2)}) copy-start(pred[16]{0:T(512)(128)(4,1)} %get-tuple-element.17) | copy-start | bytes 52
  78.9 6.3 %collective-permute-start = (f32[4,64,128]{2,1,0:T(8,128)S(1)}, f32[4,64,128]{2,1,0:T(8,128)S(1)}, u32[]{:S(2)}, u32[]{:S(2)}) collective-permute-start(f32[4,64,128]{2,1,0:T(8,128)S(1)} %convolution_add_fusion), channel_id=1, source_target_pairs={{0,16},{16,32},{32,48},{48,64},{64,80},{80,96},{96,112},{112,128},... | collective-permute-start | bytes 393224 | tf_op jit(solution)/shard_map/ppermute | solution.py:16
  91.3 124.9 %all-gather.3.cloned.1.call-start = ((), (), s32[]{:S(2)}) async-start(), calls=%async_computation.2 | async-start | bytes 7028736 | tf_op jit(solution)/shard_map/all_gather | solution.py:158
  91.9 196.6 %all-gather.5.cloned.1.call-start = ((), (), s32[]{:S(2)}) async-start(), calls=%async_computation.3 | async-start | bytes 7028736 | tf_op jit(solution)/shard_map/all_gather | solution.py:159
  92.5 123.7 %copy-start.29 = (f32[2048]{0:T(1024)S(1)}, f32[2048]{0:T(1024)}, u32[]{:S(2)}) copy-start(f32[2048]{0:T(1024)} %param.34) | copy-start | bytes 24580
  216.2 72.3 %copy-start.30 = (f32[2048]{0:T(1024)S(1)}, f32[2048]{0:T(1024)}, u32[]{:S(2)}) copy-start(f32[2048]{0:T(1024)} %param.35) | copy-start | bytes 24580
  223.6 96.0 %copy-start.2 = (f32[256,1576]{0,1:T(8,128)S(1)}, f32[256,1576]{0,1:T(8,128)}, u32[]{:S(2)}) copy-start(f32[256,1576]{0,1:T(8,128)} %get-tuple-element.28) | copy-start | bytes 4841476
  223.6 96.0 %copy-start.20 = (s32[256]{0:T(256)S(1)}, s32[256]{0:T(256)}, u32[]{:S(2)}) copy-start(s32[256]{0:T(256)} %param.43) | copy-start | bytes 3076
  295.7 51.6 %copy-start.25 = (s32[16]{0:T(128)S(1)}, s32[16]{0:T(128)}, u32[]{:S(2)}) copy-start(s32[16]{0:T(128)} %copy-done.23) | copy-start | bytes 196
  (15 other events, 23.3 us)
Sparse Core Ops, SparseCore 0:
  91.5 122.2 all-reduce.3
Sparse Core Ops, SparseCore 1:
  95.0 96.9 all-gather.2
  195.0 93.5 all-gather.4
where the time goes:
time: 357 us; the launch traced here: 356 us
  waiting for transfers between devices  196 us (55%)
  blocking collectives  74.5 us (21%)
  matrix products  23.4 us (7%)
  starting transfers between devices  18 us (5%)
  between operations  17.7 us (5%)
  other arithmetic  16.7 us (5%)
  local copies, waits for them, and re-layouts  10.3 us (3%)
    psum x1, waiting for transfers between devices, body(): partial_value, squares = lax.psum((partial_value, squares), 'vocab')  95.6 us
    all_gather x1, waiting for transfers between devices, body(): lax.all_gather(ref_head, 'grp', axis=0, tiled=True)  64.9 us
    all_to_all x1, waiting for transfers between devices, body(): lax.all_to_all(outgoing, 'grp', split_axis=0, concat_axis=0, tiled=True)  32.3 us
    psum x1, blocking collectives, body(): lax.psum((policy_total, ref_total, policy_pick, ref_pick), 'vocab')  25.5 us
    psum x1, blocking collectives, body(): partial_value, squares = lax.psum((partial_value, squares), 'vocab')  25.1 us
    pmax x1, blocking collectives, body(): policy_top, ref_top = lax.pmax((policy_top, ref_top), 'vocab')  23.9 us
    dot_general x2, matrix products, add_rows(): return jnp.dot(normed, piece, preferred_element_type=jnp.float32)  14.5 us
    all_to_all x1, starting transfers between devices, body(): lax.all_to_all(outgoing, 'grp', split_axis=0, concat_axis=0, tiled=True)  13.9 us
  transfers between devices with their start and end apart: 5, of which 4 were waited for; matrix products, arithmetic and copies ran while one was open for 7% of the time, Pallas kernels for 0%

commit v1 on v0

v1 whole, which is shorter than its diff:
```python
import functools

import jax
import jax.numpy as jnp
from jax import lax
from jax.experimental import pallas as pl
from jax.experimental.pallas import tpu as pltpu
from jax.sharding import PartitionSpec as P

INNER = 4096
EPS = 1e-05
F32 = jnp.float32
BF16 = jnp.bfloat16
NT = (((1,), (1,)), ((), ()))
TN = (((0,), (0,)), ((), ()))
VM = pl.BlockSpec(memory_space=pltpu.VMEM)
SM = pl.BlockSpec(memory_space=pltpu.SMEM)


def params(limit=48 << 20):
    return pltpu.CompilerParams(vmem_limit_bytes=limit)


def cost(flops, moved, transcendentals=0):
    return pl.CostEstimate(flops=flops, bytes_accessed=moved, transcendentals=transcendentals)


def split(value):
    high = value.astype(BF16)
    low = (value - high.astype(F32)).astype(BF16)
    return high, low


def choose_kernel(slot_ref, pages_ref, out_ref):
    for dest in range(out_ref.shape[0]):
        out_ref[dest] = pages_ref[slot_ref[dest]]


def choose_pages(send_slot, saved_pages):
    groups = send_slot.shape[0]
    shape = (groups,) + saved_pages.shape[1:]
    return pl.pallas_call(
        choose_kernel,
        out_shape=jax.ShapeDtypeStruct(shape, saved_pages.dtype),
        in_specs=[SM, VM],
        out_specs=VM,
        compiler_params=params(),
        cost_estimate=cost(0, 2 * groups * 65536),
        name="choose_pages",
    )(send_slot, saved_pages)


def scan_kernel(
    len_ref, x_ref, z_ref, b_ref, c_ref, raw_ref, par_ref, base_ref, decay_ref, sum_ref, keep_ref
):
    tokens, channels = x_ref.shape
    heads = raw_ref.shape[0]
    width = channels // heads
    rows = lax.broadcasted_iota(jnp.int32, (tokens, tokens), 0)
    cols = lax.broadcasted_iota(jnp.int32, (tokens, tokens), 1)
    row_req = jnp.zeros((tokens, tokens), jnp.int32)
    col_req = jnp.zeros((tokens, tokens), jnp.int32)
    end = jnp.int32(0)
    last_start = jnp.int32(0)
    requests = len_ref.shape[1]
    for r in range(requests):
        last_start = end
        end = end + len_ref[0, r]
        row_req = row_req + (rows >= end).astype(jnp.int32)
        col_req = col_req + (cols >= end).astype(jnp.int32)
    same = row_req == col_req
    causal = jnp.logical_and(same, cols <= rows)
    upto = jnp.logical_and(same, rows <= cols).astype(F32)
    step = jax.nn.softplus(raw_ref[...] + par_ref[1])
    log_decay = -jnp.exp(par_ref[0]) * step
    seg = jnp.dot(
        jnp.concatenate([log_decay, log_decay], axis=0),
        upto,
        precision=lax.Precision.HIGHEST,
        preferred_element_type=F32,
    )
    both = jnp.concatenate([seg[:heads], step], axis=0)
    turned = both.T
    scores = lax.dot_general(c_ref[...], b_ref[...], NT, preferred_element_type=F32)
    x = x_ref[...]
    x_f = x.astype(F32)
    channel_head = lax.broadcasted_iota(jnp.int32, (tokens, channels), 1) // width
    mixed = jnp.zeros((tokens, channels), F32)
    reach = jnp.zeros((tokens, channels), F32)
    weight = jnp.zeros((tokens, channels), F32)
    in_last = rows[:, :1] >= last_start
    for h in range(heads):
        column = turned[:, h : h + 1]
        row = both[h : h + 1, :]
        fade = jnp.exp(jnp.where(causal, column - row, 0.0))
        mixing = jnp.where(causal, fade * scores * both[heads + h : heads + h + 1, :], 0.0)
        out = jnp.dot(mixing.astype(BF16), x, preferred_element_type=F32)
        mine = channel_head == h
        skip = par_ref[2, h : h + 1, :]
        mixed = jnp.where(mine, out + skip * x_f, mixed)
        reach = jnp.where(mine, jnp.exp(column), reach)
        tail = jnp.where(in_last, column[tokens - 1 :, :] - column, 0.0)
        tail = jnp.where(in_last, jnp.exp(tail) * turned[:, heads + h : heads + h + 1], 0.0)
        weight = jnp.where(mine, tail, weight)
    gate = jax.nn.silu(z_ref[...].astype(F32))
    base_ref[...] = mixed * gate
    decay_ref[...] = reach * gate
    high, low = split(x_f * weight)
    b = b_ref[...]
    sum_ref[...] = lax.dot_general(high, b, TN, preferred_element_type=F32) + lax.dot_general(
        low, b, TN, preferred_element_type=F32
    )
    keep_ref[...] = jnp.broadcast_to(reach[tokens - 1 :, :], (128, channels)).T


def scan_parts(lengths, x, z, b, c, raw, per_head):
    tokens, channels = x.shape
    states = b.shape[1]
    big = jax.ShapeDtypeStruct((tokens, channels), F32)
    state = jax.ShapeDtypeStruct((channels, states), F32)
    return pl.pallas_call(
        scan_kernel,
        out_shape=(big, big, state, state),
        in_specs=[SM] + [VM] * 6,
        out_specs=(VM,) * 4,
        compiler_params=params(),
        cost_estimate=cost(400_000_000, 2_000_000, 500_000),
        name="scan_parts",
    )(lengths, x, z, b, c, raw, per_head)


def ending_kernel(own_ref, res_ref, page_ref, sum_ref, keep_ref, out_ref):
    flag = (res_ref[0, 15] > 0).astype(F32)
    out_ref[...] = sum_ref[...] + keep_ref[...] * flag * page_ref[0].astype(F32)


def end_state(owners, resumed, incoming, summed, keep):
    last = owners.shape[0] - 1
    channels, states = summed.shape
    whole = pl.BlockSpec((channels, states), lambda i, own, res: (0, 0))
    return pl.pallas_call(
        ending_kernel,
        out_shape=jax.ShapeDtypeStruct((channels, states), F32),
        grid_spec=pltpu.PrefetchScalarGridSpec(
            num_scalar_prefetch=2,
            grid=(1,),
            in_specs=[
                pl.BlockSpec((1, channels, states), lambda i, own, res: (own[last], 0, 0)),
                whole,
                whole,
            ],
            out_specs=whole,
        ),
        compiler_params=params(),
        cost_estimate=cost(70_000, 400_000),
        name="end_state",
    )(owners, resumed, incoming, summed, keep)


def reads_kernel(len_ref, own_ref, res_ref, group_ref, c_ref, inc_ref, out_ref):
    c = c_ref[...]
    tokens = c.shape[0]
    token = lax.broadcasted_iota(jnp.int32, c.shape, 0)
    requests = len_ref.shape[1]
    first = (group_ref[0] == 0).astype(jnp.int32)
    total = None
    start = jnp.int32(0)
    zero = jnp.zeros_like(c)
    for r in range(0, requests, 2):
        lhs, rhs = [], []
        for k in (r, r + 1):
            size = len_ref[0, k]
            live = res_ref[0, k] if k else res_ref[0, 0] * first
            stop = start + size * live
            lhs.append(jnp.where(jnp.logical_and(token >= start, token < stop), c, zero))
            rhs.append(inc_ref[own_ref[k]])
            start = start + size
        term = lax.dot_general(
            jnp.concatenate(lhs, axis=1),
            jnp.concatenate(rhs, axis=1),
            NT,
            preferred_element_type=F32,
        )
        total = term if total is None else total + term
    out_ref[...] = total


def page_reads(lengths, owners, resumed, group, c, incoming):
    tokens = c.shape[0]
    channels = incoming.shape[1]
    return pl.pallas_call(
        reads_kernel,
        out_shape=jax.ShapeDtypeStruct((tokens, channels), F32),
        in_specs=[SM] * 4 + [VM] * 2,
        out_specs=VM,
        compiler_params=params(),
        cost_estimate=cost(300_000_000, 2_500_000),
        name="page_reads",
    )(lengths, owners, resumed, group, c, incoming)


def project_kernel(
    len_ref, group_ref, c_ref, carry_ref, reads_ref, base_ref, decay_ref, gain_ref, w_ref, out_ref
):
    c = c_ref[...]
    token = lax.broadcasted_iota(jnp.int32, c.shape, 0)
    stop = len_ref[0, 0] * (group_ref[0] > 0).astype(jnp.int32)
    first = jnp.where(token < stop, c, jnp.zeros_like(c))
    high, low = split(carry_ref[...])
    start = reads_ref[...] + lax.dot_general(first, high, NT, preferred_element_type=F32)
    start = start + lax.dot_general(first, low, NT, preferred_element_type=F32)
    gated = base_ref[...] + decay_ref[...] * start
    square = jnp.sum(gated * gated, axis=1, keepdims=True)
    weighted = (gated * gain_ref[...]).astype(BF16)
    model = w_ref.shape[1]
    out_ref[:, :model] = jnp.dot(weighted, w_ref[...], preferred_element_type=F32).astype(BF16)
    lane = lax.broadcasted_iota(jnp.int32, (c.shape[0], 128), 1)
    rounded = square.astype(BF16).astype(F32)
    pair = jnp.where(lane == 0, rounded, jnp.where(lane == 1, square - rounded, 0.0))
    out_ref[:, model:] = pair.astype(BF16)


def project(lengths, group, c, carry, reads, base, decay, gain, w):
    tokens = c.shape[0]
    model = w.shape[1]
    return pl.pallas_call(
        project_kernel,
        out_shape=jax.ShapeDtypeStruct((tokens, model + 128), BF16),
        in_specs=[SM] * 2 + [VM] * 7,
        out_specs=VM,
        compiler_params=params(),
        cost_estimate=cost(300_000_000, 3_500_000),
        name="project",
    )(lengths, group, c, carry, reads, base, decay, gain, w)


def norm_kernel(place_ref, recv_ref, res_ref, gain_ref, out_ref):
    model = res_ref.shape[1]
    total = jnp.sum(recv_ref[...].astype(F32), axis=0)
    square = total[:, model : model + 1] + total[:, model + 1 : model + 2]
    hidden = res_ref[...].astype(F32) + total[:, :model] * lax.rsqrt(square / INNER + EPS)
    factor = lax.rsqrt(jnp.mean(hidden * hidden, axis=1, keepdims=True) + EPS)
    normed = (hidden * factor * gain_ref[...]).astype(BF16)
    for k in range(out_ref.shape[0]):
        out_ref[k] = normed


def norm_rows(place, recv, residual, gain):
    parts, mine, wide = recv.shape
    model = residual.shape[1]
    return pl.pallas_call(
        norm_kernel,
        out_shape=jax.ShapeDtypeStruct((parts, mine, model), BF16),
        grid_spec=pltpu.PrefetchScalarGridSpec(
            num_scalar_prefetch=1,
            grid=(1,),
            in_specs=[
                pl.BlockSpec((parts, mine, wide), lambda i, p: (0, 0, 0)),
                pl.BlockSpec((mine, model), lambda i, p: (p[0], 0)),
                pl.BlockSpec((1, model), lambda i, p: (0, 0)),
            ],
            out_specs=pl.BlockSpec((parts, mine, model), lambda i, p: (0, 0, 0)),
        ),
        compiler_params=params(),
        cost_estimate=cost(1_000_000, 3_200_000),
        name="norm_rows",
    )(place, recv, residual, gain)


def ref_norm_kernel(x_ref, gain_ref, out_ref):
    x = x_ref[...].astype(F32)
    factor = lax.rsqrt(jnp.mean(x * x, axis=1, keepdims=True) + EPS)
    out_ref[...] = (x * factor * gain_ref[...]).astype(BF16)


def ref_norm(x, gain):
    return pl.pallas_call(
        ref_norm_kernel,
        out_shape=jax.ShapeDtypeStruct(x.shape, BF16),
        in_specs=[VM, VM],
        out_specs=VM,
        compiler_params=params(),
        cost_estimate=cost(2_000_000, 2_000_000),
        name="ref_norm",
    )(x, gain)


def score_kernel(columns, place_ref, both_ref, target_ref, head_ref, out_ref, stats):
    model = pl.program_id(0)
    tile = pl.program_id(1)
    block = head_ref.shape[3]
    groups, _, deep, _ = head_ref.shape
    head = head_ref[...].reshape(groups * deep, block)
    logits = jnp.dot(both_ref[0], head, preferred_element_type=F32)
    column = lax.broadcasted_iota(jnp.int32, logits.shape, 1) + tile * block
    inside = column < columns
    logits = jnp.where(inside, logits, -jnp.inf)
    wanted = target_ref[...][:, :1] - place_ref[0] * columns
    pick = jnp.sum(jnp.where(jnp.logical_and(column == wanted, inside), logits, 0.0), axis=1, keepdims=True)
    top = jnp.max(logits, axis=1, keepdims=True)
    lane = lax.broadcasted_iota(jnp.int32, stats.shape, 1)
    at = model * 3

    @pl.when(jnp.logical_and(model == 0, tile == 0))
    def _():
        stats[...] = jnp.zeros_like(stats)

    old = stats[...]

    def read(k):
        return jnp.sum(jnp.where(lane == at + k, old, 0.0), axis=1, keepdims=True)

    fresh = tile == 0
    old_top = jnp.where(fresh, top, read(0))
    new_top = jnp.maximum(old_top, top)
    total = read(1) * jnp.exp(old_top - new_top) + jnp.sum(jnp.exp(logits - new_top), axis=1, keepdims=True)
    picked = read(2) + pick
    new = jnp.where(lane == at, new_top, old)
    new = jnp.where(lane == at + 1, total, new)
    new = jnp.where(lane == at + 2, picked, new)
    stats[...] = new

    @pl.when(jnp.logical_and(model == 1, tile == pl.num_programs(1) - 1))
    def _():
        out_ref[...] = jnp.broadcast_to(new.T[:8, :][None], out_ref.shape)


def scores(place, both, target, heads, parts):
    groups, models, deep, columns = heads.shape
    tokens, depth = both.shape[1:]
    block = 512
    tiles = pl.cdiv(columns, block)
    return pl.pallas_call(
        functools.partial(score_kernel, columns),
        out_shape=jax.ShapeDtypeStruct((parts, 8, tokens), F32),
        grid_spec=pltpu.PrefetchScalarGridSpec(
            num_scalar_prefetch=1,
            grid=(models, tiles),
            in_specs=[
                pl.BlockSpec((1, tokens, depth), lambda m, j, p: (m, 0, 0)),
                pl.BlockSpec((tokens, 128), lambda m, j, p: (0, 0)),
                pl.BlockSpec((groups, 1, deep, block), lambda m, j, p: (0, m, 0, j)),
            ],
            out_specs=pl.BlockSpec((parts, 8, tokens), lambda m, j, p: (0, 0, 0)),
            scratch_shapes=[pltpu.VMEM((tokens, 128), F32)],
        ),
        compiler_params=params(),
        cost_estimate=cost(3_400_000_000, 15_000_000, 800_000),
        name="scores",
    )(place, both, target, heads)


def final_kernel(len_ref, recv_ref, logp_ref, sums_ref):
    recv = recv_ref[...]
    rows = []
    for k in (0, 3):
        tops = recv[:, k]
        top = jnp.max(tops, axis=0, keepdims=True)
        total = jnp.sum(recv[:, k + 1] * jnp.exp(tops - top), axis=0, keepdims=True)
        pick = jnp.sum(recv[:, k + 2], axis=0, keepdims=True)
        rows.append(pick - (top + jnp.log(total)))
    ref, policy = rows
    logp_ref[0:1, :] = policy
    logp_ref[1:2, :] = ref
    token = lax.broadcasted_iota(jnp.int32, policy.shape, 1)
    lane = lax.broadcasted_iota(jnp.int32, sums_ref.shape, 1)
    gap = policy - ref
    total = jnp.zeros(sums_ref.shape, F32)
    row = lax.broadcasted_iota(jnp.int32, sums_ref.shape, 0)
    start = jnp.int32(0)
    for r in range(len_ref.shape[1]):
        stop = start + len_ref[0, r]
        inside = jnp.logical_and(token >= start, token < stop)
        a = jnp.sum(jnp.where(inside, policy, 0.0), axis=1, keepdims=True)
        b = jnp.sum(jnp.where(inside, gap, 0.0), axis=1, keepdims=True)
        total = jnp.where(lane == r, jnp.where(row == 0, a, b), total)
        start = stop
    sums_ref[...] = total


def finish(lengths, recv):
    tokens = recv.shape[2]
    requests = lengths.shape[1]
    return pl.pallas_call(
        final_kernel,
        out_shape=(
            jax.ShapeDtypeStruct((2, tokens), F32),
            jax.ShapeDtypeStruct((2, requests), F32),
        ),
        in_specs=[SM, VM],
        out_specs=(VM, VM),
        compiler_params=params(),
        cost_estimate=cost(200_000, 150_000),
        name="finish",
    )(lengths, recv)


def from_behind(x, axis, by):
    count = lax.axis_size(axis)
    pairs = [(i, i + by) for i in range(count) if 0 <= i + by < count]
    return lax.ppermute(x, axis, pairs)


def body(
    inner_x,
    gate_z,
    state_b,
    state_c,
    step_raw,
    decay_log,
    step_bias,
    skip_gain,
    norm_gain,
    out_weight,
    residual,
    ref_hidden,
    policy_gain,
    ref_gain,
    policy_head,
    ref_head,
    saved_pages,
    lengths,
    page_owner,
    page_slot,
    resumed,
    targets,
):
    parts = lax.axis_size("vocab")
    tokens, channels = inner_x.shape
    group = lax.axis_index("grp")
    place = lax.axis_index("vocab")[None].astype(jnp.int32)
    my_group = group[None].astype(jnp.int32)

    heads = lax.all_gather(jnp.stack([ref_head, policy_head]), "grp", axis=0)

    send_slot = jnp.sum(jnp.where(page_owner == group, page_slot, 0), axis=1)
    owners = lax.dynamic_index_in_dim(page_owner, group, 0, keepdims=False)
    outgoing = choose_pages(send_slot, saved_pages)
    incoming = lax.all_to_all(outgoing, "grp", split_axis=0, concat_axis=0, tiled=True)

    per_head = jnp.broadcast_to(
        jnp.stack([decay_log, step_bias, skip_gain])[:, :, None], (3, decay_log.shape[0], tokens)
    )
    base, decay, summed, keep = scan_parts(
        lengths, inner_x, gate_z, state_b, state_c, step_raw, per_head
    )
    ref_normed = ref_norm(ref_hidden, ref_gain[None])
    target = jnp.broadcast_to(targets[:, None], (tokens, 128))

    ending = end_state(owners, resumed, incoming, summed, keep)
    carried = from_behind(ending, "grp", 1)
    reads = page_reads(lengths, owners, resumed, my_group, state_c, incoming)
    partial = project(
        lengths, my_group, state_c, carried, reads, base, decay, norm_gain[None], out_weight
    )
    recv = lax.all_to_all(
        partial.reshape(parts, tokens // parts, -1), "vocab", split_axis=0, concat_axis=0, tiled=True
    )
    mine = norm_rows(place, recv, residual, policy_gain[None])
    normed = lax.all_to_all(mine, "vocab", split_axis=0, concat_axis=0, tiled=True)
    both = jnp.stack([ref_normed, normed.reshape(tokens, -1)])
    stats = scores(place, both, target, heads, parts)
    recv = lax.all_to_all(stats, "vocab", split_axis=0, concat_axis=0, tiled=True)
    return finish(lengths, recv)


def solution(mesh):
    in_specs = (
        P("grp", "vocab"),
        P("grp", "vocab"),
        P("grp", None),
        P("grp", None),
        P("vocab", "grp"),
        P("vocab"),
        P("vocab"),
        P("vocab"),
        P("vocab"),
        P("vocab", None),
        P("grp", None),
        P("grp", None),
        P(),
        P(),
        P("grp", "vocab"),
        P("grp", "vocab"),
        P("grp", "vocab", None),
        P("grp", None),
        P(),
        P(),
        P("grp", None),
        P("grp"),
    )
    out_specs = (P(None, "grp"), P(None, "grp"))
    return jax.shard_map(body, mesh=mesh, in_specs=in_specs, out_specs=out_specs, check_vma=False)
```

time: 357 us -> 215 us (0.60)
  waiting for transfers between devices: 196 us -> 120 us
  blocking collectives: 74.5 us -> 16.8 us
  matrix products: 23.4 us -> 0 us
  Pallas kernels: 0 us -> 22.4 us
  starting transfers between devices: 18 us -> 34.4 us
  other arithmetic: 16.7 us -> 4.03 us
  local copies, waits for them, and re-layouts: 10.3 us -> 2.69 us
    psum x1 -> x0, waiting for transfers between devices: 95.6 us -> none  [body(): partial_value, squares = lax.psum((partial_value, squares), 'vocab')]
    all_gather x2 -> x1, waiting for transfers between devices: 64.9 us -> 3.94 us  [body(): heads = lax.all_gather(jnp.stack([ref_head, policy_head]), 'grp', axis=0)]
    all_to_all x0 -> x2, waiting for transfers between devices: none -> 56.2 us  [the longest x1 29.2 us: body(): lax.all_to_all(partial.reshape(parts, tokens // parts, -1), 'vocab', spli...]
    psum x2 -> x0, blocking collectives: 50.6 us -> none  [the longest x1 25.5 us: body(): lax.psum((policy_total, ref_total, policy_pick, ref_pick), 'vocab')]
    all_to_all x1, waiting for transfers between devices: 32.3 us -> 59.2 us  [body(): lax.all_to_all(outgoing, 'grp', split_axis=0, concat_axis=0, tiled=True)]
    pmax x1 -> x0, blocking collectives: 23.9 us -> none  [body(): policy_top, ref_top = lax.pmax((policy_top, ref_top), 'vocab')]
    dot_general x10 -> x0, matrix products: 23.4 us -> none  [the longest x2 14.5 us: add_rows(): return jnp.dot(normed, piece, preferred_element_type=jnp.float32)]
    pallas_call x0 -> x9, Pallas kernels: none -> 22.4 us  [the longest x1 12.2 us: scores(): pl.pallas_call(functools.partial(score_kernel, columns), out_shape=jax.Sh...]
  transfers between devices with their start and end apart: 5 -> 5, of which waited for: 4 -> 5; matrix products, arithmetic and copies ran while one was open for 7% -> 1% of each run, Pallas kernels for 0% -> 4%
where the time goes in v1:
time: 215 us
  waiting for transfers between devices  120 us (56%)
  starting transfers between devices  34.4 us (16%)
  Pallas kernels  22.4 us (10%)
  blocking collectives  16.8 us (8%)
  between operations  14.3 us (7%)
  other arithmetic  4.03 us (2%)
  local copies, waits for them, and re-layouts  2.69 us (1%)
    all_to_all x1, waiting for transfers between devices, body(): lax.all_to_all(outgoing, 'grp', split_axis=0, concat_axis=0, tiled=True)  59.2 us
    all_to_all x1, waiting for transfers between devices, body(): lax.all_to_all(partial.reshape(parts, tokens // parts, -1), 'vocab', spli...  29.2 us
    all_to_all x1, waiting for transfers between devices, body(): lax.all_to_all(mine, 'vocab', split_axis=0, concat_axis=0, tiled=True)  27 us
    all_to_all x1, blocking collectives, body(): lax.all_to_all(stats, 'vocab', split_axis=0, concat_axis=0, tiled=True)  16.8 us
    all_to_all x1, starting transfers between devices, body(): lax.all_to_all(outgoing, 'grp', split_axis=0, concat_axis=0, tiled=True)  13.9 us
    pallas_call x1, Pallas kernels, scores(): pl.pallas_call(functools.partial(score_kernel, columns), out_shape=jax.Sh...  12.2 us
    all_to_all x1, starting transfers between devices, body(): lax.all_to_all(partial.reshape(parts, tokens // parts, -1), 'vocab', spli...  9.71 us
    ppermute x1, starting transfers between devices, from_behind(): return lax.ppermute(x, axis, pairs)  6.45 us
  transfers between devices with their start and end apart: 5, of which 5 were waited for; matrix products, arithmetic and copies ran while one was open for 1% of the time, Pallas kernels for 4%

profile of v1, /device:TPU:1, one launch (start us, length us, event | category | flops | bytes accessed | tf_op | source)
XLA Modules:
  0.0 214.6 jit_solution(15446204660423725740)
XLA Ops:
  7.2 1.9 pad_maximum_fusion.1
  9.1 0.7 select_reduce_fusion.slot_ref
  9.8 0.9 copy-done.4
  10.8 0.7 choose_pages.1
  11.5 1.3 copy-done
  12.9 13.9 %all-to-all-start = ((bf16[32,256,128]{2,1,0:T(8,128)(2,1)}), bf16[32,256,128]{2,1,0:T(8,128)(2,1)S(1)}, u32[]{:S(2)}, u32[]{:S(2)}) async-start(bf16[32,256,128]{2,1,0:T(8,128)(2,1)} %copy-done), calls=%async_computation | async-start | bytes 4194304 | tf_op jit(solution)/shard_map/all_to_all | solution.py:439
  27.1 2.2 %scan_parts.1 = (f32[256,256]{1,0:T(8,128)S(1)}, f32[256,256]{1,0:T(8,128)S(1)}, f32[256,128]{1,0:T(8,128)S(1)}, f32[256,128]{1,0:T(8,128)S(1)}) custom-call(s32[1,16]{1,0:T(1,128)S(1)} %copy-done.8, bf16[256,256]{1,0:T(8,128)(2,1)S(1)} %copy-done.11, bf16[256,256]{1,0:T(8,128)(2,1)S(1)} %copy-done.12, bf16[256,128]{1,0:T(8,128)(2,1)S(1)} %copy-done.13, ...), custom_call_target="tpu_custom_call" | custom-call | flops 400000000 | bytes 2000000 | tf_op jit(solution)/shard_map/scan_parts/pallas_call | solution.py:121
  29.4 59.2 %all-to-all-done.page_ref.inc_ref = bf16[32,256,128]{2,1,0:T(8,128)(2,1)S(1)} async-done(((bf16[32,256,128]{2,1,0:T(8,128)(2,1)}), bf16[32,256,128]{2,1,0:T(8,128)(2,1)S(1)}, u32[]{:S(2)}, u32[]{:S(2)}) %all-to-all-start) | async-done | bytes 2097184 | tf_op jit(solution)/shard_map/all_to_all | solution.py:439
  88.5 0.6 end_state.1
  89.1 6.5 %collective-permute-start = (f32[256,128]{1,0:T(8,128)S(1)}, f32[256,128]{1,0:T(8,128)S(1)}, u32[]{:S(2)}, u32[]{:S(2)}) collective-permute-start(f32[256,128]{1,0:T(8,128)S(1)} %end_state.1), channel_id=1, source_target_pairs={{0,16},{16,32},{32,48},{48,64},{64,80},{80,96},{96,112},{112,128},... | collective-permute-start | bytes 393224 | tf_op jit(solution)/shard_map/ppermute | solution.py:401
  95.6 1.3 page_reads.1.reads_ref
  96.9 0.7 collective-permute-done.carry_ref
  97.5 2.3 %project.1 = bf16[256,2176]{1,0:T(8,128)(2,1)} custom-call(s32[1,16]{1,0:T(1,128)S(1)} %copy-done.8, s32[1]{0:T(128)} %bitcast.3.group_ref, bf16[256,128]{1,0:T(8,128)(2,1)S(1)} %copy-done.5, f32[256,128]{1,0:T(8,128)S(1)} %collective-permute-done.carry_ref, f32[256,256]{1,0:T(8,128)S(1)} %page_reads.1.reads_ref, f32[256,256]{1,0:T(8,128)S(1)} %get-tuple-element.8.base_ref, ...), custom_call_target="tpu_custom_call" | custom-call | flops 300000000 | bytes 3500000 | tf_op jit(solution)/shard_map/project/pallas_call | solution.py:226
  99.8 9.7 %all-to-all-start.1 = ((bf16[16,16,2176]{2,1,0:T(8,128)(2,1)}), bf16[16,16,2176]{2,1,0:T(8,128)(2,1)S(1)}, u32[]{:S(2)}, u32[]{:S(2)}) async-start(bf16[16,16,2176]{2,1,0:T(8,128)(2,1)} %bitcast.8), calls=%async_computation.1 | async-start | bytes 2228224 | tf_op jit(solution)/shard_map/all_to_all | solution.py:456
  109.5 29.2 %all-to-all-done.1.recv_ref = bf16[16,16,2176]{2,1,0:T(8,128)(2,1)S(1)} async-done(((bf16[16,16,2176]{2,1,0:T(8,128)(2,1)}), bf16[16,16,2176]{2,1,0:T(8,128)(2,1)S(1)}, u32[]{:S(2)}, u32[]{:S(2)}) %all-to-all-start.1) | async-done | bytes 1114144 | tf_op jit(solution)/shard_map/all_to_all | solution.py:456
  138.7 1.4 norm_rows.1
  140.1 4.4 %all-to-all-start.2 = ((bf16[16,16,2048]{2,1,0:T(8,128)(2,1)}), bf16[16,16,2048]{2,1,0:T(8,128)(2,1)}, u32[]{:S(2)}, u32[]{:S(2)}) async-start(bf16[16,16,2048]{2,1,0:T(8,128)(2,1)} %norm_rows.1), calls=%async_computation.2 | async-start | bytes 2097152 | tf_op jit(solution)/shard_map/all_to_all | solution.py:460
  144.5 0.4 ref_norm.1
  144.9 27.0 %all-to-all-done.2 = bf16[16,16,2048]{2,1,0:T(8,128)(2,1)} async-done(((bf16[16,16,2048]{2,1,0:T(8,128)(2,1)}), bf16[16,16,2048]{2,1,0:T(8,128)(2,1)}, u32[]{:S(2)}, u32[]{:S(2)}) %all-to-all-start.2) | async-done | bytes 1048608 | tf_op jit(solution)/shard_map/all_to_all | solution.py:460
  171.9 1.4 pad_maximum_fusion.both_ref
  173.3 3.9 %all-gather.3.cloned.1.call-done = bf16[64,64,1576]{2,1,0:T(8,128)(2,1)} async-done(((bf16[2,64,1576]{2,1,0:T(8,128)(2,1)}), bf16[64,64,1576]{2,1,0:T(8,128)(2,1)}) %all-gather.3.cloned.1.call-update) | async-done | bytes 12910608 | tf_op jit(solution)/shard_map/all_gather | solution.py:434
  177.4 12.2 %scores.1 = f32[16,8,256]{2,1,0:T(8,128)S(1)} custom-call(s32[1]{0:T(128)} %bitcast.place_ref, bf16[2,256,2048]{2,1,0:T(8,128)(2,1)S(1)} %pad_maximum_fusion.both_ref, s32[256,128]{1,0:T(8,128)S(1)} %broadcast_in_dim.38.target_ref, bf16[32,2,64,1576]{3,2,1,0:T(8,128)(2,1)} %bitcast.18), custom_call_target="tpu_custom_call" | custom-call | flops 3400000000 | bytes 15000000 | tf_op jit(solution)/shard_map/scores/pallas_call | solution.py:333
  189.6 16.8 %all_to_all.20.recv_ref = f32[16,8,256]{2,1,0:T(8,128)S(1)} all-to-all(f32[16,8,256]{2,1,0:T(8,128)S(1)} %scores.1), channel_id=1, replica_groups=mesh['grp'=32,'vocab'=16] {'vocab'}, dimensions={0} | all-to-all | bytes 262144 | tf_op jit(solution)/shard_map/all_to_all | solution.py:463
  206.4 1.3 finish.1
  (44 shorter events, 0.5 us)
Async XLA Ops:
  7.2 170.1 %all-gather.3.cloned.1.call-start = ((), (), s32[]{:S(2)}) async-start(), calls=%async_computation.4 | async-start | bytes 14057472 | tf_op jit(solution)/shard_map/all_gather | solution.py:434
  11.5 1.3 copy-start
  12.8 14.0 %copy-start.15 = (s32[32,16]{0,1:T(8,128)S(1)}, s32[32,16]{0,1:T(8,128)}, u32[]{:S(2)}) copy-start(s32[32,16]{0,1:T(8,128)} %param.40) | copy-start | bytes 6148
  12.8 14.2 %copy-start.17 = (f32[4]{0:T(128)S(1)}, f32[4]{0:T(128)}, u32[]{:S(2)}) copy-start(f32[4]{0:T(128)} %param.29) | copy-start | bytes 52
  12.8 14.2 %copy-start.18 = (f32[4]{0:T(128)S(1)}, f32[4]{0:T(128)}, u32[]{:S(2)}) copy-start(f32[4]{0:T(128)} %param.28) | copy-start | bytes 52
  12.8 14.2 %copy-start.19 = (f32[4]{0:T(128)S(1)}, f32[4]{0:T(128)}, u32[]{:S(2)}) copy-start(f32[4]{0:T(128)} %param.27) | copy-start | bytes 52
  12.8 14.3 %copy-start.5 = (bf16[256,128]{1,0:T(8,128)(2,1)S(1)}, bf16[256,128]{1,0:T(8,128)(2,1)}, u32[]{:S(2)}) copy-start(bf16[256,128]{1,0:T(8,128)(2,1)} %c_ref.5) | copy-start | bytes 196612
  12.8 14.3 %copy-start.8 = (s32[1,16]{1,0:T(1,128)S(1)}, s32[1,16]{1,0:T(1,128)}, u32[]{:S(2)}) copy-start(s32[1,16]{1,0:T(1,128)} %len_ref.7) | copy-start | bytes 196
  12.8 14.2 %copy-start.11 = (bf16[256,256]{1,0:T(8,128)(2,1)S(1)}, bf16[256,256]{1,0:T(8,128)(2,1)}, u32[]{:S(2)}) copy-start(bf16[256,256]{1,0:T(8,128)(2,1)} %x_ref.3) | copy-start | bytes 393220
  12.8 14.2 %copy-start.12 = (bf16[256,256]{1,0:T(8,128)(2,1)S(1)}, bf16[256,256]{1,0:T(8,128)(2,1)}, u32[]{:S(2)}) copy-start(bf16[256,256]{1,0:T(8,128)(2,1)} %z_ref.1) | copy-start | bytes 393220
  12.9 14.2 %copy-start.13 = (bf16[256,128]{1,0:T(8,128)(2,1)S(1)}, bf16[256,128]{1,0:T(8,128)(2,1)}, u32[]{:S(2)}) copy-start(bf16[256,128]{1,0:T(8,128)(2,1)} %b_ref.1) | copy-start | bytes 196612
  12.9 14.2 %copy-start.14 = (f32[4,256]{1,0:T(4,128)S(1)}, f32[4,256]{1,0:T(4,128)}, u32[]{:S(2)}) copy-start(f32[4,256]{1,0:T(4,128)} %raw_ref.1) | copy-start | bytes 12292
  12.9 75.7 %copy-start.9 = (s32[1,16]{1,0:T(1,128)S(1)}, s32[1,16]{1,0:T(1,128)}, u32[]{:S(2)}) copy-start(s32[1,16]{1,0:T(1,128)} %res_ref.4) | copy-start | bytes 196
  12.9 75.6 %all-to-all-start = ((bf16[32,256,128]{2,1,0:T(8,128)(2,1)}), bf16[32,256,128]{2,1,0:T(8,128)(2,1)S(1)}, u32[]{:S(2)}, u32[]{:S(2)}) async-start(bf16[32,256,128]{2,1,0:T(8,128)(2,1)} %copy-done), calls=%async_computation | async-start | bytes 4194304 | tf_op jit(solution)/shard_map/all_to_all | solution.py:439
  88.5 9.0 %copy-start.3 = (bf16[256,2048]{1,0:T(8,128)(2,1)S(1)}, bf16[256,2048]{1,0:T(8,128)(2,1)}, u32[]{:S(2)}) copy-start(bf16[256,2048]{1,0:T(8,128)(2,1)} %w_ref.1) | copy-start | bytes 3145732
  88.5 9.0 %copy-start.10 = (f32[256]{0:T(256)S(1)}, f32[256]{0:T(256)}, u32[]{:S(2)}) copy-start(f32[256]{0:T(256)} %param.30) | copy-start | bytes 3076
  89.1 8.4 %collective-permute-start = (f32[256,128]{1,0:T(8,128)S(1)}, f32[256,128]{1,0:T(8,128)S(1)}, u32[]{:S(2)}, u32[]{:S(2)}) collective-permute-start(f32[256,128]{1,0:T(8,128)S(1)} %end_state.1), channel_id=1, source_target_pairs={{0,16},{16,32},{32,48},{48,64},{64,80},{80,96},{96,112},{112,128},... | collective-permute-start | bytes 393224 | tf_op jit(solution)/shard_map/ppermute | solution.py:401
  97.5 41.2 %copy-start.1 = (bf16[256,2048]{1,0:T(8,128)(2,1)S(1)}, bf16[256,2048]{1,0:T(8,128)(2,1)}, u32[]{:S(2)}) copy-start(bf16[256,2048]{1,0:T(8,128)(2,1)} %res_ref.5) | copy-start | bytes 3145732
  97.5 41.2 %copy-start.6 = (f32[2048]{0:T(1024)S(1)}, f32[2048]{0:T(1024)}, u32[]{:S(2)}) copy-start(f32[2048]{0:T(1024)} %param.34) | copy-start | bytes 24580
  99.8 39.0 %all-to-all-start.1 = ((bf16[16,16,2176]{2,1,0:T(8,128)(2,1)}), bf16[16,16,2176]{2,1,0:T(8,128)(2,1)S(1)}, u32[]{:S(2)}, u32[]{:S(2)}) async-start(bf16[16,16,2176]{2,1,0:T(8,128)(2,1)} %bitcast.8), calls=%async_computation.1 | async-start | bytes 2228224 | tf_op jit(solution)/shard_map/all_to_all | solution.py:456
  138.7 5.8 %copy-start.7 = (f32[2048]{0:T(1024)S(1)}, f32[2048]{0:T(1024)}, u32[]{:S(2)}) copy-start(f32[2048]{0:T(1024)} %param.35) | copy-start | bytes 24580
  140.1 4.4 %copy-start.2 = (bf16[256,2048]{1,0:T(8,128)(2,1)S(1)}, bf16[256,2048]{1,0:T(8,128)(2,1)}, u32[]{:S(2)}) copy-start(bf16[256,2048]{1,0:T(8,128)(2,1)} %x_ref.2) | copy-start | bytes 3145732
  140.1 31.8 %all-to-all-start.2 = ((bf16[16,16,2048]{2,1,0:T(8,128)(2,1)}), bf16[16,16,2048]{2,1,0:T(8,128)(2,1)}, u32[]{:S(2)}, u32[]{:S(2)}) async-start(bf16[16,16,2048]{2,1,0:T(8,128)(2,1)} %norm_rows.1), calls=%async_computation.2 | async-start | bytes 2097152 | tf_op jit(solution)/shard_map/all_to_all | solution.py:460
  171.9 5.4 %copy-start.16 = (s32[256]{0:T(256)S(1)}, s32[256]{0:T(256)}, u32[]{:S(2)}) copy-start(s32[256]{0:T(256)} %param.43) | copy-start | bytes 3076
  (1 other events, 0.9 us)
Sparse Core Ops, SparseCore 0:
  11.2 166.0 all-gather.2

commit v2 on v1

--- a/solution.py
+++ b/solution.py
@@ -31,27 +31,97 @@
     return high, low
 
 
-def choose_kernel(slot_ref, pages_ref, out_ref):
-    for dest in range(out_ref.shape[0]):
-        out_ref[dest] = pages_ref[slot_ref[dest]]
-
-
-def choose_pages(send_slot, saved_pages):
-    groups = send_slot.shape[0]
-    shape = (groups,) + saved_pages.shape[1:]
-    return pl.pallas_call(
-        choose_kernel,
-        out_shape=jax.ShapeDtypeStruct(shape, saved_pages.dtype),
-        in_specs=[SM, VM],
+def send_kernel(groups, len_ref, own_ref, res_ref, group_ref, first_ref, c_ref, out_ref):
+    reach = out_ref.shape[0]
+    tokens, states = c_ref.shape
+    requests = len_ref.shape[1]
+    span = groups // reach
+    my_x = group_ref[0] // reach
+    c = c_ref[...]
+    rows = out_ref.shape[1] - tokens
+    sub = lax.broadcasted_iota(jnp.int32, (rows, states), 0)
+    token = sub * states + lax.broadcasted_iota(jnp.int32, (rows, states), 1)
+    for dest in range(reach):
+        number = jnp.full((rows, states), -1, jnp.int32)
+        start = jnp.int32(0)
+        for r in range(requests):
+            stop = start + len_ref[0, r]
+            if r:
+                owner = own_ref[r]
+                page = (my_x - owner // reach + span) % span
+                live = res_ref[0, r] > 0
+            else:
+                owner = first_ref[0]
+                page = jnp.int32(span)
+                live = jnp.logical_or(group_ref[0] > 0, res_ref[0, 0] > 0)
+            hit = jnp.logical_and(owner % reach == dest, live)
+            page = jnp.where(hit, page, -1)
+            inside = jnp.logical_and(token >= start, token < stop)
+            number = jnp.where(inside, page, number)
+            start = stop
+        out_ref[dest, :tokens, :] = c
+        out_ref[dest, tokens:, :] = number.astype(F32).astype(BF16)
+
+
+def send_rows(groups, lengths, owners, resumed, group, first_owner, c, reach):
+    tokens, states = c.shape
+    return pl.pallas_call(
+        functools.partial(send_kernel, groups),
+        out_shape=jax.ShapeDtypeStruct((reach, tokens + 16, states), BF16),
+        in_specs=[SM] * 5 + [VM],
         out_specs=VM,
         compiler_params=params(),
-        cost_estimate=cost(0, 2 * groups * 65536),
-        name="choose_pages",
-    )(send_slot, saved_pages)
+        cost_estimate=cost(100_000, 400_000),
+        name="send_rows",
+    )(lengths, owners, resumed, group, first_owner, c)
+
+
+def reads_kernel(table_ref, recv_ref, *refs):
+    *page_refs, out_ref, pages = refs
+    groups, wide, states = recv_ref.shape
+    tokens = wide - 16
+    count = table_ref.shape[1]
+    slots = page_refs[0].shape[0]
+    for k, ref in enumerate(page_refs):
+        pages[k * slots : (k + 1) * slots] = ref[...]
+    for j in range(groups):
+        c = recv_ref[j, :tokens, :].astype(F32)
+        numbers = recv_ref[j, tokens:, :].astype(F32).T
+        blocks = [
+            jnp.broadcast_to(numbers[:, k : k + 1], (states, states)) for k in range(tokens // states)
+        ]
+        number = jnp.concatenate(blocks, axis=0)
+        lhs, rhs = [], []
+        for s in range(count):
+            lhs.append(jnp.where(number == float(s), c, 0.0).astype(BF16))
+            rhs.append(pages[table_ref[j, s]])
+        term = lax.dot_general(
+            jnp.concatenate(lhs, axis=1),
+            jnp.concatenate(rhs, axis=1),
+            NT,
+            preferred_element_type=F32,
+        )
+        out_ref[j] = term.astype(BF16)
+
+
+def page_reads(table, recv, pages):
+    groups = recv.shape[0]
+    tokens = recv.shape[1] - 16
+    slots, channels, states = pages[0].shape
+    return pl.pallas_call(
+        reads_kernel,
+        out_shape=jax.ShapeDtypeStruct((groups, tokens, channels), BF16),
+        in_specs=[SM] + [VM] * (1 + len(pages)),
+        out_specs=VM,
+        scratch_shapes=[pltpu.VMEM((len(pages) * slots, channels, states), BF16)],
+        compiler_params=params(),
+        cost_estimate=cost(700_000_000, 3_000_000),
+        name="page_reads",
+    )(table, recv, *pages)
 
 
 def scan_kernel(
-    len_ref, x_ref, z_ref, b_ref, c_ref, raw_ref, par_ref, base_ref, decay_ref, sum_ref, keep_ref
+    len_ref, res_ref, x_ref, z_ref, b_ref, c_ref, raw_ref, par_ref, base_ref, decay_ref, carry_ref
 ):
     tokens, channels = x_ref.shape
     heads = raw_ref.shape[0]
@@ -107,96 +177,33 @@
     decay_ref[...] = reach * gate
     high, low = split(x_f * weight)
     b = b_ref[...]
-    sum_ref[...] = lax.dot_general(high, b, TN, preferred_element_type=F32) + lax.dot_general(
-        low, b, TN, preferred_element_type=F32
-    )
-    keep_ref[...] = jnp.broadcast_to(reach[tokens - 1 :, :], (128, channels)).T
-
-
-def scan_parts(lengths, x, z, b, c, raw, per_head):
+    states = b.shape[1]
+    carry_ref[:channels, :] = lax.dot_general(
+        high, b, TN, preferred_element_type=F32
+    ) + lax.dot_general(low, b, TN, preferred_element_type=F32)
+    live = (res_ref[0, requests - 1] > 0).astype(F32)
+    keep = reach[tokens - 1 :, :] * live
+    sub = lax.broadcasted_iota(jnp.int32, (8, states), 0)
+    tail = jnp.zeros((8, states), F32)
+    for k in range(channels // states):
+        piece = jnp.broadcast_to(keep[:, k * states : (k + 1) * states], (8, states))
+        tail = jnp.where(sub == k, piece, tail)
+    carry_ref[channels:, :] = tail
+
+
+def scan_parts(lengths, resumed, x, z, b, c, raw, per_head):
     tokens, channels = x.shape
     states = b.shape[1]
     big = jax.ShapeDtypeStruct((tokens, channels), F32)
-    state = jax.ShapeDtypeStruct((channels, states), F32)
     return pl.pallas_call(
         scan_kernel,
-        out_shape=(big, big, state, state),
-        in_specs=[SM] + [VM] * 6,
-        out_specs=(VM,) * 4,
+        out_shape=(big, big, jax.ShapeDtypeStruct((channels + 8, states), F32)),
+        in_specs=[SM] * 2 + [VM] * 6,
+        out_specs=(VM,) * 3,
         compiler_params=params(),
         cost_estimate=cost(400_000_000, 2_000_000, 500_000),
         name="scan_parts",
-    )(lengths, x, z, b, c, raw, per_head)
-
-
-def ending_kernel(own_ref, res_ref, page_ref, sum_ref, keep_ref, out_ref):
-    flag = (res_ref[0, 15] > 0).astype(F32)
-    out_ref[...] = sum_ref[...] + keep_ref[...] * flag * page_ref[0].astype(F32)
-
-
-def end_state(owners, resumed, incoming, summed, keep):
-    last = owners.shape[0] - 1
-    channels, states = summed.shape
-    whole = pl.BlockSpec((channels, states), lambda i, own, res: (0, 0))
-    return pl.pallas_call(
-        ending_kernel,
-        out_shape=jax.ShapeDtypeStruct((channels, states), F32),
-        grid_spec=pltpu.PrefetchScalarGridSpec(
-            num_scalar_prefetch=2,
-            grid=(1,),
-            in_specs=[
-                pl.BlockSpec((1, channels, states), lambda i, own, res: (own[last], 0, 0)),
-                whole,
-                whole,
-            ],
-            out_specs=whole,
-        ),
-        compiler_params=params(),
-        cost_estimate=cost(70_000, 400_000),
-        name="end_state",
-    )(owners, resumed, incoming, summed, keep)
-
-
-def reads_kernel(len_ref, own_ref, res_ref, group_ref, c_ref, inc_ref, out_ref):
-    c = c_ref[...]
-    tokens = c.shape[0]
-    token = lax.broadcasted_iota(jnp.int32, c.shape, 0)
-    requests = len_ref.shape[1]
-    first = (group_ref[0] == 0).astype(jnp.int32)
-    total = None
-    start = jnp.int32(0)
-    zero = jnp.zeros_like(c)
-    for r in range(0, requests, 2):
-        lhs, rhs = [], []
-        for k in (r, r + 1):
-            size = len_ref[0, k]
-            live = res_ref[0, k] if k else res_ref[0, 0] * first
-            stop = start + size * live
-            lhs.append(jnp.where(jnp.logical_and(token >= start, token < stop), c, zero))
-            rhs.append(inc_ref[own_ref[k]])
-            start = start + size
-        term = lax.dot_general(
-            jnp.concatenate(lhs, axis=1),
-            jnp.concatenate(rhs, axis=1),
-            NT,
-            preferred_element_type=F32,
-        )
-        total = term if total is None else total + term
-    out_ref[...] = total
-
-
-def page_reads(lengths, owners, resumed, group, c, incoming):
-    tokens = c.shape[0]
-    channels = incoming.shape[1]
-    return pl.pallas_call(
-        reads_kernel,
-        out_shape=jax.ShapeDtypeStruct((tokens, channels), F32),
-        in_specs=[SM] * 4 + [VM] * 2,
-        out_specs=VM,
-        compiler_params=params(),
-        cost_estimate=cost(300_000_000, 2_500_000),
-        name="page_reads",
-    )(lengths, owners, resumed, group, c, incoming)
+    )(lengths, resumed, x, z, b, c, raw, per_head)
 
 
 def project_kernel(
@@ -206,8 +213,15 @@
     token = lax.broadcasted_iota(jnp.int32, c.shape, 0)
     stop = len_ref[0, 0] * (group_ref[0] > 0).astype(jnp.int32)
     first = jnp.where(token < stop, c, jnp.zeros_like(c))
-    high, low = split(carry_ref[...])
-    start = reads_ref[...] + lax.dot_general(first, high, NT, preferred_element_type=F32)
+    tokens, channels = base_ref.shape
+    states = c.shape[1]
+    high, low = split(carry_ref[:channels, :])
+    start = jnp.sum(reads_ref[...].astype(F32), axis=0)
+    rows = [carry_ref[channels + k : channels + k + 1, :] for k in range(channels // states)]
+    keep = jnp.concatenate(rows, axis=1)
+    among = lax.broadcasted_iota(jnp.int32, (tokens, channels), 0) < stop
+    start = jnp.where(among, start * keep, start)
+    start = start + lax.dot_general(first, high, NT, preferred_element_type=F32)
     start = start + lax.dot_general(first, low, NT, preferred_element_type=F32)
     gated = base_ref[...] + decay_ref[...] * start
     square = jnp.sum(gated * gated, axis=1, keepdims=True)
@@ -285,69 +299,107 @@
     )(x, gain)
 
 
-def score_kernel(columns, place_ref, both_ref, target_ref, head_ref, out_ref, stats):
-    model = pl.program_id(0)
-    tile = pl.program_id(1)
-    block = head_ref.shape[3]
-    groups, _, deep, _ = head_ref.shape
+def score_kernel(
+    columns, tiles, place_ref, ref_ref, pol_ref, target_ref, head_ref, out_ref,
+    rows, logits, tops, sums, picks, stats,
+):
+    step = pl.program_id(0)
+    steps = pl.num_programs(0)
+    groups, _, deep, block = head_ref.shape
+    low = float(jnp.finfo(F32).min)
+
+    @pl.when(step == 0)
+    def _():
+        rows[...] = ref_ref[...]
+        stats[...] = jnp.zeros_like(stats)
+
+    @pl.when(step == tiles)
+    def _():
+        rows[...] = pol_ref[...]
+
+    @pl.when(lax.rem(step + tiles - 1, tiles) == 0)
+    def _():
+        tops[...] = jnp.full_like(tops, low)
+        sums[...] = jnp.zeros_like(sums)
+        picks[...] = jnp.zeros_like(picks)
+
+    before = jnp.maximum(step - 1, 0)
+    tile = lax.rem(before, tiles)
     head = head_ref[...].reshape(groups * deep, block)
-    logits = jnp.dot(both_ref[0], head, preferred_element_type=F32)
-    column = lax.broadcasted_iota(jnp.int32, logits.shape, 1) + tile * block
-    inside = column < columns
-    logits = jnp.where(inside, logits, -jnp.inf)
-    wanted = target_ref[...][:, :1] - place_ref[0] * columns
-    pick = jnp.sum(jnp.where(jnp.logical_and(column == wanted, inside), logits, 0.0), axis=1, keepdims=True)
-    top = jnp.max(logits, axis=1, keepdims=True)
-    lane = lax.broadcasted_iota(jnp.int32, stats.shape, 1)
-    at = model * 3
-
-    @pl.when(jnp.logical_and(model == 0, tile == 0))
+    old_slot = lax.rem(step + 1, 2)
+    wanted = target_ref[...] - place_ref[0] * columns - tile * block
+    room = columns - tile * block
+    lane = lax.broadcasted_iota(jnp.int32, wanted.shape, 1)
+    pieces, pick = [], picks[...]
+    top = tops[...]
+    for k in range(block // 128):
+        here = lane + k * 128
+        piece = logits[old_slot, :, k * 128 : (k + 1) * 128]
+        piece = jnp.where(here < room, piece, low)
+        pick = pick + jnp.where(jnp.logical_and(here == wanted, here < room), piece, 0.0)
+        pieces.append(piece)
+        top = jnp.maximum(top, piece)
+    total = sums[...] * jnp.exp(tops[...] - top)
+    for piece in pieces:
+        total = total + jnp.exp(piece - top)
+    logits[lax.rem(step, 2)] = jnp.dot(rows[...], head, preferred_element_type=F32)
+    tops[...] = top
+    sums[...] = total
+    picks[...] = pick
+
+    @pl.when(jnp.logical_and(tile == tiles - 1, step > 0))
     def _():
-        stats[...] = jnp.zeros_like(stats)
-
-    old = stats[...]
-
-    def read(k):
-        return jnp.sum(jnp.where(lane == at + k, old, 0.0), axis=1, keepdims=True)
-
-    fresh = tile == 0
-    old_top = jnp.where(fresh, top, read(0))
-    new_top = jnp.maximum(old_top, top)
-    total = read(1) * jnp.exp(old_top - new_top) + jnp.sum(jnp.exp(logits - new_top), axis=1, keepdims=True)
-    picked = read(2) + pick
-    new = jnp.where(lane == at, new_top, old)
-    new = jnp.where(lane == at + 1, total, new)
-    new = jnp.where(lane == at + 2, picked, new)
-    stats[...] = new
-
-    @pl.when(jnp.logical_and(model == 1, tile == pl.num_programs(1) - 1))
+        at = 3 * (before // tiles)
+        peak = jnp.max(top, axis=1, keepdims=True)
+        whole = jnp.sum(total * jnp.exp(top - peak), axis=1, keepdims=True)
+        chosen = jnp.sum(pick, axis=1, keepdims=True)
+        new = jnp.where(lane == at, peak, stats[...])
+        new = jnp.where(lane == at + 1, whole, new)
+        stats[...] = jnp.where(lane == at + 2, chosen, new)
+
+    @pl.when(step == steps - 1)
     def _():
-        out_ref[...] = jnp.broadcast_to(new.T[:8, :][None], out_ref.shape)
-
-
-def scores(place, both, target, heads, parts):
+        out_ref[...] = jnp.broadcast_to(stats[...].T[:8, :][None], out_ref.shape)
+
+
+def scores(place, ref_rows, policy_rows, target, heads, parts):
     groups, models, deep, columns = heads.shape
-    tokens, depth = both.shape[1:]
+    tokens, depth = ref_rows.shape
     block = 512
     tiles = pl.cdiv(columns, block)
-    return pl.pallas_call(
-        functools.partial(score_kernel, columns),
+    last = models * tiles - 1
+    plain = pltpu.VMEM((tokens, 128), F32)
+
+    def head_at(i, p):
+        now = jnp.minimum(i, last)
+        return (0, now // tiles, 0, lax.rem(now, tiles))
+
+    return pl.pallas_call(
+        functools.partial(score_kernel, columns, tiles),
         out_shape=jax.ShapeDtypeStruct((parts, 8, tokens), F32),
         grid_spec=pltpu.PrefetchScalarGridSpec(
             num_scalar_prefetch=1,
-            grid=(models, tiles),
+            grid=(models * tiles + 1,),
             in_specs=[
-                pl.BlockSpec((1, tokens, depth), lambda m, j, p: (m, 0, 0)),
-                pl.BlockSpec((tokens, 128), lambda m, j, p: (0, 0)),
-                pl.BlockSpec((groups, 1, deep, block), lambda m, j, p: (0, m, 0, j)),
+                pl.BlockSpec((tokens, depth), lambda i, p: (0, 0)),
+                pl.BlockSpec((tokens, depth), lambda i, p: (0, 0)),
+                pl.BlockSpec((tokens, 128), lambda i, p: (0, 0)),
+                pl.BlockSpec((groups, 1, deep, block), head_at),
             ],
-            out_specs=pl.BlockSpec((parts, 8, tokens), lambda m, j, p: (0, 0, 0)),
-            scratch_shapes=[pltpu.VMEM((tokens, 128), F32)],
+            out_specs=pl.BlockSpec((parts, 8, tokens), lambda i, p: (0, 0, 0)),
+            scratch_shapes=[
+                pltpu.VMEM((tokens, depth), BF16),
+                pltpu.VMEM((2, tokens, block), F32),
+                plain,
+                plain,
+                plain,
+                plain,
+            ],
         ),
         compiler_params=params(),
         cost_estimate=cost(3_400_000_000, 15_000_000, 800_000),
         name="scores",
-    )(place, both, target, heads)
+    )(place, ref_rows, policy_rows, target, heads)
 
 
 def final_kernel(len_ref, recv_ref, logp_ref, sums_ref):
@@ -427,29 +479,56 @@
 ):
     parts = lax.axis_size("vocab")
     tokens, channels = inner_x.shape
+    groups = lax.axis_size("grp")
+    slots = saved_pages.shape[0]
     group = lax.axis_index("grp")
     place = lax.axis_index("vocab")[None].astype(jnp.int32)
     my_group = group[None].astype(jnp.int32)
 
+    ring = 8
+    span = groups // ring
+    lines = [[x * ring + k for k in range(ring)] for x in range(span)]
     heads = lax.all_gather(jnp.stack([ref_head, policy_head]), "grp", axis=0)
 
-    send_slot = jnp.sum(jnp.where(page_owner == group, page_slot, 0), axis=1)
+    my_x, my_z = group >> 3, group & 7
+    last = page_owner.shape[1] - 1
+    before_owner = jnp.concatenate([page_owner[:1, 0], page_owner[:-1, last]])
+    before_slot = jnp.concatenate([page_slot[:1, 0], page_slot[:-1, last]])
+    first_row = my_x * ring
+    asked = lax.dynamic_slice_in_dim(page_owner, first_row, ring, 0)[:, 1:]
+    asked_slot = lax.dynamic_slice_in_dim(page_slot, first_row, ring, 0)[:, 1:]
+    step = jnp.arange(span, dtype=jnp.int32)
+    wanted = ((my_x - step) & (span - 1)) * ring + my_z
+    match = asked[:, None, :] == wanted[None, :, None]
+    found = jnp.sum(jnp.where(match, asked_slot[:, None, :], 0), axis=2) + slots * step[None, :]
+    first_page = ((my_x - (before_owner >> 3)) & (span - 1)) * slots + before_slot
+    first_page = lax.dynamic_slice_in_dim(first_page, first_row, ring, 0)
+    table = jnp.concatenate([found, first_page[:, None]], axis=1)
     owners = lax.dynamic_index_in_dim(page_owner, group, 0, keepdims=False)
-    outgoing = choose_pages(send_slot, saved_pages)
-    incoming = lax.all_to_all(outgoing, "grp", split_axis=0, concat_axis=0, tiled=True)
-
+    first_owner = lax.dynamic_slice_in_dim(before_owner, group, 1)
+
+    asking = send_rows(groups, lengths, owners, resumed, my_group, first_owner, state_c, ring)
+    asking = lax.all_to_all(
+        asking, "grp", split_axis=0, concat_axis=0, tiled=True, axis_index_groups=lines
+    )
+    pages = [saved_pages]
+    for k in range(1, span):
+        pairs = [(i, (i + k * ring) % groups) for i in range(groups)]
+        pages.append(lax.ppermute(saved_pages, "grp", pairs))
     per_head = jnp.broadcast_to(
         jnp.stack([decay_log, step_bias, skip_gain])[:, :, None], (3, decay_log.shape[0], tokens)
     )
-    base, decay, summed, keep = scan_parts(
-        lengths, inner_x, gate_z, state_b, state_c, step_raw, per_head
-    )
+    base, decay, ending = scan_parts(
+        lengths, resumed, inner_x, gate_z, state_b, state_c, step_raw, per_head
+    )
+    carried = from_behind(ending, "grp", 1)
     ref_normed = ref_norm(ref_hidden, ref_gain[None])
     target = jnp.broadcast_to(targets[:, None], (tokens, 128))
 
-    ending = end_state(owners, resumed, incoming, summed, keep)
-    carried = from_behind(ending, "grp", 1)
-    reads = page_reads(lengths, owners, resumed, my_group, state_c, incoming)
+    reads = page_reads(table, asking, pages)
+    reads = lax.all_to_all(
+        reads, "grp", split_axis=0, concat_axis=0, tiled=True, axis_index_groups=lines
+    )
     partial = project(
         lengths, my_group, state_c, carried, reads, base, decay, norm_gain[None], out_weight
     )
@@ -458,8 +537,8 @@
     )
     mine = norm_rows(place, recv, residual, policy_gain[None])
     normed = lax.all_to_all(mine, "vocab", split_axis=0, concat_axis=0, tiled=True)
-    both = jnp.stack([ref_normed, normed.reshape(tokens, -1)])
-    stats = scores(place, both, target, heads, parts)
+    normed = normed.reshape(tokens, -1)
+    stats = scores(place, ref_normed, normed, target, heads, parts)
     recv = lax.all_to_all(stats, "vocab", split_axis=0, concat_axis=0, tiled=True)
     return finish(lengths, recv)
 

time: 215 us -> 200 us (0.930)
  waiting for transfers between devices: 120 us -> 90 us
  starting transfers between devices: 34.4 us -> 50.2 us
  blocking collectives: 16.8 us -> 12.5 us
  Pallas kernels: 22.4 us -> 26.3 us
    all_to_all x1 -> x2, waiting for transfers between devices: 59.2 us -> 0.01 us  [the longest x1 0.01 us: body(): lax.all_to_all(asking, 'grp', split_axis=0, concat_axis=0, tiled=True, ax...]
    ppermute x1, waiting for transfers between devices: 0.65 us -> 21.1 us  [from_behind(): return lax.ppermute(x, axis, pairs)]
    ppermute x0 -> x3, waiting for transfers between devices: none -> 12.1 us  [body(): pages.append(lax.ppermute(saved_pages, 'grp', pairs))]
    ppermute x0 -> x3, starting transfers between devices: none -> 10.5 us  [body(): pages.append(lax.ppermute(saved_pages, 'grp', pairs))]
    all_to_all x1 -> x2, starting transfers between devices: 13.9 us -> 18.9 us  [the longest x1 10.9 us: body(): lax.all_to_all(asking, 'grp', split_axis=0, concat_axis=0, tiled=True, ax...]
    all_to_all x1, blocking collectives: 16.8 us -> 12.5 us  [body(): lax.all_to_all(stats, 'vocab', split_axis=0, concat_axis=0, tiled=True)]
    all_gather x1, waiting for transfers between devices: 3.94 us -> 0.01 us  [body(): heads = lax.all_gather(jnp.stack([ref_head, policy_head]), 'grp', axis=0)]
    all_to_all x1, starting transfers between devices: 9.71 us -> 13.6 us  [body(): lax.all_to_all(partial.reshape(parts, tokens // parts, -1), 'vocab', spli...]
  transfers between devices with their start and end apart: 5 -> 9, of which waited for: 5 -> 5; matrix products, arithmetic and copies ran while one was open for 1% -> 2% of each run, Pallas kernels for 4% -> 6%
where the time goes in v2:
time: 200 us; the launch traced here: 199 us
  waiting for transfers between devices  90 us (45%)
  starting transfers between devices  50.2 us (25%)
  Pallas kernels  26.3 us (13%)
  between operations  14.3 us (7%)
  blocking collectives  12.5 us (6%)
  other arithmetic  3.53 us (2%)
  local copies, waits for them, and re-layouts  2.65 us (1%)
    all_to_all x1, waiting for transfers between devices, body(): lax.all_to_all(partial.reshape(parts, tokens // parts, -1), 'vocab', spli...  29.2 us
    all_to_all x1, waiting for transfers between devices, body(): lax.all_to_all(mine, 'vocab', split_axis=0, concat_axis=0, tiled=True)  27.5 us
    ppermute x1, waiting for transfers between devices, from_behind(): return lax.ppermute(x, axis, pairs)  21.1 us
    all_to_all x1, starting transfers between devices, body(): lax.all_to_all(partial.reshape(parts, tokens // parts, -1), 'vocab', spli...  13.6 us
    all_to_all x1, blocking collectives, body(): lax.all_to_all(stats, 'vocab', split_axis=0, concat_axis=0, tiled=True)  12.5 us
    pallas_call x1, Pallas kernels, scores(): pl.pallas_call(functools.partial(score_kernel, columns, tiles), out_shape...  12.5 us
    ppermute x3, waiting for transfers between devices, body(): pages.append(lax.ppermute(saved_pages, 'grp', pairs))  12.1 us
    all_to_all x1, starting transfers between devices, body(): lax.all_to_all(asking, 'grp', split_axis=0, concat_axis=0, tiled=True, ax...  10.9 us
  transfers between devices with their start and end apart: 9, of which 5 were waited for; matrix products, arithmetic and copies ran while one was open for 2% of the time, Pallas kernels for 6%

profile of v2, /device:TPU:1, one launch (start us, length us, event | category | flops | bytes accessed | tf_op | source)
XLA Modules:
  0.0 199.5 jit_solution(4152892287298309830)
XLA Ops:
  7.3 1.9 pad_maximum_fusion
  10.3 1.3 add_add_fusion
  11.6 0.6 dynamic_slice.20.first_ref
  12.4 3.4 %send_rows.1 = bf16[8,272,128]{2,1,0:T(8,128)(2,1)} custom-call(s32[1,16]{1,0:T(1,128)S(1)} %copy-done.7, s32[16]{0:T(128)S(1)} %dynamic-slice_reduce_fusion.own_ref, s32[1,16]{1,0:T(1,128)S(1)} %copy-done.9, s32[1]{0:T(128)} %bitcast.2.group_ref, s32[1]{0:T(128)} %dynamic_slice.20.first_ref, bf16[256,128]{1,0:T(8,128)(2,1)S(1)} %copy-done.3), custom_call_target="tpu_custom_call" | custom-call | flops 100000 | bytes 400000 | tf_op jit(solution)/shard_map/send_rows/pallas_call | solution.py:68
  15.8 10.9 %all-to-all-start = ((bf16[8,272,128]{2,1,0:T(8,128)(2,1)}), bf16[8,272,128]{2,1,0:T(8,128)(2,1)S(1)}, u32[]{:S(2)}, u32[]{:S(2)}) async-start(bf16[8,272,128]{2,1,0:T(8,128)(2,1)} %send_rows.1), calls=%async_computation | async-start | bytes 1114112 | tf_op jit(solution)/shard_map/all_to_all | solution.py:511
  26.6 3.1 %collective-permute-start.1 = (bf16[4,256,128]{2,1,0:T(8,128)(2,1)S(1)}, bf16[4,256,128]{2,1,0:T(8,128)(2,1)S(1)}, u32[]{:S(2)}, u32[]{:S(2)}) collective-permute-start(bf16[4,256,128]{2,1,0:T(8,128)(2,1)S(1)} %copy-done.4), channel_id=1, source_target_pairs={{0,128},{16,144},{32,160},{48,176},{64,192},{80,208},{96,224},{112... | collective-permute-start | bytes 786440 | tf_op jit(solution)/shard_map/ppermute | solution.py:517
  29.8 4.4 %collective-permute-start.2 = (bf16[4,256,128]{2,1,0:T(8,128)(2,1)S(1)}, bf16[4,256,128]{2,1,0:T(8,128)(2,1)S(1)}, u32[]{:S(2)}, u32[]{:S(2)}) collective-permute-start(bf16[4,256,128]{2,1,0:T(8,128)(2,1)S(1)} %copy-done.4), channel_id=1, source_target_pairs={{0,256},{16,272},{32,288},{48,304},{64,320},{80,336},{96,352},{112... | collective-permute-start | bytes 786440 | tf_op jit(solution)/shard_map/ppermute | solution.py:517
  34.1 3.1 %collective-permute-start.3 = (bf16[4,256,128]{2,1,0:T(8,128)(2,1)S(1)}, bf16[4,256,128]{2,1,0:T(8,128)(2,1)S(1)}, u32[]{:S(2)}, u32[]{:S(2)}) collective-permute-start(bf16[4,256,128]{2,1,0:T(8,128)(2,1)S(1)} %copy-done.4), channel_id=1, source_target_pairs={{0,384},{16,400},{32,416},{48,432},{64,448},{80,464},{96,480},{112... | collective-permute-start | bytes 786440 | tf_op jit(solution)/shard_map/ppermute | solution.py:517
  38.1 9.7 %collective-permute-done.2.refs_2_ = bf16[4,256,128]{2,1,0:T(8,128)(2,1)S(1)} collective-permute-done((bf16[4,256,128]{2,1,0:T(8,128)(2,1)S(1)}, bf16[4,256,128]{2,1,0:T(8,128)(2,1)S(1)}, u32[]{:S(2)}, u32[]{:S(2)}) %collective-permute-start.2) | collective-permute-done | bytes 262176 | tf_op jit(solution)/shard_map/ppermute | solution.py:517
  47.8 2.5 %collective-permute-done.3.refs_3_ = bf16[4,256,128]{2,1,0:T(8,128)(2,1)S(1)} collective-permute-done((bf16[4,256,128]{2,1,0:T(8,128)(2,1)S(1)}, bf16[4,256,128]{2,1,0:T(8,128)(2,1)S(1)}, u32[]{:S(2)}, u32[]{:S(2)}) %collective-permute-start.3) | collective-permute-done | bytes 262176 | tf_op jit(solution)/shard_map/ppermute | solution.py:517
  50.2 2.8 %page_reads.1 = bf16[8,256,256]{2,1,0:T(8,128)(2,1)} custom-call(s32[8,5]{1,0:T(8,128)S(1)} %pad_add_fusion.table_ref, bf16[8,272,128]{2,1,0:T(8,128)(2,1)S(1)} %all-to-all-done.recv_ref, bf16[4,256,128]{2,1,0:T(8,128)(2,1)S(1)} %copy-done.4, bf16[4,256,128]{2,1,0:T(8,128)(2,1)S(1)} %collective-permute-done.1.refs_1_, ...), custom_call_target="tpu_custom_call" | custom-call | flops 700000000 | bytes 3000000 | tf_op jit(solution)/shard_map/page_reads/pallas_call | solution.py:111
  53.0 8.0 %all-to-all-start.1 = ((bf16[8,256,256]{2,1,0:T(8,128)(2,1)}), bf16[8,256,256]{2,1,0:T(8,128)(2,1)S(1)}, u32[]{:S(2)}, u32[]{:S(2)}) async-start(bf16[8,256,256]{2,1,0:T(8,128)(2,1)} %page_reads.1), calls=%async_computation.1 | async-start | bytes 2097152 | tf_op jit(solution)/shard_map/all_to_all | solution.py:529
  61.2 2.3 %scan_parts.1 = (f32[256,256]{1,0:T(8,128)S(1)}, f32[256,256]{1,0:T(8,128)S(1)}, f32[264,128]{1,0:T(8,128)S(1)}) custom-call(s32[1,16]{1,0:T(1,128)S(1)} %copy-done.7, s32[1,16]{1,0:T(1,128)S(1)} %copy-done.9, bf16[256,256]{1,0:T(8,128)(2,1)S(1)} %copy-done.10, bf16[256,256]{1,0:T(8,128)(2,1)S(1)} %copy-done.11, bf16[256,128]{1,0:T(8,128)(2,1)S(1)} %copy-done.12, ...), custom_call_target="tpu_custom_call" | custom-call | flops 400000000 | bytes 2000000 | tf_op jit(solution)/shard_map/scan_parts/pallas_call | solution.py:198
  63.5 3.4 %collective-permute-start = (f32[264,128]{1,0:T(8,128)S(1)}, f32[264,128]{1,0:T(8,128)S(1)}, u32[]{:S(2)}, u32[]{:S(2)}) collective-permute-start(f32[264,128]{1,0:T(8,128)S(1)} %get-tuple-element.5), channel_id=1, source_target_pairs={{0,16},{16,32},{32,48},{48,64},{64,80},{80,96},{96,112},{112,128},... | collective-permute-start | bytes 405512 | tf_op jit(solution)/shard_map/ppermute | solution.py:453
  66.8 21.1 %collective-permute-done.carry_ref = f32[264,128]{1,0:T(8,128)S(1)} collective-permute-done((f32[264,128]{1,0:T(8,128)S(1)}, f32[264,128]{1,0:T(8,128)S(1)}, u32[]{:S(2)}, u32[]{:S(2)}) %collective-permute-start) | collective-permute-done | bytes 135200 | tf_op jit(solution)/shard_map/ppermute | solution.py:453
  88.0 2.3 %project.1 = bf16[256,2176]{1,0:T(8,128)(2,1)} custom-call(s32[1,16]{1,0:T(1,128)S(1)} %copy-done.7, s32[1]{0:T(128)} %bitcast.2.group_ref, bf16[256,128]{1,0:T(8,128)(2,1)S(1)} %copy-done.3, f32[264,128]{1,0:T(8,128)S(1)} %collective-permute-done.carry_ref, bf16[8,256,256]{2,1,0:T(8,128)(2,1)S(1)} %all-to-all-done.1.reads_ref, ...), custom_call_target="tpu_custom_call" | custom-call | flops 300000000 | bytes 3500000 | tf_op jit(solution)/shard_map/project/pallas_call | solution.py:240
  90.3 13.6 %all-to-all-start.2 = ((bf16[16,16,2176]{2,1,0:T(8,128)(2,1)}), bf16[16,16,2176]{2,1,0:T(8,128)(2,1)S(1)}, u32[]{:S(2)}, u32[]{:S(2)}) async-start(bf16[16,16,2176]{2,1,0:T(8,128)(2,1)} %bitcast.12), calls=%async_computation.2 | async-start | bytes 2228224 | tf_op jit(solution)/shard_map/all_to_all | solution.py:535
  103.9 29.2 %all-to-all-done.2.recv_ref = bf16[16,16,2176]{2,1,0:T(8,128)(2,1)S(1)} async-done(((bf16[16,16,2176]{2,1,0:T(8,128)(2,1)}), bf16[16,16,2176]{2,1,0:T(8,128)(2,1)S(1)}, u32[]{:S(2)}, u32[]{:S(2)}) %all-to-all-start.2) | async-done | bytes 1114144 | tf_op jit(solution)/shard_map/all_to_all | solution.py:535
  133.2 1.4 norm_rows.1
  134.6 3.7 %all-to-all-start.3 = ((bf16[16,16,2048]{2,1,0:T(8,128)(2,1)}), bf16[16,16,2048]{2,1,0:T(8,128)(2,1)S(1)}, u32[]{:S(2)}, u32[]{:S(2)}) async-start(bf16[16,16,2048]{2,1,0:T(8,128)(2,1)} %norm_rows.1), calls=%async_computation.3 | async-start | bytes 2097152 | tf_op jit(solution)/shard_map/all_to_all | solution.py:539
  138.7 27.5 %all-to-all-done.3 = bf16[16,16,2048]{2,1,0:T(8,128)(2,1)S(1)} async-done(((bf16[16,16,2048]{2,1,0:T(8,128)(2,1)}), bf16[16,16,2048]{2,1,0:T(8,128)(2,1)S(1)}, u32[]{:S(2)}, u32[]{:S(2)}) %all-to-all-start.3) | async-done | bytes 1048608 | tf_op jit(solution)/shard_map/all_to_all | solution.py:539
  166.3 12.5 %scores.1 = f32[16,8,256]{2,1,0:T(8,128)S(1)} custom-call(s32[1]{0:T(128)} %bitcast.place_ref, bf16[256,2048]{1,0:T(8,128)(2,1)S(1)} %ref_norm.1.ref_ref, bf16[256,2048]{1,0:T(8,128)(2,1)S(1)} %bitcast.21, s32[256,128]{1,0:T(8,128)S(1)} %broadcast_in_dim.55.target_ref, bf16[32,2,64,1576]{3,2,1,0:T(8,128)(2,1)} %bitcast.25), custom_call_target="tpu_custom_call" | custom-call | flops 3400000000 | bytes 15000000 | tf_op jit(solution)/shard_map/scores/pallas_call | solution.py:377
  178.8 12.5 %all_to_all.25.recv_ref = f32[16,8,256]{2,1,0:T(8,128)S(1)} all-to-all(f32[16,8,256]{2,1,0:T(8,128)S(1)} %scores.1), channel_id=1, replica_groups=mesh['grp'=32,'vocab'=16] {'vocab'}, dimensions={0} | all-to-all | bytes 262144 | tf_op jit(solution)/shard_map/all_to_all | solution.py:542
  191.3 1.3 finish.1
  (66 shorter events, 2.9 us)
Async XLA Ops:
  7.2 5.2 %copy-start.3 = (bf16[256,128]{1,0:T(8,128)(2,1)S(1)}, bf16[256,128]{1,0:T(8,128)(2,1)}, u32[]{:S(2)}) copy-start(bf16[256,128]{1,0:T(8,128)(2,1)} %c_ref.5) | copy-start | bytes 196612
  7.2 5.2 %copy-start.7 = (s32[1,16]{1,0:T(1,128)S(1)}, s32[1,16]{1,0:T(1,128)}, u32[]{:S(2)}) copy-start(s32[1,16]{1,0:T(1,128)} %len_ref.7) | copy-start | bytes 196
  7.2 159.0 %all-gather.3.cloned.1.call-start = ((), (), s32[]{:S(2)}) async-start(), calls=%async_computation.5 | async-start | bytes 14057472 | tf_op jit(solution)/shard_map/all_gather | solution.py:491
  9.1 17.5 %copy-start.4 = (bf16[4,256,128]{2,1,0:T(8,128)(2,1)S(1)}, bf16[4,256,128]{2,1,0:T(8,128)(2,1)}, u32[]{:S(2)}) copy-start(bf16[4,256,128]{2,1,0:T(8,128)(2,1)} %refs_0_.1) | copy-start | bytes 786436
  15.8 34.5 %all-to-all-start = ((bf16[8,272,128]{2,1,0:T(8,128)(2,1)}), bf16[8,272,128]{2,1,0:T(8,128)(2,1)S(1)}, u32[]{:S(2)}, u32[]{:S(2)}) async-start(bf16[8,272,128]{2,1,0:T(8,128)(2,1)} %send_rows.1), calls=%async_computation | async-start | bytes 1114112 | tf_op jit(solution)/shard_map/all_to_all | solution.py:511
  26.6 11.4 %collective-permute-start.1 = (bf16[4,256,128]{2,1,0:T(8,128)(2,1)S(1)}, bf16[4,256,128]{2,1,0:T(8,128)(2,1)S(1)}, u32[]{:S(2)}, u32[]{:S(2)}) collective-permute-start(bf16[4,256,128]{2,1,0:T(8,128)(2,1)S(1)} %copy-done.4), channel_id=1, source_target_pairs={{0,128},{16,144},{32,160},{48,176},{64,192},{80,208},{96,224},{112... | collective-permute-start | bytes 786440 | tf_op jit(solution)/shard_map/ppermute | solution.py:517
  29.8 18.0 %collective-permute-start.2 = (bf16[4,256,128]{2,1,0:T(8,128)(2,1)S(1)}, bf16[4,256,128]{2,1,0:T(8,128)(2,1)S(1)}, u32[]{:S(2)}, u32[]{:S(2)}) collective-permute-start(bf16[4,256,128]{2,1,0:T(8,128)(2,1)S(1)} %copy-done.4), channel_id=1, source_target_pairs={{0,256},{16,272},{32,288},{48,304},{64,320},{80,336},{96,352},{112... | collective-permute-start | bytes 786440 | tf_op jit(solution)/shard_map/ppermute | solution.py:517
  34.1 16.1 %collective-permute-start.3 = (bf16[4,256,128]{2,1,0:T(8,128)(2,1)S(1)}, bf16[4,256,128]{2,1,0:T(8,128)(2,1)S(1)}, u32[]{:S(2)}, u32[]{:S(2)}) collective-permute-start(bf16[4,256,128]{2,1,0:T(8,128)(2,1)S(1)} %copy-done.4), channel_id=1, source_target_pairs={{0,384},{16,400},{32,416},{48,432},{64,448},{80,464},{96,480},{112... | collective-permute-start | bytes 786440 | tf_op jit(solution)/shard_map/ppermute | solution.py:517
  53.0 8.1 %copy-start.17 = (f32[4]{0:T(128)S(1)}, f32[4]{0:T(128)}, u32[]{:S(2)}) copy-start(f32[4]{0:T(128)} %param.29) | copy-start | bytes 52
  53.0 8.1 %copy-start.18 = (f32[4]{0:T(128)S(1)}, f32[4]{0:T(128)}, u32[]{:S(2)}) copy-start(f32[4]{0:T(128)} %param.28) | copy-start | bytes 52
  53.0 8.1 %copy-start.19 = (f32[4]{0:T(128)S(1)}, f32[4]{0:T(128)}, u32[]{:S(2)}) copy-start(f32[4]{0:T(128)} %param.27) | copy-start | bytes 52
  53.0 8.2 %copy-start.10 = (bf16[256,256]{1,0:T(8,128)(2,1)S(1)}, bf16[256,256]{1,0:T(8,128)(2,1)}, u32[]{:S(2)}) copy-start(bf16[256,256]{1,0:T(8,128)(2,1)} %x_ref.3) | copy-start | bytes 393220
  53.0 8.2 %copy-start.11 = (bf16[256,256]{1,0:T(8,128)(2,1)S(1)}, bf16[256,256]{1,0:T(8,128)(2,1)}, u32[]{:S(2)}) copy-start(bf16[256,256]{1,0:T(8,128)(2,1)} %z_ref.1) | copy-start | bytes 393220
  53.0 8.2 %copy-start.12 = (bf16[256,128]{1,0:T(8,128)(2,1)S(1)}, bf16[256,128]{1,0:T(8,128)(2,1)}, u32[]{:S(2)}) copy-start(bf16[256,128]{1,0:T(8,128)(2,1)} %b_ref.1) | copy-start | bytes 196612
  53.0 8.2 %copy-start.13 = (f32[4,256]{1,0:T(4,128)S(1)}, f32[4,256]{1,0:T(4,128)}, u32[]{:S(2)}) copy-start(f32[4,256]{1,0:T(4,128)} %raw_ref.1) | copy-start | bytes 12292
  53.0 34.9 %all-to-all-start.1 = ((bf16[8,256,256]{2,1,0:T(8,128)(2,1)}), bf16[8,256,256]{2,1,0:T(8,128)(2,1)S(1)}, u32[]{:S(2)}, u32[]{:S(2)}) async-start(bf16[8,256,256]{2,1,0:T(8,128)(2,1)} %page_reads.1), calls=%async_computation.1 | async-start | bytes 2097152 | tf_op jit(solution)/shard_map/all_to_all | solution.py:529
  61.1 26.9 %copy-start.2 = (bf16[256,2048]{1,0:T(8,128)(2,1)S(1)}, bf16[256,2048]{1,0:T(8,128)(2,1)}, u32[]{:S(2)}) copy-start(bf16[256,2048]{1,0:T(8,128)(2,1)} %w_ref.1) | copy-start | bytes 3145732
  61.1 26.9 %copy-start.8 = (f32[256]{0:T(256)S(1)}, f32[256]{0:T(256)}, u32[]{:S(2)}) copy-start(f32[256]{0:T(256)} %param.30) | copy-start | bytes 3076
  63.5 24.5 %collective-permute-start = (f32[264,128]{1,0:T(8,128)S(1)}, f32[264,128]{1,0:T(8,128)S(1)}, u32[]{:S(2)}, u32[]{:S(2)}) collective-permute-start(f32[264,128]{1,0:T(8,128)S(1)} %get-tuple-element.5), channel_id=1, source_target_pairs={{0,16},{16,32},{32,48},{48,64},{64,80},{80,96},{96,112},{112,128},... | collective-permute-start | bytes 405512 | tf_op jit(solution)/shard_map/ppermute | solution.py:453
  90.3 42.9 %copy-start = (bf16[256,2048]{1,0:T(8,128)(2,1)S(1)}, bf16[256,2048]{1,0:T(8,128)(2,1)}, u32[]{:S(2)}) copy-start(bf16[256,2048]{1,0:T(8,128)(2,1)} %res_ref.5) | copy-start | bytes 3145732
  90.3 42.9 %copy-start.5 = (f32[2048]{0:T(1024)S(1)}, f32[2048]{0:T(1024)}, u32[]{:S(2)}) copy-start(f32[2048]{0:T(1024)} %param.34) | copy-start | bytes 24580
  90.3 42.9 %all-to-all-start.2 = ((bf16[16,16,2176]{2,1,0:T(8,128)(2,1)}), bf16[16,16,2176]{2,1,0:T(8,128)(2,1)S(1)}, u32[]{:S(2)}, u32[]{:S(2)}) async-start(bf16[16,16,2176]{2,1,0:T(8,128)(2,1)} %bitcast.12), calls=%async_computation.2 | async-start | bytes 2228224 | tf_op jit(solution)/shard_map/all_to_all | solution.py:535
  134.6 31.7 %all-to-all-start.3 = ((bf16[16,16,2048]{2,1,0:T(8,128)(2,1)}), bf16[16,16,2048]{2,1,0:T(8,128)(2,1)S(1)}, u32[]{:S(2)}, u32[]{:S(2)}) async-start(bf16[16,16,2048]{2,1,0:T(8,128)(2,1)} %norm_rows.1), calls=%async_computation.3 | async-start | bytes 2097152 | tf_op jit(solution)/shard_map/all_to_all | solution.py:539
  138.3 27.9 %copy-start.16 = (s32[256]{0:T(256)S(1)}, s32[256]{0:T(256)}, u32[]{:S(2)}) copy-start(s32[256]{0:T(256)} %param.43) | copy-start | bytes 3076
  (5 other events, 17.3 us)
Sparse Core Ops, SparseCore 0:
  11.2 144.4 all-gather.2

commit v3 on v2

--- a/solution.py
+++ b/solution.py
@@ -13,8 +13,6 @@
 BF16 = jnp.bfloat16
 NT = (((1,), (1,)), ((), ()))
 TN = (((0,), (0,)), ((), ()))
-VM = pl.BlockSpec(memory_space=pltpu.VMEM)
-SM = pl.BlockSpec(memory_space=pltpu.SMEM)
 
 
 def params(limit=48 << 20):
@@ -23,6 +21,32 @@
 
 def cost(flops, moved, transcendentals=0):
     return pl.CostEstimate(flops=flops, bytes_accessed=moved, transcendentals=transcendentals)
+
+
+def settled(x):
+    return pltpu.with_memory_space_constraint(x, pltpu.HBM)
+
+
+def whole(x):
+    zeros = (0,) * len(x.shape)
+    return pl.BlockSpec(x.shape, lambda *_: zeros)
+
+
+def call(kernel, name, outs, scalars, arrays, estimate, scratch=()):
+    return pl.pallas_call(
+        kernel,
+        out_shape=outs,
+        grid_spec=pltpu.PrefetchScalarGridSpec(
+            num_scalar_prefetch=len(scalars),
+            grid=(1,),
+            in_specs=[whole(x) for x in arrays],
+            out_specs=jax.tree.map(whole, outs),
+            scratch_shapes=list(scratch),
+        ),
+        compiler_params=params(),
+        cost_estimate=estimate,
+        name=name,
+    )(*scalars, *arrays)
 
 
 def split(value):
@@ -31,66 +55,84 @@
     return high, low
 
 
-def send_kernel(groups, len_ref, own_ref, res_ref, group_ref, first_ref, c_ref, out_ref):
+def send_kernel(own_ref, len_ref, res_ref, group_ref, core_ref, c_ref, out_ref):
     reach = out_ref.shape[0]
     tokens, states = c_ref.shape
     requests = len_ref.shape[1]
-    span = groups // reach
+    span = own_ref.shape[0] // reach
     my_x = group_ref[0] // reach
-    c = c_ref[...]
-    rows = out_ref.shape[1] - tokens
-    sub = lax.broadcasted_iota(jnp.int32, (rows, states), 0)
-    token = sub * states + lax.broadcasted_iota(jnp.int32, (rows, states), 1)
+    half = tokens // 2
+    begin = pl.multiple_of(core_ref[0] * half, half)
+    c = c_ref[pl.ds(begin, half)]
+    shape = (out_ref.shape[1] - half, states)
+    token = lax.broadcasted_iota(jnp.int32, shape, 1) + begin
+    group = group_ref[0]
+    number = jnp.full(shape, -1, jnp.int32)
+    home = jnp.full(shape, -1, jnp.int32)
+    start = jnp.int32(0)
+    for r in range(requests):
+        stop = start + len_ref[0, r]
+        if r:
+            owner = own_ref[group, r]
+            page = (my_x - owner // reach + span) % span
+            live = res_ref[0, r]
+        else:
+            behind = own_ref[jnp.maximum(group - 1, 0), requests - 1]
+            owner = jnp.where(group > 0, behind, own_ref[0, 0])
+            page = jnp.int32(span)
+            live = jnp.where(group > 0, 1, res_ref[0, 0])
+        page = jnp.where(live > 0, page, -1)
+        inside = jnp.logical_and(token >= start, token < stop)
+        number = jnp.where(inside, page, number)
+        home = jnp.where(inside, owner % reach, home)
+        start = stop
     for dest in range(reach):
-        number = jnp.full((rows, states), -1, jnp.int32)
-        start = jnp.int32(0)
-        for r in range(requests):
-            stop = start + len_ref[0, r]
-            if r:
-                owner = own_ref[r]
-                page = (my_x - owner // reach + span) % span
-                live = res_ref[0, r] > 0
-            else:
-                owner = first_ref[0]
-                page = jnp.int32(span)
-                live = jnp.logical_or(group_ref[0] > 0, res_ref[0, 0] > 0)
-            hit = jnp.logical_and(owner % reach == dest, live)
-            page = jnp.where(hit, page, -1)
-            inside = jnp.logical_and(token >= start, token < stop)
-            number = jnp.where(inside, page, number)
-            start = stop
-        out_ref[dest, :tokens, :] = c
-        out_ref[dest, tokens:, :] = number.astype(F32).astype(BF16)
-
-
-def send_rows(groups, lengths, owners, resumed, group, first_owner, c, reach):
+        out_ref[dest, :half, :] = c
+        mine = jnp.where(home == dest, number, -1)
+        out_ref[dest, half:, :] = mine.astype(F32).astype(BF16)
+
+
+def send_rows(page_owner, lengths, resumed, group, core, c, reach):
     tokens, states = c.shape
+    return call(
+        send_kernel, "send_rows", jax.ShapeDtypeStruct((reach, tokens // 2 + 16, states), BF16),
+        [page_owner, lengths, resumed, group, core], [c], cost(100_000, 700_000),
+    )
+
+
+def after_kernel(_, pages_ref, out_ref):
+    out_ref[...] = pages_ref[...]
+
+
+def after(first, pages):
     return pl.pallas_call(
-        functools.partial(send_kernel, groups),
-        out_shape=jax.ShapeDtypeStruct((reach, tokens + 16, states), BF16),
-        in_specs=[SM] * 5 + [VM],
-        out_specs=VM,
+        after_kernel,
+        out_shape=jax.ShapeDtypeStruct(pages.shape, pages.dtype),
+        grid=(1,),
+        in_specs=[pl.BlockSpec(memory_space=pltpu.HBM), whole(pages)],
+        out_specs=whole(pages),
         compiler_params=params(),
-        cost_estimate=cost(100_000, 400_000),
-        name="send_rows",
-    )(lengths, owners, resumed, group, first_owner, c)
-
-
-def reads_kernel(table_ref, recv_ref, *refs):
+        cost_estimate=cost(0, 500_000),
+        name="after",
+    )(first, pages)
+
+
+def reads_kernel(table_ref, core_ref, own_ref, far_ref, *refs):
     *page_refs, out_ref, pages = refs
-    groups, wide, states = recv_ref.shape
-    tokens = wide - 16
+    groups, wide, states = own_ref.shape
+    half = wide - 16
     count = table_ref.shape[1]
     slots = page_refs[0].shape[0]
     for k, ref in enumerate(page_refs):
         pages[k * slots : (k + 1) * slots] = ref[...]
     for j in range(groups):
-        c = recv_ref[j, :tokens, :].astype(F32)
-        numbers = recv_ref[j, tokens:, :].astype(F32).T
-        blocks = [
-            jnp.broadcast_to(numbers[:, k : k + 1], (states, states)) for k in range(tokens // states)
-        ]
-        number = jnp.concatenate(blocks, axis=0)
+        halves, numbers = [], []
+        for ref in (own_ref, far_ref):
+            halves.append(ref[j, :half, :].astype(F32))
+            turned = ref[j, half:, :].astype(F32).T
+            numbers.append(jnp.broadcast_to(turned[:, :1], (half, states)))
+        c = jnp.concatenate(halves, axis=0)
+        number = jnp.concatenate(numbers, axis=0)
         lhs, rhs = [], []
         for s in range(count):
             lhs.append(jnp.where(number == float(s), c, 0.0).astype(BF16))
@@ -101,23 +143,19 @@
             NT,
             preferred_element_type=F32,
         )
-        out_ref[j] = term.astype(BF16)
-
-
-def page_reads(table, recv, pages):
-    groups = recv.shape[0]
-    tokens = recv.shape[1] - 16
+        term = term.astype(BF16)
+        out_ref[j, pl.ds(pl.multiple_of(core_ref[0] * half, half), half)] = term[:half]
+        out_ref[j, pl.ds(pl.multiple_of((1 - core_ref[0]) * half, half), half)] = term[half:]
+
+
+def page_reads(table, core, own, far, pages):
+    groups = own.shape[0]
+    tokens = 2 * (own.shape[1] - 16)
     slots, channels, states = pages[0].shape
-    return pl.pallas_call(
-        reads_kernel,
-        out_shape=jax.ShapeDtypeStruct((groups, tokens, channels), BF16),
-        in_specs=[SM] + [VM] * (1 + len(pages)),
-        out_specs=VM,
-        scratch_shapes=[pltpu.VMEM((len(pages) * slots, channels, states), BF16)],
-        compiler_params=params(),
-        cost_estimate=cost(700_000_000, 3_000_000),
-        name="page_reads",
-    )(table, recv, *pages)
+    return call(
+        reads_kernel, "page_reads", jax.ShapeDtypeStruct((groups, tokens, channels), BF16),
+        [table, core], [own, far, *pages], cost(700_000_000, 3_000_000), [pltpu.VMEM((len(pages) * slots, channels, states), BF16)],
+    )
 
 
 def scan_kernel(
@@ -195,19 +233,15 @@
     tokens, channels = x.shape
     states = b.shape[1]
     big = jax.ShapeDtypeStruct((tokens, channels), F32)
-    return pl.pallas_call(
-        scan_kernel,
-        out_shape=(big, big, jax.ShapeDtypeStruct((channels + 8, states), F32)),
-        in_specs=[SM] * 2 + [VM] * 6,
-        out_specs=(VM,) * 3,
-        compiler_params=params(),
-        cost_estimate=cost(400_000_000, 2_000_000, 500_000),
-        name="scan_parts",
-    )(lengths, resumed, x, z, b, c, raw, per_head)
+    return call(
+        scan_kernel, "scan_parts", (big, big, jax.ShapeDtypeStruct((channels + 8, states), F32)),
+        [lengths, resumed], [x, z, b, c, raw, per_head], cost(400_000_000, 2_000_000, 500_000),
+    )
 
 
 def project_kernel(
-    len_ref, group_ref, c_ref, carry_ref, reads_ref, base_ref, decay_ref, gain_ref, w_ref, out_ref
+    len_ref, group_ref, core_ref, c_ref, carry_ref, reads_ref, base_ref, decay_ref, gain_ref, w_ref,
+    send_ref, keep_ref, ready, pairs,
 ):
     c = c_ref[...]
     token = lax.broadcasted_iota(jnp.int32, c.shape, 0)
@@ -227,25 +261,45 @@
     square = jnp.sum(gated * gated, axis=1, keepdims=True)
     weighted = (gated * gain_ref[...]).astype(BF16)
     model = w_ref.shape[1]
-    out_ref[:, :model] = jnp.dot(weighted, w_ref[...], preferred_element_type=F32).astype(BF16)
     lane = lax.broadcasted_iota(jnp.int32, (c.shape[0], 128), 1)
     rounded = square.astype(BF16).astype(F32)
     pair = jnp.where(lane == 0, rounded, jnp.where(lane == 1, square - rounded, 0.0))
+    ready[...] = weighted
+    pairs[...] = pair.astype(BF16)
+    half = send_ref.shape[0]
+    for out_ref, which in ((send_ref, 1 - core_ref[0]), (keep_ref, core_ref[0])):
+        part = pl.ds(pl.multiple_of(which * half, half), half)
+        out_ref[:, :model] = jnp.dot(ready[part], w_ref[...], preferred_element_type=F32).astype(BF16)
+        out_ref[:, model:] = pairs[part]
+
+
+def project(lengths, group, core, c, carry, reads, base, decay, gain, w):
+    tokens, channels = base.shape
+    model = w.shape[1]
+    half = jax.ShapeDtypeStruct((tokens // 2, model + 128), BF16)
+    return call(
+        project_kernel, "project", (half, half),
+        [lengths, group, core], [c, carry, reads, base, decay, gain, w], cost(300_000_000, 3_500_000), [pltpu.VMEM((tokens, channels), BF16), pltpu.VMEM((tokens, 128), BF16)],
+    )
+
+
+def pair_kernel(a_ref, b_ref, out_ref):
+    model = a_ref.shape[1] - 128
+    a, b = a_ref[...].astype(F32), b_ref[...].astype(F32)
+    total = a + b
+    out_ref[:, :model] = total[:, :model].astype(BF16)
+    square = total[:, model : model + 1] + total[:, model + 1 : model + 2]
+    lane = lax.broadcasted_iota(jnp.int32, (a.shape[0], 128), 1)
+    rounded = square.astype(BF16).astype(F32)
+    pair = jnp.where(lane == 0, rounded, jnp.where(lane == 1, square - rounded, 0.0))
     out_ref[:, model:] = pair.astype(BF16)
 
 
-def project(lengths, group, c, carry, reads, base, decay, gain, w):
-    tokens = c.shape[0]
-    model = w.shape[1]
-    return pl.pallas_call(
-        project_kernel,
-        out_shape=jax.ShapeDtypeStruct((tokens, model + 128), BF16),
-        in_specs=[SM] * 2 + [VM] * 7,
-        out_specs=VM,
-        compiler_params=params(),
-        cost_estimate=cost(300_000_000, 3_500_000),
-        name="project",
-    )(lengths, group, c, carry, reads, base, decay, gain, w)
+def pair_sum(a, b):
+    return call(
+        pair_kernel, "pair_sum", jax.ShapeDtypeStruct(a.shape, BF16),
+        [], [a, b], cost(300_000, 1_700_000),
+    )
 
 
 def norm_kernel(place_ref, recv_ref, res_ref, gain_ref, out_ref):
@@ -288,24 +342,19 @@
 
 
 def ref_norm(x, gain):
-    return pl.pallas_call(
-        ref_norm_kernel,
-        out_shape=jax.ShapeDtypeStruct(x.shape, BF16),
-        in_specs=[VM, VM],
-        out_specs=VM,
-        compiler_params=params(),
-        cost_estimate=cost(2_000_000, 2_000_000),
-        name="ref_norm",
-    )(x, gain)
+    return call(
+        ref_norm_kernel, "ref_norm", jax.ShapeDtypeStruct(x.shape, BF16),
+        [], [x, gain], cost(2_000_000, 2_000_000),
+    )
 
 
 def score_kernel(
-    columns, tiles, place_ref, ref_ref, pol_ref, target_ref, head_ref, out_ref,
+    columns, tiles, place_ref, core_ref, ref_ref, own_ref, far_ref, target_ref, head_ref, out_ref,
     rows, logits, tops, sums, picks, stats,
 ):
     step = pl.program_id(0)
     steps = pl.num_programs(0)
-    groups, _, deep, block = head_ref.shape
+    block = head_ref.shape[1]
     low = float(jnp.finfo(F32).min)
 
     @pl.when(step == 0)
@@ -315,7 +364,9 @@
 
     @pl.when(step == tiles)
     def _():
-        rows[...] = pol_ref[...]
+        half = own_ref.shape[0]
+        rows[pl.ds(pl.multiple_of(core_ref[0] * half, half), half)] = own_ref[...]
+        rows[pl.ds(pl.multiple_of((1 - core_ref[0]) * half, half), half)] = far_ref[...]
 
     @pl.when(lax.rem(step + tiles - 1, tiles) == 0)
     def _():
@@ -325,31 +376,57 @@
 
     before = jnp.maximum(step - 1, 0)
     tile = lax.rem(before, tiles)
-    head = head_ref[...].reshape(groups * deep, block)
     old_slot = lax.rem(step + 1, 2)
-    wanted = target_ref[...] - place_ref[0] * columns - tile * block
-    room = columns - tile * block
-    lane = lax.broadcasted_iota(jnp.int32, wanted.shape, 1)
-    pieces, pick = [], picks[...]
-    top = tops[...]
-    for k in range(block // 128):
-        here = lane + k * 128
-        piece = logits[old_slot, :, k * 128 : (k + 1) * 128]
-        piece = jnp.where(here < room, piece, low)
-        pick = pick + jnp.where(jnp.logical_and(here == wanted, here < room), piece, 0.0)
-        pieces.append(piece)
-        top = jnp.maximum(top, piece)
-    total = sums[...] * jnp.exp(tops[...] - top)
-    for piece in pieces:
-        total = total + jnp.exp(piece - top)
-    logits[lax.rem(step, 2)] = jnp.dot(rows[...], head, preferred_element_type=F32)
-    tops[...] = top
-    sums[...] = total
-    picks[...] = pick
+    lane = lax.broadcasted_iota(jnp.int32, target_ref.shape, 1)
+    model = before // tiles
+    first = model * columns
+    begin = (first // block + tile) * block
+    rest = max(columns - (tiles - 1) * block, 2 * columns - (columns // block + tiles - 1) * block)
+    rest = (rest + 255) // 256 * 256
+
+    def work(width):
+        wanted = target_ref[...] - place_ref[0] * columns + first - begin
+        floor = first - begin
+        room = floor + columns
+        pieces, pick = [], picks[...]
+        top = tops[...]
+        for k in range(block // 128):
+            here = lane + k * 128
+            piece = logits[old_slot, :, k * 128 : (k + 1) * 128]
+            inside = jnp.logical_and(here >= floor, here < room)
+            piece = jnp.where(inside, piece, low)
+            pick = pick + jnp.where(jnp.logical_and(here == wanted, inside), piece, 0.0)
+            pieces.append(piece)
+            top = jnp.maximum(top, piece)
+        total = sums[...] * jnp.exp(tops[...] - top)
+        for piece in pieces:
+            total = total + jnp.exp(piece - top)
+        if width:
+            logits[lax.rem(step, 2), :, :width] = jnp.dot(
+                rows[...], head_ref[:, :width], preferred_element_type=F32
+            )
+        tops[...] = top
+        sums[...] = total
+        picks[...] = pick
+
+    is_rest = lax.rem(step, tiles) == tiles - 1
+
+    @pl.when(jnp.logical_and(step < steps - 1, jnp.logical_not(is_rest)))
+    def _():
+        work(block)
+
+    @pl.when(jnp.logical_and(step < steps - 1, is_rest))
+    def _():
+        work(min(rest, block))
+
+    @pl.when(step == steps - 1)
+    def _():
+        work(0)
 
     @pl.when(jnp.logical_and(tile == tiles - 1, step > 0))
     def _():
-        at = 3 * (before // tiles)
+        at = 3 * model
+        top, total, pick = tops[...], sums[...], picks[...]
         peak = jnp.max(top, axis=1, keepdims=True)
         whole = jnp.sum(total * jnp.exp(top - peak), axis=1, keepdims=True)
         chosen = jnp.sum(pick, axis=1, keepdims=True)
@@ -362,31 +439,33 @@
         out_ref[...] = jnp.broadcast_to(stats[...].T[:8, :][None], out_ref.shape)
 
 
-def scores(place, ref_rows, policy_rows, target, heads, parts):
-    groups, models, deep, columns = heads.shape
+def scores(place, core, ref_rows, own_rows, far_rows, target, heads, parts):
+    models, columns = 2, heads.shape[1] // 2
     tokens, depth = ref_rows.shape
     block = 512
     tiles = pl.cdiv(columns, block)
+    assert pl.cdiv(2 * columns, block) - columns // block == tiles
     last = models * tiles - 1
     plain = pltpu.VMEM((tokens, 128), F32)
 
-    def head_at(i, p):
+    def head_at(i, p, c):
         now = jnp.minimum(i, last)
-        return (0, now // tiles, 0, lax.rem(now, tiles))
+        return (0, now // tiles * columns // block + lax.rem(now, tiles))
 
     return pl.pallas_call(
         functools.partial(score_kernel, columns, tiles),
         out_shape=jax.ShapeDtypeStruct((parts, 8, tokens), F32),
         grid_spec=pltpu.PrefetchScalarGridSpec(
-            num_scalar_prefetch=1,
+            num_scalar_prefetch=2,
             grid=(models * tiles + 1,),
             in_specs=[
-                pl.BlockSpec((tokens, depth), lambda i, p: (0, 0)),
-                pl.BlockSpec((tokens, depth), lambda i, p: (0, 0)),
-                pl.BlockSpec((tokens, 128), lambda i, p: (0, 0)),
-                pl.BlockSpec((groups, 1, deep, block), head_at),
+                pl.BlockSpec((tokens, depth), lambda i, p, c: (0, 0)),
+                pl.BlockSpec((tokens // 2, depth), lambda i, p, c: (0, 0)),
+                pl.BlockSpec((tokens // 2, depth), lambda i, p, c: (0, 0)),
+                pl.BlockSpec((tokens, 128), lambda i, p, c: (0, 0)),
+                pl.BlockSpec((depth, block), head_at),
             ],
-            out_specs=pl.BlockSpec((parts, 8, tokens), lambda i, p: (0, 0, 0)),
+            out_specs=pl.BlockSpec((parts, 8, tokens), lambda i, p, c: (0, 0, 0)),
             scratch_shapes=[
                 pltpu.VMEM((tokens, depth), BF16),
                 pltpu.VMEM((2, tokens, block), F32),
@@ -399,7 +478,7 @@
         compiler_params=params(),
         cost_estimate=cost(3_400_000_000, 15_000_000, 800_000),
         name="scores",
-    )(place, ref_rows, policy_rows, target, heads)
+    )(place, core, ref_rows, own_rows, far_rows, target, heads)
 
 
 def final_kernel(len_ref, recv_ref, logp_ref, sums_ref):
@@ -433,18 +512,13 @@
 def finish(lengths, recv):
     tokens = recv.shape[2]
     requests = lengths.shape[1]
-    return pl.pallas_call(
-        final_kernel,
-        out_shape=(
+    return call(
+        final_kernel, "finish", (
             jax.ShapeDtypeStruct((2, tokens), F32),
             jax.ShapeDtypeStruct((2, requests), F32),
         ),
-        in_specs=[SM, VM],
-        out_specs=(VM, VM),
-        compiler_params=params(),
-        cost_estimate=cost(200_000, 150_000),
-        name="finish",
-    )(lengths, recv)
+        [lengths], [recv], cost(200_000, 150_000),
+    )
 
 
 def from_behind(x, axis, by):
@@ -479,16 +553,37 @@
 ):
     parts = lax.axis_size("vocab")
     tokens, channels = inner_x.shape
+    inner_x, gate_z, state_b, state_c, step_raw, out_weight, residual, ref_hidden = map(
+        settled, (inner_x, gate_z, state_b, state_c, step_raw, out_weight, residual, ref_hidden)
+    )
+    lengths, resumed = settled(lengths), settled(resumed)
+    norm_gain, policy_gain, ref_gain = map(settled, (norm_gain[None], policy_gain[None], ref_gain[None]))
     groups = lax.axis_size("grp")
     slots = saved_pages.shape[0]
     group = lax.axis_index("grp")
     place = lax.axis_index("vocab")[None].astype(jnp.int32)
     my_group = group[None].astype(jnp.int32)
 
+    core = place & 1
+    other = [(i, i ^ 1) for i in range(parts)]
     ring = 8
     span = groups // ring
     lines = [[x * ring + k for k in range(ring)] for x in range(span)]
-    heads = lax.all_gather(jnp.stack([ref_head, policy_head]), "grp", axis=0)
+    heads = lax.all_gather(
+        jnp.concatenate([ref_head, policy_head], axis=1), "grp", axis=0, tiled=True
+    )
+
+    asking = send_rows(page_owner, lengths, resumed, my_group, core, state_c, ring)
+    asking, page_owner, page_slot = lax.optimization_barrier((asking, page_owner, page_slot))
+    saved_pages = after(asking, settled(saved_pages))
+    asking = lax.all_to_all(
+        asking, "grp", split_axis=0, concat_axis=0, tiled=True, axis_index_groups=lines
+    )
+    far_asking = lax.ppermute(asking, "vocab", other)
+    pages = [saved_pages]
+    for k in range(1, span):
+        pairs = [(i, (i + k * ring) % groups) for i in range(groups)]
+        pages.append(lax.ppermute(saved_pages, "grp", pairs))
 
     my_x, my_z = group >> 3, group & 7
     last = page_owner.shape[1] - 1
@@ -504,17 +599,7 @@
     first_page = ((my_x - (before_owner >> 3)) & (span - 1)) * slots + before_slot
     first_page = lax.dynamic_slice_in_dim(first_page, first_row, ring, 0)
     table = jnp.concatenate([found, first_page[:, None]], axis=1)
-    owners = lax.dynamic_index_in_dim(page_owner, group, 0, keepdims=False)
-    first_owner = lax.dynamic_slice_in_dim(before_owner, group, 1)
-
-    asking = send_rows(groups, lengths, owners, resumed, my_group, first_owner, state_c, ring)
-    asking = lax.all_to_all(
-        asking, "grp", split_axis=0, concat_axis=0, tiled=True, axis_index_groups=lines
-    )
-    pages = [saved_pages]
-    for k in range(1, span):
-        pairs = [(i, (i + k * ring) % groups) for i in range(groups)]
-        pages.append(lax.ppermute(saved_pages, "grp", pairs))
+
     per_head = jnp.broadcast_to(
         jnp.stack([decay_log, step_bias, skip_gain])[:, :, None], (3, decay_log.shape[0], tokens)
     )
@@ -522,23 +607,29 @@
         lengths, resumed, inner_x, gate_z, state_b, state_c, step_raw, per_head
     )
     carried = from_behind(ending, "grp", 1)
-    ref_normed = ref_norm(ref_hidden, ref_gain[None])
+    ref_normed = ref_norm(ref_hidden, ref_gain)
     target = jnp.broadcast_to(targets[:, None], (tokens, 128))
 
-    reads = page_reads(table, asking, pages)
+    reads = page_reads(table, core, asking, far_asking, pages)
     reads = lax.all_to_all(
         reads, "grp", split_axis=0, concat_axis=0, tiled=True, axis_index_groups=lines
     )
-    partial = project(
-        lengths, my_group, state_c, carried, reads, base, decay, norm_gain[None], out_weight
-    )
+    rails = [[k * 2 + c for k in range(parts // 2)] for c in range(2)]
+    theirs, ours = project(
+        lengths, my_group, core, state_c, carried, reads, base, decay, norm_gain, out_weight
+    )
+    summed = pair_sum(ours, lax.ppermute(theirs, "vocab", other))
     recv = lax.all_to_all(
-        partial.reshape(parts, tokens // parts, -1), "vocab", split_axis=0, concat_axis=0, tiled=True
-    )
-    mine = norm_rows(place, recv, residual, policy_gain[None])
-    normed = lax.all_to_all(mine, "vocab", split_axis=0, concat_axis=0, tiled=True)
-    normed = normed.reshape(tokens, -1)
-    stats = scores(place, ref_normed, normed, target, heads, parts)
+        summed.reshape(parts // 2, tokens // parts, -1), "vocab",
+        split_axis=0, concat_axis=0, tiled=True, axis_index_groups=rails,
+    )
+    mine = norm_rows(core * (parts // 2) + (place >> 1), recv, residual, policy_gain)
+    normed = lax.all_to_all(
+        mine, "vocab", split_axis=0, concat_axis=0, tiled=True, axis_index_groups=rails
+    )
+    normed = normed.reshape(tokens // 2, -1)
+    far = lax.ppermute(normed, "vocab", other)
+    stats = scores(place, core, ref_normed, normed, far, target, heads, parts)
     recv = lax.all_to_all(stats, "vocab", split_axis=0, concat_axis=0, tiled=True)
     return finish(lengths, recv)
 

time: 200 us -> 191 us (0.955)
  waiting for transfers between devices: 90 us -> 52.9 us
  blocking collectives: 12.5 us -> 36.9 us
  starting transfers between devices: 50.2 us -> 46.2 us
  local copies, waits for them, and re-layouts: 2.65 us -> 6.02 us
  Pallas kernels: 26.3 us -> 29.1 us
    all_to_all x2 -> x1, waiting for transfers between devices: 56.7 us -> 18.7 us  [body(): lax.all_to_all(summed.reshape(parts // 2, tokens // parts, -1), 'vocab',...]
    all_to_all x0 -> x1, blocking collectives: none -> 20.1 us  [body(): lax.all_to_all(mine, 'vocab', split_axis=0, concat_axis=0, tiled=True, ax...]
    ppermute x3, waiting for transfers between devices: 12.1 us -> 0.01 us  [body(): pages.append(lax.ppermute(saved_pages, 'grp', pairs))]
    ppermute x0 -> x3, starting transfers between devices: none -> 11.3 us  [the longest x1 6.01 us: body(): far_asking = lax.ppermute(asking, 'vocab', other)]
    all_to_all x2 -> x1, starting transfers between devices: 17.4 us -> 6.57 us  [body(): lax.all_to_all(summed.reshape(parts // 2, tokens // parts, -1), 'vocab',...]
    all_to_all x1, waiting for transfers between devices: 0.01 us -> 6.06 us  [body(): lax.all_to_all(asking, 'grp', split_axis=0, concat_axis=0, tiled=True, ax...]
    pallas_call x6 -> x8, Pallas kernels: 12.5 us -> 17 us  [the longest x7 16 us: call(): pl.pallas_call(kernel, out_shape=outs, grid_spec=pltpu.PrefetchScalarGrid...]
    all_to_all x1, starting transfers between devices: 8.01 us -> 3.56 us  [body(): lax.all_to_all(reads, 'grp', split_axis=0, concat_axis=0, tiled=True, axi...]
  transfers between devices with their start and end apart: 9 -> 11, of which waited for: 5 -> 6; matrix products, arithmetic and copies ran while one was open for 2% -> 4% of each run, Pallas kernels for 6% -> 9%
where the time goes in v3:
time: 191 us; the launch traced here: 190 us
  waiting for transfers between devices  52.9 us (28%)
  starting transfers between devices  46.2 us (24%)
  blocking collectives  36.9 us (19%)
  Pallas kernels  29.1 us (15%)
  between operations  14.2 us (7%)
  local copies, waits for them, and re-layouts  6.02 us (3%)
  other arithmetic  4.2 us (2%)
    ppermute x1, waiting for transfers between devices, from_behind(): return lax.ppermute(x, axis, pairs)  22.2 us
    all_to_all x1, blocking collectives, body(): lax.all_to_all(mine, 'vocab', split_axis=0, concat_axis=0, tiled=True, ax...  20.1 us
    all_to_all x1, waiting for transfers between devices, body(): lax.all_to_all(summed.reshape(parts // 2, tokens // parts, -1), 'vocab',...  18.7 us
    all_to_all x1, blocking collectives, body(): lax.all_to_all(stats, 'vocab', split_axis=0, concat_axis=0, tiled=True)  16.8 us
    pallas_call x7, Pallas kernels, call(): pl.pallas_call(kernel, out_shape=outs, grid_spec=pltpu.PrefetchScalarGrid...  16 us
    ppermute x3, starting transfers between devices, body(): pages.append(lax.ppermute(saved_pages, 'grp', pairs))  11.4 us
    pallas_call x1, Pallas kernels, scores(): pl.pallas_call(functools.partial(score_kernel, columns, tiles), out_shape...  11 us
    all_to_all x1, starting transfers between devices, body(): lax.all_to_all(asking, 'grp', split_axis=0, concat_axis=0, tiled=True, ax...  10 us
  transfers between devices with their start and end apart: 11, of which 6 were waited for; matrix products, arithmetic and copies ran while one was open for 4% of the time, Pallas kernels for 9%

profile of v3, /device:TPU:1, one launch (start us, length us, event | category | flops | bytes accessed | tf_op | source)
XLA Modules:
  0.0 189.5 jit_solution(5431234443734037950)
XLA Ops:
  7.2 1.9 %pad_maximum_fusion = bf16[64,3152]{1,0:T(8,128)(2,1)} fusion(bf16[64,1576]{1,0:T(8,128)(2,1)} %param.36, bf16[64,1576]{1,0:T(8,128)(2,1)} %param.37), kind=kLoop, calls=%fused_computation | loop fusion | flops 806912 | bytes 806912 | tf_op jit(solution)/shard_map/concatenate | solution.py:573
  9.9 2.7 %send_rows.1._ = bf16[8,144,128]{2,1,0:T(8,128)(2,1)} custom-call(s32[32,16]{1,0:T(8,128)S(1)} %copy.28.own_ref, s32[1,16]{1,0:T(1,128)} %len_ref.7, s32[1,16]{1,0:T(1,128)} %res_ref.4, s32[1]{0:T(128)} %bitcast.2.group_ref, s32[1]{0:T(128)S(6)} %and.18.core_ref, bf16[256,128]{1,0:T(8,128)(2,1)} %c_ref.5), custom_call_target="tpu_custom_call" | custom-call | flops 100000 | bytes 700000 | tf_op jit(solution)/shard_map/send_rows/pallas_call | solution.py:36
  13.6 3.9 %collective-permute-start.2 = (bf16[4,256,128]{2,1,0:T(8,128)(2,1)S(1)}, bf16[4,256,128]{2,1,0:T(8,128)(2,1)S(1)}, u32[]{:S(2)}, u32[]{:S(2)}) collective-permute-start(bf16[4,256,128]{2,1,0:T(8,128)(2,1)S(1)} %after.1.refs_0_), channel_id=1, source_target_pairs={{0,128},{16,144},{32,160},{48,176},{64,192},{80,208},{96,224},{112... | collective-permute-start | bytes 786440 | tf_op jit(solution)/shard_map/ppermute | solution.py:586
  17.6 4.4 %collective-permute-start.3 = (bf16[4,256,128]{2,1,0:T(8,128)(2,1)S(1)}, bf16[4,256,128]{2,1,0:T(8,128)(2,1)S(1)}, u32[]{:S(2)}, u32[]{:S(2)}) collective-permute-start(bf16[4,256,128]{2,1,0:T(8,128)(2,1)S(1)} %after.1.refs_0_), channel_id=1, source_target_pairs={{0,256},{16,272},{32,288},{48,304},{64,320},{80,336},{96,352},{112... | collective-permute-start | bytes 786440 | tf_op jit(solution)/shard_map/ppermute | solution.py:586
  21.9 3.1 %collective-permute-start.4 = (bf16[4,256,128]{2,1,0:T(8,128)(2,1)S(1)}, bf16[4,256,128]{2,1,0:T(8,128)(2,1)S(1)}, u32[]{:S(2)}, u32[]{:S(2)}) collective-permute-start(bf16[4,256,128]{2,1,0:T(8,128)(2,1)S(1)} %after.1.refs_0_), channel_id=1, source_target_pairs={{0,384},{16,400},{32,416},{48,432},{64,448},{80,464},{96,480},{112... | collective-permute-start | bytes 786440 | tf_op jit(solution)/shard_map/ppermute | solution.py:586
  25.0 10.0 %all-to-all-start = ((bf16[8,144,128]{2,1,0:T(8,128)(2,1)}), bf16[8,144,128]{2,1,0:T(8,128)(2,1)S(1)}, u32[]{:S(2)}, u32[]{:S(2)}) async-start(bf16[8,144,128]{2,1,0:T(8,128)(2,1)} %send_rows.1._), calls=%async_computation | async-start | bytes 589824 | tf_op jit(solution)/shard_map/all_to_all | solution.py:579
  41.6 6.1 %all-to-all-done.own_ref = bf16[8,144,128]{2,1,0:T(8,128)(2,1)S(1)} async-done(((bf16[8,144,128]{2,1,0:T(8,128)(2,1)}), bf16[8,144,128]{2,1,0:T(8,128)(2,1)S(1)}, u32[]{:S(2)}, u32[]{:S(2)}) %all-to-all-start) | async-done | bytes 294944 | tf_op jit(solution)/shard_map/all_to_all | solution.py:579
  47.7 6.0 %collective-permute-start.1 = (bf16[8,144,128]{2,1,0:T(8,128)(2,1)S(1)}, bf16[8,144,128]{2,1,0:T(8,128)(2,1)S(1)}, u32[]{:S(2)}, u32[]{:S(2)}) collective-permute-start(bf16[8,144,128]{2,1,0:T(8,128)(2,1)S(1)} %all-to-all-done.own_ref), channel_id=1, source_target_pairs={{0,1},{1,0},{2,3},{3,2},{4,5},{5,4},{6,7},{7,6},{8,9},{9,8},{10,11... | collective-permute-start | bytes 884744 | tf_op jit(solution)/shard_map/ppermute | solution.py:582
  54.9 2.9 %page_reads.1 = bf16[8,256,256]{2,1,0:T(8,128)(2,1)} custom-call(s32[8,5]{1,0:T(8,128)S(1)} %pad_add_fusion.table_ref, s32[1]{0:T(128)S(6)} %and.18.core_ref, bf16[8,144,128]{2,1,0:T(8,128)(2,1)S(1)} %all-to-all-done.own_ref, bf16[8,144,128]{2,1,0:T(8,128)(2,1)S(1)} %collective-permute-done.1.far_ref, bf16[4,256,128]{2,1,0:T(8,128)(2,1)S(1)} %after.1.refs_0_, ...), custom_call_target="tpu_custom_call" | custom-call | flops 700000000 | bytes 3000000 | tf_op jit(solution)/shard_map/page_reads/pallas_call | solution.py:36
  57.8 3.6 %all-to-all-start.1 = ((bf16[8,256,256]{2,1,0:T(8,128)(2,1)}), bf16[8,256,256]{2,1,0:T(8,128)(2,1)S(1)}, u32[]{:S(2)}, u32[]{:S(2)}) async-start(bf16[8,256,256]{2,1,0:T(8,128)(2,1)} %page_reads.1), calls=%async_computation.1 | async-start | bytes 2097152 | tf_op jit(solution)/shard_map/all_to_all | solution.py:614
  62.2 3.4 %scan_parts.1 = (f32[256,256]{1,0:T(8,128)S(1)}, f32[256,256]{1,0:T(8,128)S(1)}, f32[264,128]{1,0:T(8,128)S(1)}) custom-call(s32[1,16]{1,0:T(1,128)} %len_ref.7, s32[1,16]{1,0:T(1,128)} %res_ref.4, bf16[256,256]{1,0:T(8,128)(2,1)} %x_ref.3, bf16[256,256]{1,0:T(8,128)(2,1)} %z_ref.1, bf16[256,128]{1,0:T(8,128)(2,1)} %b_ref.1, bf16[256,128]{1,0:T(8,128)(2,1)} %c_ref.5, ...), custom_call_target="tpu_custom_call" | custom-call | flops 400000000 | bytes 2000000 | tf_op jit(solution)/shard_map/scan_parts/pallas_call | solution.py:36
  65.5 3.3 %collective-permute-start = (f32[264,128]{1,0:T(8,128)S(1)}, f32[264,128]{1,0:T(8,128)S(1)}, u32[]{:S(2)}, u32[]{:S(2)}) collective-permute-start(f32[264,128]{1,0:T(8,128)S(1)} %get-tuple-element.10), channel_id=1, source_target_pairs={{0,16},{16,32},{32,48},{48,64},{64,80},{80,96},{96,112},{112,128},... | collective-permute-start | bytes 405512 | tf_op jit(solution)/shard_map/ppermute | solution.py:527
  68.8 22.2 %collective-permute-done.carry_ref = f32[264,128]{1,0:T(8,128)S(1)} collective-permute-done((f32[264,128]{1,0:T(8,128)S(1)}, f32[264,128]{1,0:T(8,128)S(1)}, u32[]{:S(2)}, u32[]{:S(2)}) %collective-permute-start) | collective-permute-done | bytes 135200 | tf_op jit(solution)/shard_map/ppermute | solution.py:527
  91.0 2.8 %project.1 = (bf16[128,2176]{1,0:T(8,128)(2,1)S(1)}, bf16[128,2176]{1,0:T(8,128)(2,1)S(1)}) custom-call(s32[1,16]{1,0:T(1,128)} %len_ref.7, s32[1]{0:T(128)} %bitcast.2.group_ref, s32[1]{0:T(128)S(6)} %and.18.core_ref, bf16[256,128]{1,0:T(8,128)(2,1)} %c_ref.5, f32[264,128]{1,0:T(8,128)S(1)} %collective-permute-done.carry_ref, ...), custom_call_target="tpu_custom_call" | custom-call | flops 300000000 | bytes 3500000 | tf_op jit(solution)/shard_map/project/pallas_call | solution.py:36
  93.9 2.7 %collective-permute-start.5 = (bf16[128,2176]{1,0:T(8,128)(2,1)S(1)}, bf16[128,2176]{1,0:T(8,128)(2,1)S(1)}, u32[]{:S(2)}, u32[]{:S(2)}) collective-permute-start(bf16[128,2176]{1,0:T(8,128)(2,1)S(1)} %get-tuple-element.17), channel_id=1, source_target_pairs={{0,1},{1,0},{2,3},{3,2},{4,5},{5,4},{6,7},{7,6},{8,9},{9,8},{10,11... | collective-permute-start | bytes 1671176 | tf_op jit(solution)/shard_map/ppermute | solution.py:621
  96.5 1.6 collective-permute-done.5.b_ref
  99.3 6.6 %all-to-all-start.2 = ((bf16[8,16,2176]{2,1,0:T(8,128)(2,1)}), bf16[8,16,2176]{2,1,0:T(8,128)(2,1)S(1)}, u32[]{:S(2)}, u32[]{:S(2)}) async-start(bf16[8,16,2176]{2,1,0:T(8,128)(2,1)} %bitcast.12), calls=%async_computation.2 | async-start | bytes 1114112 | tf_op jit(solution)/shard_map/all_to_all | solution.py:622
  105.9 18.7 %all-to-all-done.2.recv_ref = bf16[8,16,2176]{2,1,0:T(8,128)(2,1)S(1)} async-done(((bf16[8,16,2176]{2,1,0:T(8,128)(2,1)}), bf16[8,16,2176]{2,1,0:T(8,128)(2,1)S(1)}, u32[]{:S(2)}, u32[]{:S(2)}) %all-to-all-start.2) | async-done | bytes 557088 | tf_op jit(solution)/shard_map/all_to_all | solution.py:622
  125.7 20.1 %all_to_all.25 = bf16[8,16,2048]{2,1,0:T(8,128)(2,1)S(1)} all-to-all(bf16[8,16,2048]{2,1,0:T(8,128)(2,1)S(1)} %norm_rows.1), channel_id=1, replica_groups={{0,2,4,6,8,10,12,14},{1,3,5,7,9,11,13,15},{16,18,20,22,24,26,28,30},{17..., dimensions={0} | all-to-all | bytes 1048576 | tf_op jit(solution)/shard_map/all_to_all | solution.py:627
  145.8 2.6 %collective-permute-start.6 = (bf16[128,2048]{1,0:T(8,128)(2,1)S(1)}, bf16[128,2048]{1,0:T(8,128)(2,1)S(1)}, u32[]{:S(2)}, u32[]{:S(2)}) collective-permute-start(bf16[128,2048]{1,0:T(8,128)(2,1)S(1)} %bitcast.18), channel_id=1, source_target_pairs={{0,1},{1,0},{2,3},{3,2},{4,5},{5,4},{6,7},{7,6},{8,9},{9,8},{10,11... | collective-permute-start | bytes 1572872 | tf_op jit(solution)/shard_map/ppermute | solution.py:631
  148.4 1.6 ref_norm.1.ref_ref
  150.1 3.3 %all-gather.2.cloned.1.call-done.head_ref = bf16[2048,3152]{1,0:T(8,128)(2,1)} async-done(((bf16[64,3152]{1,0:T(8,128)(2,1)}), bf16[2048,3152]{1,0:T(8,128)(2,1)}) %all-gather.2.cloned.1.call-update) | async-done | bytes 12910608 | tf_op jit(solution)/shard_map/all_gather | solution.py:572
  153.5 11.0 %scores.1 = f32[16,8,256]{2,1,0:T(8,128)S(1)} custom-call(s32[1]{0:T(128)} %bitcast.place_ref, s32[1]{0:T(128)S(6)} %and.18.core_ref, bf16[256,2048]{1,0:T(8,128)(2,1)S(1)} %ref_norm.1.ref_ref, bf16[128,2048]{1,0:T(8,128)(2,1)S(1)} %bitcast.19, bf16[128,2048]{1,0:T(8,128)(2,1)S(1)} %collective-permute-done.6.far_ref, ...), custom_call_target="tpu_custom_call" | custom-call | flops 3400000000 | bytes 15000000 | tf_op jit(solution)/shard_map/scores/pallas_call | solution.py:455
  164.5 16.8 %all_to_all.26.recv_ref = f32[16,8,256]{2,1,0:T(8,128)S(1)} all-to-all(f32[16,8,256]{2,1,0:T(8,128)S(1)} %scores.1), channel_id=1, replica_groups=mesh['grp'=32,'vocab'=16] {'vocab'}, dimensions={0} | all-to-all | bytes 262144 | tf_op jit(solution)/shard_map/all_to_all | solution.py:633
  (34 shorter events, 14.2 us)
Async XLA Ops:
  7.2 146.2 %copy-start = (s32[256]{0:T(256)S(1)}, s32[256]{0:T(256)}, u32[]{:S(2)}) copy-start(s32[256]{0:T(256)} %param.43) | copy-start | bytes 3076
  7.2 146.2 %all-gather.2.cloned.1.call-start = ((), (), s32[]{:S(2)}) async-start(), calls=%async_computation.5 | async-start | bytes 13516800 | tf_op jit(solution)/shard_map/all_gather | solution.py:572
  13.6 40.2 %collective-permute-start.2 = (bf16[4,256,128]{2,1,0:T(8,128)(2,1)S(1)}, bf16[4,256,128]{2,1,0:T(8,128)(2,1)S(1)}, u32[]{:S(2)}, u32[]{:S(2)}) collective-permute-start(bf16[4,256,128]{2,1,0:T(8,128)(2,1)S(1)} %after.1.refs_0_), channel_id=1, source_target_pairs={{0,128},{16,144},{32,160},{48,176},{64,192},{80,208},{96,224},{112... | collective-permute-start | bytes 786440 | tf_op jit(solution)/shard_map/ppermute | solution.py:586
  17.6 36.3 %collective-permute-start.3 = (bf16[4,256,128]{2,1,0:T(8,128)(2,1)S(1)}, bf16[4,256,128]{2,1,0:T(8,128)(2,1)S(1)}, u32[]{:S(2)}, u32[]{:S(2)}) collective-permute-start(bf16[4,256,128]{2,1,0:T(8,128)(2,1)S(1)} %after.1.refs_0_), channel_id=1, source_target_pairs={{0,256},{16,272},{32,288},{48,304},{64,320},{80,336},{96,352},{112... | collective-permute-start | bytes 786440 | tf_op jit(solution)/shard_map/ppermute | solution.py:586
  21.9 31.9 %collective-permute-start.4 = (bf16[4,256,128]{2,1,0:T(8,128)(2,1)S(1)}, bf16[4,256,128]{2,1,0:T(8,128)(2,1)S(1)}, u32[]{:S(2)}, u32[]{:S(2)}) collective-permute-start(bf16[4,256,128]{2,1,0:T(8,128)(2,1)S(1)} %after.1.refs_0_), channel_id=1, source_target_pairs={{0,384},{16,400},{32,416},{48,432},{64,448},{80,464},{96,480},{112... | collective-permute-start | bytes 786440 | tf_op jit(solution)/shard_map/ppermute | solution.py:586
  25.0 22.7 %all-to-all-start = ((bf16[8,144,128]{2,1,0:T(8,128)(2,1)}), bf16[8,144,128]{2,1,0:T(8,128)(2,1)S(1)}, u32[]{:S(2)}, u32[]{:S(2)}) async-start(bf16[8,144,128]{2,1,0:T(8,128)(2,1)} %send_rows.1._), calls=%async_computation | async-start | bytes 589824 | tf_op jit(solution)/shard_map/all_to_all | solution.py:579
  47.7 7.2 %collective-permute-start.1 = (bf16[8,144,128]{2,1,0:T(8,128)(2,1)S(1)}, bf16[8,144,128]{2,1,0:T(8,128)(2,1)S(1)}, u32[]{:S(2)}, u32[]{:S(2)}) collective-permute-start(bf16[8,144,128]{2,1,0:T(8,128)(2,1)S(1)} %all-to-all-done.own_ref), channel_id=1, source_target_pairs={{0,1},{1,0},{2,3},{3,2},{4,5},{5,4},{6,7},{7,6},{8,9},{9,8},{10,11... | collective-permute-start | bytes 884744 | tf_op jit(solution)/shard_map/ppermute | solution.py:582
  57.8 33.2 %all-to-all-start.1 = ((bf16[8,256,256]{2,1,0:T(8,128)(2,1)}), bf16[8,256,256]{2,1,0:T(8,128)(2,1)S(1)}, u32[]{:S(2)}, u32[]{:S(2)}) async-start(bf16[8,256,256]{2,1,0:T(8,128)(2,1)} %page_reads.1), calls=%async_computation.1 | async-start | bytes 2097152 | tf_op jit(solution)/shard_map/all_to_all | solution.py:614
  65.5 25.5 %collective-permute-start = (f32[264,128]{1,0:T(8,128)S(1)}, f32[264,128]{1,0:T(8,128)S(1)}, u32[]{:S(2)}, u32[]{:S(2)}) collective-permute-start(f32[264,128]{1,0:T(8,128)S(1)} %get-tuple-element.10), channel_id=1, source_target_pairs={{0,16},{16,32},{32,48},{48,64},{64,80},{80,96},{96,112},{112,128},... | collective-permute-start | bytes 405512 | tf_op jit(solution)/shard_map/ppermute | solution.py:527
  93.9 4.2 %collective-permute-start.5 = (bf16[128,2176]{1,0:T(8,128)(2,1)S(1)}, bf16[128,2176]{1,0:T(8,128)(2,1)S(1)}, u32[]{:S(2)}, u32[]{:S(2)}) collective-permute-start(bf16[128,2176]{1,0:T(8,128)(2,1)S(1)} %get-tuple-element.17), channel_id=1, source_target_pairs={{0,1},{1,0},{2,3},{3,2},{4,5},{5,4},{6,7},{7,6},{8,9},{9,8},{10,11... | collective-permute-start | bytes 1671176 | tf_op jit(solution)/shard_map/ppermute | solution.py:621
  99.3 25.2 %all-to-all-start.2 = ((bf16[8,16,2176]{2,1,0:T(8,128)(2,1)}), bf16[8,16,2176]{2,1,0:T(8,128)(2,1)S(1)}, u32[]{:S(2)}, u32[]{:S(2)}) async-start(bf16[8,16,2176]{2,1,0:T(8,128)(2,1)} %bitcast.12), calls=%async_computation.2 | async-start | bytes 1114112 | tf_op jit(solution)/shard_map/all_to_all | solution.py:622
  145.8 4.3 %collective-permute-start.6 = (bf16[128,2048]{1,0:T(8,128)(2,1)S(1)}, bf16[128,2048]{1,0:T(8,128)(2,1)S(1)}, u32[]{:S(2)}, u32[]{:S(2)}) collective-permute-start(bf16[128,2048]{1,0:T(8,128)(2,1)S(1)} %bitcast.18), channel_id=1, source_target_pairs={{0,1},{1,0},{2,3},{3,2},{4,5},{5,4},{6,7},{7,6},{8,9},{9,8},{10,11... | collective-permute-start | bytes 1572872 | tf_op jit(solution)/shard_map/ppermute | solution.py:631
Sparse Core Ops, SparseCore 0:
  11.2 142.1 all-gather.1

commit v4 on v3

--- a/solution.py
+++ b/solution.py
@@ -349,130 +349,102 @@
 
 
 def score_kernel(
-    columns, tiles, place_ref, core_ref, ref_ref, own_ref, far_ref, target_ref, head_ref, out_ref,
-    rows, logits, tops, sums, picks, stats,
+    columns, block, place_ref, core_ref, ref_ref, own_ref, far_ref, target_ref, head_ref, out_ref,
+    head, rows, logits_a, logits_b, tops, sums, picks, sems,
 ):
-    step = pl.program_id(0)
-    steps = pl.num_programs(0)
-    block = head_ref.shape[1]
+    wide = head.shape[1]
     low = float(jnp.finfo(F32).min)
-
-    @pl.when(step == 0)
-    def _():
-        rows[...] = ref_ref[...]
-        stats[...] = jnp.zeros_like(stats)
-
-    @pl.when(step == tiles)
-    def _():
-        half = own_ref.shape[0]
-        rows[pl.ds(pl.multiple_of(core_ref[0] * half, half), half)] = own_ref[...]
-        rows[pl.ds(pl.multiple_of((1 - core_ref[0]) * half, half), half)] = far_ref[...]
-
-    @pl.when(lax.rem(step + tiles - 1, tiles) == 0)
-    def _():
-        tops[...] = jnp.full_like(tops, low)
-        sums[...] = jnp.zeros_like(sums)
-        picks[...] = jnp.zeros_like(picks)
-
-    before = jnp.maximum(step - 1, 0)
-    tile = lax.rem(before, tiles)
-    old_slot = lax.rem(step + 1, 2)
+    cuts = [(c, min(c + block, wide)) for c in range(0, wide, block)]
+    copies = []
+    for k, (c, d) in enumerate(cuts):
+        copies.append(pltpu.make_async_copy(head_ref.at[:, c:d], head.at[:, c:d], sems.at[k]))
+        copies[-1].start()
+    half = own_ref.shape[0]
+    rows[pl.ds(pl.multiple_of(core_ref[0] * half, half), half)] = own_ref[...]
+    rows[pl.ds(pl.multiple_of((1 - core_ref[0]) * half, half), half)] = far_ref[...]
+    tops[...] = jnp.full_like(tops, low)
+    sums[...] = jnp.zeros_like(sums)
+    picks[...] = jnp.zeros_like(picks)
+    jobs = []
+    for model in range(2):
+        first, stop = model * columns, (model + 1) * columns
+        for k, (c, d) in enumerate(cuts):
+            if c < stop and d > first:
+                jobs.append((model, k, c, min(d, (stop + 127) // 128 * 128)))
     lane = lax.broadcasted_iota(jnp.int32, target_ref.shape, 1)
-    model = before // tiles
-    first = model * columns
-    begin = (first // block + tile) * block
-    rest = max(columns - (tiles - 1) * block, 2 * columns - (columns // block + tiles - 1) * block)
-    rest = (rest + 255) // 256 * 256
-
-    def work(width):
-        wanted = target_ref[...] - place_ref[0] * columns + first - begin
-        floor = first - begin
-        room = floor + columns
-        pieces, pick = [], picks[...]
-        top = tops[...]
-        for k in range(block // 128):
-            here = lane + k * 128
-            piece = logits[old_slot, :, k * 128 : (k + 1) * 128]
-            inside = jnp.logical_and(here >= floor, here < room)
-            piece = jnp.where(inside, piece, low)
-            pick = pick + jnp.where(jnp.logical_and(here == wanted, inside), piece, 0.0)
+    local = target_ref[...] - place_ref[0] * columns
+    local = jnp.where(jnp.logical_and(local >= 0, local < columns), local, -2 * wide)
+
+    def statistics(job, logits):
+        model, _, c, d = job
+        first, stop = model * columns, (model + 1) * columns
+        wanted = local + (first - c)
+        old = tops[model]
+        top, pick, pieces = old, picks[model], []
+        for k in range((d - c) // 128):
+            start = c + k * 128
+            piece = logits[:, k * 128 : (k + 1) * 128]
+            if start < first:
+                piece = jnp.where(lane >= first - start, piece, low)
+            if start + 128 > stop:
+                piece = jnp.where(lane < stop - start, piece, low)
+            pick = pick + jnp.where(lane == wanted - k * 128, piece, 0.0)
             pieces.append(piece)
             top = jnp.maximum(top, piece)
-        total = sums[...] * jnp.exp(tops[...] - top)
+        total = sums[model] * jnp.exp(old - top)
         for piece in pieces:
             total = total + jnp.exp(piece - top)
-        if width:
-            logits[lax.rem(step, 2), :, :width] = jnp.dot(
-                rows[...], head_ref[:, :width], preferred_element_type=F32
-            )
-        tops[...] = top
-        sums[...] = total
-        picks[...] = pick
-
-    is_rest = lax.rem(step, tiles) == tiles - 1
-
-    @pl.when(jnp.logical_and(step < steps - 1, jnp.logical_not(is_rest)))
-    def _():
-        work(block)
-
-    @pl.when(jnp.logical_and(step < steps - 1, is_rest))
-    def _():
-        work(min(rest, block))
-
-    @pl.when(step == steps - 1)
-    def _():
-        work(0)
-
-    @pl.when(jnp.logical_and(tile == tiles - 1, step > 0))
-    def _():
-        at = 3 * model
-        top, total, pick = tops[...], sums[...], picks[...]
-        peak = jnp.max(top, axis=1, keepdims=True)
-        whole = jnp.sum(total * jnp.exp(top - peak), axis=1, keepdims=True)
-        chosen = jnp.sum(pick, axis=1, keepdims=True)
-        new = jnp.where(lane == at, peak, stats[...])
-        new = jnp.where(lane == at + 1, whole, new)
-        stats[...] = jnp.where(lane == at + 2, chosen, new)
-
-    @pl.when(step == steps - 1)
-    def _():
-        out_ref[...] = jnp.broadcast_to(stats[...].T[:8, :][None], out_ref.shape)
-
-
-def scores(place, core, ref_rows, own_rows, far_rows, target, heads, parts):
-    models, columns = 2, heads.shape[1] // 2
-    tokens, depth = ref_rows.shape
+        tops[model] = top
+        sums[model] = total
+        picks[model] = pick
+
+    waited = set()
+    for i, job in enumerate(jobs):
+        model, k, c, d = job
+        if k not in waited:
+            copies[k].wait()
+            waited.add(k)
+        logits = (logits_a, logits_b)[i % 2]
+        left = ref_ref if model == 0 else rows
+        logits[:, : d - c] = jnp.dot(left[...], head[:, c:d], preferred_element_type=F32)
+        if i:
+            statistics(jobs[i - 1], (logits_a, logits_b)[(i - 1) % 2])
+    statistics(jobs[-1], (logits_a, logits_b)[(len(jobs) - 1) % 2])
+    stats = jnp.zeros(target_ref.shape, F32)
+    for model in range(2):
+        peak = jnp.max(tops[model], axis=1, keepdims=True)
+        whole_sum = jnp.sum(sums[model] * jnp.exp(tops[model] - peak), axis=1, keepdims=True)
+        chosen = jnp.sum(picks[model], axis=1, keepdims=True)
+        stats = jnp.where(lane == 3 * model, peak, stats)
+        stats = jnp.where(lane == 3 * model + 1, whole_sum, stats)
+        stats = jnp.where(lane == 3 * model + 2, chosen, stats)
+    out_ref[...] = jnp.broadcast_to(stats.T[:8, :][None], out_ref.shape)
+
+
+def scores(place, core, ref_rows, own_rows, far_rows, target, heads, columns, parts):
+    depth, wide = heads.shape
+    tokens = ref_rows.shape[0]
     block = 512
-    tiles = pl.cdiv(columns, block)
-    assert pl.cdiv(2 * columns, block) - columns // block == tiles
-    last = models * tiles - 1
-    plain = pltpu.VMEM((tokens, 128), F32)
-
-    def head_at(i, p, c):
-        now = jnp.minimum(i, last)
-        return (0, now // tiles * columns // block + lax.rem(now, tiles))
-
+    state = pltpu.VMEM((2, tokens, 128), F32)
+    out = jax.ShapeDtypeStruct((parts, 8, tokens), F32)
     return pl.pallas_call(
-        functools.partial(score_kernel, columns, tiles),
-        out_shape=jax.ShapeDtypeStruct((parts, 8, tokens), F32),
+        functools.partial(score_kernel, columns, block),
+        out_shape=out,
         grid_spec=pltpu.PrefetchScalarGridSpec(
             num_scalar_prefetch=2,
-            grid=(models * tiles + 1,),
-            in_specs=[
-                pl.BlockSpec((tokens, depth), lambda i, p, c: (0, 0)),
-                pl.BlockSpec((tokens // 2, depth), lambda i, p, c: (0, 0)),
-                pl.BlockSpec((tokens // 2, depth), lambda i, p, c: (0, 0)),
-                pl.BlockSpec((tokens, 128), lambda i, p, c: (0, 0)),
-                pl.BlockSpec((depth, block), head_at),
-            ],
-            out_specs=pl.BlockSpec((parts, 8, tokens), lambda i, p, c: (0, 0, 0)),
+            grid=(1,),
+            in_specs=[whole(x) for x in (ref_rows, own_rows, far_rows, target)]
+            + [pl.BlockSpec(memory_space=pltpu.HBM)],
+            out_specs=whole(out),
             scratch_shapes=[
+                pltpu.VMEM((depth, wide), BF16),
                 pltpu.VMEM((tokens, depth), BF16),
-                pltpu.VMEM((2, tokens, block), F32),
-                plain,
-                plain,
-                plain,
-                plain,
+                pltpu.VMEM((tokens, block), F32),
+                pltpu.VMEM((tokens, block), F32),
+                state,
+                state,
+                state,
+                pltpu.SemaphoreType.DMA((pl.cdiv(wide, block),)),
             ],
         ),
         compiler_params=params(),
@@ -569,8 +541,10 @@
     ring = 8
     span = groups // ring
     lines = [[x * ring + k for k in range(ring)] for x in range(span)]
+    deep, columns = policy_head.shape
+    spare = jnp.zeros((deep, -2 * columns % 128), policy_head.dtype)
     heads = lax.all_gather(
-        jnp.concatenate([ref_head, policy_head], axis=1), "grp", axis=0, tiled=True
+        jnp.concatenate([ref_head, policy_head, spare], axis=1), "grp", axis=0, tiled=True
     )
 
     asking = send_rows(page_owner, lengths, resumed, my_group, core, state_c, ring)
@@ -629,7 +603,7 @@
     )
     normed = normed.reshape(tokens // 2, -1)
     far = lax.ppermute(normed, "vocab", other)
-    stats = scores(place, core, ref_normed, normed, far, target, heads, parts)
+    stats = scores(place, core, ref_normed, normed, far, target, heads, columns, parts)
     recv = lax.all_to_all(stats, "vocab", split_axis=0, concat_axis=0, tiled=True)
     return finish(lengths, recv)
 

time: 191 us -> 187 us (0.979)
  Pallas kernels: 29.1 us -> 25.7 us
  waiting for transfers between devices: 52.9 us -> 50.7 us
  starting transfers between devices: 46.2 us -> 48.2 us
  local copies, waits for them, and re-layouts: 6.02 us -> 8 us
    pallas_call x1, Pallas kernels: 11 us -> 7.57 us  [scores(): pl.pallas_call(functools.partial(score_kernel, columns, block), out_shape...]
    concatenate x0 -> x1, local copies, waits for them, and re-layouts: none -> 1.98 us  [body(): jnp.concatenate([ref_head, policy_head, spare], axis=1)]
where the time goes in v4:
time: 187 us; the launch traced here: 186 us
  waiting for transfers between devices  50.7 us (27%)
  starting transfers between devices  48.2 us (26%)
  blocking collectives  36.9 us (20%)
  Pallas kernels  25.7 us (14%)
  between operations  14.2 us (8%)
  local copies, waits for them, and re-layouts  8 us (4%)
  other arithmetic  2.3 us (1%)
    ppermute x1, waiting for transfers between devices, from_behind(): return lax.ppermute(x, axis, pairs)  21 us
    all_to_all x1, blocking collectives, body(): lax.all_to_all(mine, 'vocab', split_axis=0, concat_axis=0, tiled=True, ax...  20.1 us
    all_to_all x1, waiting for transfers between devices, body(): lax.all_to_all(summed.reshape(parts // 2, tokens // parts, -1), 'vocab',...  18.7 us
    all_to_all x1, blocking collectives, body(): lax.all_to_all(stats, 'vocab', split_axis=0, concat_axis=0, tiled=True)  16.8 us
    pallas_call x7, Pallas kernels, call(): pl.pallas_call(kernel, out_shape=outs, grid_spec=pltpu.PrefetchScalarGrid...  16 us
    ppermute x3, starting transfers between devices, body(): pages.append(lax.ppermute(saved_pages, 'grp', pairs))  11.4 us
    all_to_all x1, starting transfers between devices, body(): lax.all_to_all(asking, 'grp', split_axis=0, concat_axis=0, tiled=True, ax...  10 us
    pallas_call x1, Pallas kernels, scores(): pl.pallas_call(functools.partial(score_kernel, columns, block), out_shape...  7.57 us
  transfers between devices with their start and end apart: 11, of which 6 were waited for; matrix products, arithmetic and copies ran while one was open for 4% of the time, Pallas kernels for 9%

profile of v4, /device:TPU:1, one launch (start us, length us, event | category | flops | bytes accessed | tf_op | source)
XLA Modules:
  0.0 186.0 jit_solution(3886468267445904257)
XLA Ops:
  7.2 2.0 %concatenate.15 = bf16[64,3200]{1,0:T(8,128)(2,1)} concatenate(bf16[64,1576]{1,0:T(8,128)(2,1)} %param.37, bf16[64,1576]{1,0:T(8,128)(2,1)} %param.36, bf16[64,48]{1,0:T(8,128)(2,1)S(1)} %broadcast_in_dim.59), dimensions={1} | concatenate | bytes 819200 | tf_op jit(solution)/shard_map/concatenate | solution.py:547
  10.0 2.7 %send_rows.1._ = bf16[8,144,128]{2,1,0:T(8,128)(2,1)} custom-call(s32[32,16]{1,0:T(8,128)S(1)} %copy.28.own_ref, s32[1,16]{1,0:T(1,128)} %len_ref.7, s32[1,16]{1,0:T(1,128)} %res_ref.4, s32[1]{0:T(128)} %bitcast.2.group_ref, s32[1]{0:T(128)S(6)} %and.18.core_ref, bf16[256,128]{1,0:T(8,128)(2,1)} %c_ref.5), custom_call_target="tpu_custom_call" | custom-call | flops 100000 | bytes 700000 | tf_op jit(solution)/shard_map/send_rows/pallas_call | solution.py:36
  13.7 3.9 %collective-permute-start.2 = (bf16[4,256,128]{2,1,0:T(8,128)(2,1)S(1)}, bf16[4,256,128]{2,1,0:T(8,128)(2,1)S(1)}, u32[]{:S(2)}, u32[]{:S(2)}) collective-permute-start(bf16[4,256,128]{2,1,0:T(8,128)(2,1)S(1)} %after.1.refs_0_), channel_id=1, source_target_pairs={{0,128},{16,144},{32,160},{48,176},{64,192},{80,208},{96,224},{112... | collective-permute-start | bytes 786440 | tf_op jit(solution)/shard_map/ppermute | solution.py:560
  17.6 4.4 %collective-permute-start.3 = (bf16[4,256,128]{2,1,0:T(8,128)(2,1)S(1)}, bf16[4,256,128]{2,1,0:T(8,128)(2,1)S(1)}, u32[]{:S(2)}, u32[]{:S(2)}) collective-permute-start(bf16[4,256,128]{2,1,0:T(8,128)(2,1)S(1)} %after.1.refs_0_), channel_id=1, source_target_pairs={{0,256},{16,272},{32,288},{48,304},{64,320},{80,336},{96,352},{112... | collective-permute-start | bytes 786440 | tf_op jit(solution)/shard_map/ppermute | solution.py:560
  22.0 3.1 %collective-permute-start.4 = (bf16[4,256,128]{2,1,0:T(8,128)(2,1)S(1)}, bf16[4,256,128]{2,1,0:T(8,128)(2,1)S(1)}, u32[]{:S(2)}, u32[]{:S(2)}) collective-permute-start(bf16[4,256,128]{2,1,0:T(8,128)(2,1)S(1)} %after.1.refs_0_), channel_id=1, source_target_pairs={{0,384},{16,400},{32,416},{48,432},{64,448},{80,464},{96,480},{112... | collective-permute-start | bytes 786440 | tf_op jit(solution)/shard_map/ppermute | solution.py:560
  25.1 10.0 %all-to-all-start = ((bf16[8,144,128]{2,1,0:T(8,128)(2,1)}), bf16[8,144,128]{2,1,0:T(8,128)(2,1)S(1)}, u32[]{:S(2)}, u32[]{:S(2)}) async-start(bf16[8,144,128]{2,1,0:T(8,128)(2,1)} %send_rows.1._), calls=%async_computation | async-start | bytes 589824 | tf_op jit(solution)/shard_map/all_to_all | solution.py:553
  41.7 5.2 %all-to-all-done.own_ref = bf16[8,144,128]{2,1,0:T(8,128)(2,1)S(1)} async-done(((bf16[8,144,128]{2,1,0:T(8,128)(2,1)}), bf16[8,144,128]{2,1,0:T(8,128)(2,1)S(1)}, u32[]{:S(2)}, u32[]{:S(2)}) %all-to-all-start) | async-done | bytes 294944 | tf_op jit(solution)/shard_map/all_to_all | solution.py:553
  46.9 6.8 %collective-permute-start.1 = (bf16[8,144,128]{2,1,0:T(8,128)(2,1)S(1)}, bf16[8,144,128]{2,1,0:T(8,128)(2,1)S(1)}, u32[]{:S(2)}, u32[]{:S(2)}) collective-permute-start(bf16[8,144,128]{2,1,0:T(8,128)(2,1)S(1)} %all-to-all-done.own_ref), channel_id=1, source_target_pairs={{0,1},{1,0},{2,3},{3,2},{4,5},{5,4},{6,7},{7,6},{8,9},{9,8},{10,11... | collective-permute-start | bytes 884744 | tf_op jit(solution)/shard_map/ppermute | solution.py:556
  54.9 2.9 %page_reads.1 = bf16[8,256,256]{2,1,0:T(8,128)(2,1)} custom-call(s32[8,5]{1,0:T(8,128)S(1)} %pad_add_fusion.table_ref, s32[1]{0:T(128)S(6)} %and.18.core_ref, bf16[8,144,128]{2,1,0:T(8,128)(2,1)S(1)} %all-to-all-done.own_ref, bf16[8,144,128]{2,1,0:T(8,128)(2,1)S(1)} %collective-permute-done.1.far_ref, bf16[4,256,128]{2,1,0:T(8,128)(2,1)S(1)} %after.1.refs_0_, ...), custom_call_target="tpu_custom_call" | custom-call | flops 700000000 | bytes 3000000 | tf_op jit(solution)/shard_map/page_reads/pallas_call | solution.py:36
  57.8 3.6 %all-to-all-start.1 = ((bf16[8,256,256]{2,1,0:T(8,128)(2,1)}), bf16[8,256,256]{2,1,0:T(8,128)(2,1)S(1)}, u32[]{:S(2)}, u32[]{:S(2)}) async-start(bf16[8,256,256]{2,1,0:T(8,128)(2,1)} %page_reads.1), calls=%async_computation.1 | async-start | bytes 2097152 | tf_op jit(solution)/shard_map/all_to_all | solution.py:588
  62.2 3.4 %scan_parts.1 = (f32[256,256]{1,0:T(8,128)S(1)}, f32[256,256]{1,0:T(8,128)S(1)}, f32[264,128]{1,0:T(8,128)S(1)}) custom-call(s32[1,16]{1,0:T(1,128)} %len_ref.7, s32[1,16]{1,0:T(1,128)} %res_ref.4, bf16[256,256]{1,0:T(8,128)(2,1)} %x_ref.3, bf16[256,256]{1,0:T(8,128)(2,1)} %z_ref.1, bf16[256,128]{1,0:T(8,128)(2,1)} %b_ref.1, bf16[256,128]{1,0:T(8,128)(2,1)} %c_ref.5, ...), custom_call_target="tpu_custom_call" | custom-call | flops 400000000 | bytes 2000000 | tf_op jit(solution)/shard_map/scan_parts/pallas_call | solution.py:36
  65.5 3.3 %collective-permute-start = (f32[264,128]{1,0:T(8,128)S(1)}, f32[264,128]{1,0:T(8,128)S(1)}, u32[]{:S(2)}, u32[]{:S(2)}) collective-permute-start(f32[264,128]{1,0:T(8,128)S(1)} %get-tuple-element.10), channel_id=1, source_target_pairs={{0,16},{16,32},{32,48},{48,64},{64,80},{80,96},{96,112},{112,128},... | collective-permute-start | bytes 405512 | tf_op jit(solution)/shard_map/ppermute | solution.py:499
  68.8 21.0 %collective-permute-done.carry_ref = f32[264,128]{1,0:T(8,128)S(1)} collective-permute-done((f32[264,128]{1,0:T(8,128)S(1)}, f32[264,128]{1,0:T(8,128)S(1)}, u32[]{:S(2)}, u32[]{:S(2)}) %collective-permute-start) | collective-permute-done | bytes 135200 | tf_op jit(solution)/shard_map/ppermute | solution.py:499
  89.8 2.8 %project.1 = (bf16[128,2176]{1,0:T(8,128)(2,1)S(1)}, bf16[128,2176]{1,0:T(8,128)(2,1)S(1)}) custom-call(s32[1,16]{1,0:T(1,128)} %len_ref.7, s32[1]{0:T(128)} %bitcast.2.group_ref, s32[1]{0:T(128)S(6)} %and.18.core_ref, bf16[256,128]{1,0:T(8,128)(2,1)} %c_ref.5, f32[264,128]{1,0:T(8,128)S(1)} %collective-permute-done.carry_ref, ...), custom_call_target="tpu_custom_call" | custom-call | flops 300000000 | bytes 3500000 | tf_op jit(solution)/shard_map/project/pallas_call | solution.py:36
  92.7 3.6 %collective-permute-start.5 = (bf16[128,2176]{1,0:T(8,128)(2,1)S(1)}, bf16[128,2176]{1,0:T(8,128)(2,1)S(1)}, u32[]{:S(2)}, u32[]{:S(2)}) collective-permute-start(bf16[128,2176]{1,0:T(8,128)(2,1)S(1)} %get-tuple-element.17), channel_id=1, source_target_pairs={{0,1},{1,0},{2,3},{3,2},{4,5},{5,4},{6,7},{7,6},{8,9},{9,8},{10,11... | collective-permute-start | bytes 1671176 | tf_op jit(solution)/shard_map/ppermute | solution.py:595
  96.3 1.6 collective-permute-done.5.b_ref
  99.0 6.9 %all-to-all-start.2 = ((bf16[8,16,2176]{2,1,0:T(8,128)(2,1)}), bf16[8,16,2176]{2,1,0:T(8,128)(2,1)S(1)}, u32[]{:S(2)}, u32[]{:S(2)}) async-start(bf16[8,16,2176]{2,1,0:T(8,128)(2,1)} %bitcast.12), calls=%async_computation.2 | async-start | bytes 1114112 | tf_op jit(solution)/shard_map/all_to_all | solution.py:596
  105.9 18.7 %all-to-all-done.2.recv_ref = bf16[8,16,2176]{2,1,0:T(8,128)(2,1)S(1)} async-done(((bf16[8,16,2176]{2,1,0:T(8,128)(2,1)}), bf16[8,16,2176]{2,1,0:T(8,128)(2,1)S(1)}, u32[]{:S(2)}, u32[]{:S(2)}) %all-to-all-start.2) | async-done | bytes 557088 | tf_op jit(solution)/shard_map/all_to_all | solution.py:596
  125.7 20.1 %all_to_all.25 = bf16[8,16,2048]{2,1,0:T(8,128)(2,1)S(1)} all-to-all(bf16[8,16,2048]{2,1,0:T(8,128)(2,1)S(1)} %norm_rows.1), channel_id=1, replica_groups={{0,2,4,6,8,10,12,14},{1,3,5,7,9,11,13,15},{16,18,20,22,24,26,28,30},{17..., dimensions={0} | all-to-all | bytes 1048576 | tf_op jit(solution)/shard_map/all_to_all | solution.py:601
  145.9 2.6 %collective-permute-start.6 = (bf16[128,2048]{1,0:T(8,128)(2,1)S(1)}, bf16[128,2048]{1,0:T(8,128)(2,1)S(1)}, u32[]{:S(2)}, u32[]{:S(2)}) collective-permute-start(bf16[128,2048]{1,0:T(8,128)(2,1)S(1)} %bitcast.18), channel_id=1, source_target_pairs={{0,1},{1,0},{2,3},{3,2},{4,5},{5,4},{6,7},{7,6},{8,9},{9,8},{10,11... | collective-permute-start | bytes 1572872 | tf_op jit(solution)/shard_map/ppermute | solution.py:605
  148.5 1.6 ref_norm.1.ref_ref
  150.2 3.2 %all-gather.2.cloned.1.call-done.head_ref = bf16[2048,3200]{1,0:T(8,128)(2,1)} async-done(((bf16[64,3200]{1,0:T(8,128)(2,1)}), bf16[2048,3200]{1,0:T(8,128)(2,1)}) %all-gather.2.cloned.1.call-update) | async-done | bytes 13107216 | tf_op jit(solution)/shard_map/all_gather | solution.py:546
  153.4 7.6 %scores.1 = f32[16,8,256]{2,1,0:T(8,128)S(1)} custom-call(s32[1]{0:T(128)} %bitcast.place_ref, s32[1]{0:T(128)S(6)} %and.18.core_ref, bf16[256,2048]{1,0:T(8,128)(2,1)S(1)} %ref_norm.1.ref_ref, bf16[128,2048]{1,0:T(8,128)(2,1)S(1)} %bitcast.19, bf16[128,2048]{1,0:T(8,128)(2,1)S(1)} %collective-permute-done.6.far_ref, ...), custom_call_target="tpu_custom_call" | custom-call | flops 3400000000 | bytes 15000000 | tf_op jit(solution)/shard_map/scores/pallas_call | solution.py:430
  161.0 16.8 %all_to_all.26.recv_ref = f32[16,8,256]{2,1,0:T(8,128)S(1)} all-to-all(f32[16,8,256]{2,1,0:T(8,128)S(1)} %scores.1), channel_id=1, replica_groups=mesh['grp'=32,'vocab'=16] {'vocab'}, dimensions={0} | all-to-all | bytes 262144 | tf_op jit(solution)/shard_map/all_to_all | solution.py:607
  (35 shorter events, 14.2 us)
Async XLA Ops:
  7.2 146.1 %copy-start = (s32[256]{0:T(256)S(1)}, s32[256]{0:T(256)}, u32[]{:S(2)}) copy-start(s32[256]{0:T(256)} %param.43) | copy-start | bytes 3076
  7.2 146.1 %all-gather.2.cloned.1.call-start = ((), (), s32[]{:S(2)}) async-start(), calls=%async_computation.5 | async-start | bytes 13516800 | tf_op jit(solution)/shard_map/all_gather | solution.py:546
  13.7 40.1 %collective-permute-start.2 = (bf16[4,256,128]{2,1,0:T(8,128)(2,1)S(1)}, bf16[4,256,128]{2,1,0:T(8,128)(2,1)S(1)}, u32[]{:S(2)}, u32[]{:S(2)}) collective-permute-start(bf16[4,256,128]{2,1,0:T(8,128)(2,1)S(1)} %after.1.refs_0_), channel_id=1, source_target_pairs={{0,128},{16,144},{32,160},{48,176},{64,192},{80,208},{96,224},{112... | collective-permute-start | bytes 786440 | tf_op jit(solution)/shard_map/ppermute | solution.py:560
  17.6 36.2 %collective-permute-start.3 = (bf16[4,256,128]{2,1,0:T(8,128)(2,1)S(1)}, bf16[4,256,128]{2,1,0:T(8,128)(2,1)S(1)}, u32[]{:S(2)}, u32[]{:S(2)}) collective-permute-start(bf16[4,256,128]{2,1,0:T(8,128)(2,1)S(1)} %after.1.refs_0_), channel_id=1, source_target_pairs={{0,256},{16,272},{32,288},{48,304},{64,320},{80,336},{96,352},{112... | collective-permute-start | bytes 786440 | tf_op jit(solution)/shard_map/ppermute | solution.py:560
  22.0 31.8 %collective-permute-start.4 = (bf16[4,256,128]{2,1,0:T(8,128)(2,1)S(1)}, bf16[4,256,128]{2,1,0:T(8,128)(2,1)S(1)}, u32[]{:S(2)}, u32[]{:S(2)}) collective-permute-start(bf16[4,256,128]{2,1,0:T(8,128)(2,1)S(1)} %after.1.refs_0_), channel_id=1, source_target_pairs={{0,384},{16,400},{32,416},{48,432},{64,448},{80,464},{96,480},{112... | collective-permute-start | bytes 786440 | tf_op jit(solution)/shard_map/ppermute | solution.py:560
  25.1 21.9 %all-to-all-start = ((bf16[8,144,128]{2,1,0:T(8,128)(2,1)}), bf16[8,144,128]{2,1,0:T(8,128)(2,1)S(1)}, u32[]{:S(2)}, u32[]{:S(2)}) async-start(bf16[8,144,128]{2,1,0:T(8,128)(2,1)} %send_rows.1._), calls=%async_computation | async-start | bytes 589824 | tf_op jit(solution)/shard_map/all_to_all | solution.py:553
  46.9 8.0 %collective-permute-start.1 = (bf16[8,144,128]{2,1,0:T(8,128)(2,1)S(1)}, bf16[8,144,128]{2,1,0:T(8,128)(2,1)S(1)}, u32[]{:S(2)}, u32[]{:S(2)}) collective-permute-start(bf16[8,144,128]{2,1,0:T(8,128)(2,1)S(1)} %all-to-all-done.own_ref), channel_id=1, source_target_pairs={{0,1},{1,0},{2,3},{3,2},{4,5},{5,4},{6,7},{7,6},{8,9},{9,8},{10,11... | collective-permute-start | bytes 884744 | tf_op jit(solution)/shard_map/ppermute | solution.py:556
  57.8 32.0 %all-to-all-start.1 = ((bf16[8,256,256]{2,1,0:T(8,128)(2,1)}), bf16[8,256,256]{2,1,0:T(8,128)(2,1)S(1)}, u32[]{:S(2)}, u32[]{:S(2)}) async-start(bf16[8,256,256]{2,1,0:T(8,128)(2,1)} %page_reads.1), calls=%async_computation.1 | async-start | bytes 2097152 | tf_op jit(solution)/shard_map/all_to_all | solution.py:588
  65.5 24.3 %collective-permute-start = (f32[264,128]{1,0:T(8,128)S(1)}, f32[264,128]{1,0:T(8,128)S(1)}, u32[]{:S(2)}, u32[]{:S(2)}) collective-permute-start(f32[264,128]{1,0:T(8,128)S(1)} %get-tuple-element.10), channel_id=1, source_target_pairs={{0,16},{16,32},{32,48},{48,64},{64,80},{80,96},{96,112},{112,128},... | collective-permute-start | bytes 405512 | tf_op jit(solution)/shard_map/ppermute | solution.py:499
  92.7 5.2 %collective-permute-start.5 = (bf16[128,2176]{1,0:T(8,128)(2,1)S(1)}, bf16[128,2176]{1,0:T(8,128)(2,1)S(1)}, u32[]{:S(2)}, u32[]{:S(2)}) collective-permute-start(bf16[128,2176]{1,0:T(8,128)(2,1)S(1)} %get-tuple-element.17), channel_id=1, source_target_pairs={{0,1},{1,0},{2,3},{3,2},{4,5},{5,4},{6,7},{7,6},{8,9},{9,8},{10,11... | collective-permute-start | bytes 1671176 | tf_op jit(solution)/shard_map/ppermute | solution.py:595
  99.0 25.6 %all-to-all-start.2 = ((bf16[8,16,2176]{2,1,0:T(8,128)(2,1)}), bf16[8,16,2176]{2,1,0:T(8,128)(2,1)S(1)}, u32[]{:S(2)}, u32[]{:S(2)}) async-start(bf16[8,16,2176]{2,1,0:T(8,128)(2,1)} %bitcast.12), calls=%async_computation.2 | async-start | bytes 1114112 | tf_op jit(solution)/shard_map/all_to_all | solution.py:596
  145.9 4.3 %collective-permute-start.6 = (bf16[128,2048]{1,0:T(8,128)(2,1)S(1)}, bf16[128,2048]{1,0:T(8,128)(2,1)S(1)}, u32[]{:S(2)}, u32[]{:S(2)}) collective-permute-start(bf16[128,2048]{1,0:T(8,128)(2,1)S(1)} %bitcast.18), channel_id=1, source_target_pairs={{0,1},{1,0},{2,3},{3,2},{4,5},{5,4},{6,7},{7,6},{8,9},{9,8},{10,11... | collective-permute-start | bytes 1572872 | tf_op jit(solution)/shard_map/ppermute | solution.py:605
Sparse Core Ops, SparseCore 0:
  11.2 142.0 all-gather.1

commit v5 on v4

--- a/solution.py
+++ b/solution.py
@@ -117,15 +117,18 @@
     )(first, pages)
 
 
-def reads_kernel(table_ref, core_ref, own_ref, far_ref, *refs):
-    *page_refs, out_ref, pages = refs
+def reads_kernel(table_ref, core_ref, side_ref, own_ref, far_ref, *refs):
+    *page_refs, keep_ref, low_ref, high_ref, pages = refs
     groups, wide, states = own_ref.shape
     half = wide - 16
     count = table_ref.shape[1]
     slots = page_refs[0].shape[0]
     for k, ref in enumerate(page_refs):
         pages[k * slots : (k + 1) * slots] = ref[...]
-    for j in range(groups):
+    split_at = low_ref.shape[2]
+    for pick in range(groups):
+        mine = pick % 2 == 0
+        j = pick // 2 * 2 + (side_ref[0] if mine else 1 - side_ref[0])
         halves, numbers = [], []
         for ref in (own_ref, far_ref):
             halves.append(ref[j, :half, :].astype(F32))
@@ -142,19 +145,40 @@
             jnp.concatenate(rhs, axis=1),
             NT,
             preferred_element_type=F32,
-        )
-        term = term.astype(BF16)
-        out_ref[j, pl.ds(pl.multiple_of(core_ref[0] * half, half), half)] = term[:half]
-        out_ref[j, pl.ds(pl.multiple_of((1 - core_ref[0]) * half, half), half)] = term[half:]
-
-
-def page_reads(table, core, own, far, pages):
+        ).astype(BF16)
+        for part, where in ((term[:half], core_ref[0]), (term[half:], 1 - core_ref[0])):
+            at = pl.ds(pl.multiple_of(where * half, half), half)
+            if mine:
+                keep_ref[pick // 2, at] = part
+            else:
+                low_ref[pick // 2, at] = part[:, :split_at]
+                high_ref[pick // 2, at] = part[:, split_at:]
+
+
+def page_reads(table, core, side, own, far, pages):
     groups = own.shape[0]
     tokens = 2 * (own.shape[1] - 16)
     slots, channels, states = pages[0].shape
-    return call(
-        reads_kernel, "page_reads", jax.ShapeDtypeStruct((groups, tokens, channels), BF16),
-        [table, core], [own, far, *pages], cost(700_000_000, 3_000_000), [pltpu.VMEM((len(pages) * slots, channels, states), BF16)],
+    kept = jax.ShapeDtypeStruct((groups // 2, tokens, channels), BF16)
+    sent = jax.ShapeDtypeStruct((groups // 2, tokens, channels // 2), BF16)
+    return call(
+        reads_kernel, "page_reads", (kept, sent, sent),
+        [table, core, side], [own, far, *pages], cost(700_000_000, 3_000_000),
+        [pltpu.VMEM((len(pages) * slots, channels, states), BF16)],
+    )
+
+
+def join_kernel(keep_ref, low_ref, high_ref, out_ref):
+    at = low_ref.shape[2]
+    keep = keep_ref[...].astype(F32)
+    out_ref[:, :, :at] = (keep[:, :, :at] + low_ref[...].astype(F32)).astype(BF16)
+    out_ref[:, :, at:] = (keep[:, :, at:] + high_ref[...].astype(F32)).astype(BF16)
+
+
+def join(keep, low, high):
+    return call(
+        join_kernel, "join", jax.ShapeDtypeStruct(keep.shape, BF16),
+        [], [keep, low, high], cost(300_000, 1_600_000),
     )
 
 
@@ -584,9 +608,17 @@
     ref_normed = ref_norm(ref_hidden, ref_gain)
     target = jnp.broadcast_to(targets[:, None], (tokens, 128))
 
-    reads = page_reads(table, core, asking, far_asking, pages)
+    keep, low, high = page_reads(table, core, my_z[None] & 1, asking, far_asking, pages)
+    beside = [(x * ring + z, x * ring + (z ^ 1)) for x in range(span) for z in range(ring)]
+    beyond = [
+        (x * ring + z, x * ring + (z + (1 if z % 2 else ring - 1)) % ring)
+        for x in range(span)
+        for z in range(ring)
+    ]
+    reads = join(keep, lax.ppermute(low, "grp", beside), lax.ppermute(high, "grp", beyond))
+    sides = [[x * ring + k for k in range(p, ring, 2)] for x in range(span) for p in range(2)]
     reads = lax.all_to_all(
-        reads, "grp", split_axis=0, concat_axis=0, tiled=True, axis_index_groups=lines
+        reads, "grp", split_axis=0, concat_axis=0, tiled=True, axis_index_groups=sides
     )
     rails = [[k * 2 + c for k in range(parts // 2)] for c in range(2)]
     theirs, ours = project(

time: 187 us -> 188 us (level)
  starting transfers between devices: 48.2 us -> 61.1 us
  waiting for transfers between devices: 50.7 us -> 42 us
  blocking collectives: 36.9 us -> 34.2 us
    ppermute x1, waiting for transfers between devices: 21 us -> 7.03 us  [from_behind(): return lax.ppermute(x, axis, pairs)]
    ppermute x0 -> x2, starting transfers between devices: none -> 8.91 us  [the longest x1 4.76 us: body(): lax.ppermute(low, 'grp', beside)]
    ppermute x1, starting transfers between devices: 3.64 us -> 11.4 us  [body(): summed = pair_sum(ours, lax.ppermute(theirs, 'vocab', other))]
    ppermute x0 -> x2, waiting for transfers between devices: none -> 7.36 us  [the longest x1 5.98 us: body(): lax.ppermute(low, 'grp', beside)]
    ppermute x3, waiting for transfers between devices: 0.01 us -> 6.01 us  [body(): pages.append(lax.ppermute(saved_pages, 'grp', pairs))]
    all_to_all x1, waiting for transfers between devices: 5.21 us -> 0.01 us  [body(): lax.all_to_all(asking, 'grp', split_axis=0, concat_axis=0, tiled=True, ax...]
    all_gather x1, waiting for transfers between devices: 3.15 us -> 0.02 us  [body(): lax.all_gather(jnp.concatenate([ref_head, policy_head, spare], axis=1), '...]
    ppermute x1, starting transfers between devices: 6.78 us -> 3.7 us  [body(): far_asking = lax.ppermute(asking, 'vocab', other)]
  transfers between devices with their start and end apart: 11 -> 13, of which waited for: 6 -> 7; matrix products, arithmetic and copies ran while one was open for 4% -> 4% of each run, Pallas kernels for 9% -> 9%
where the time goes in v5:
time: 188 us; the launch traced here: 187 us
  starting transfers between devices  61.1 us (32%)
  waiting for transfers between devices  42 us (22%)
  blocking collectives  34.2 us (18%)
  Pallas kernels  25.6 us (14%)
  between operations  14.2 us (8%)
  local copies, waits for them, and re-layouts  7.98 us (4%)
  other arithmetic  2.26 us (1%)
    all_to_all x1, blocking collectives, body(): lax.all_to_all(mine, 'vocab', split_axis=0, concat_axis=0, tiled=True, ax...  20.1 us
    all_to_all x1, waiting for transfers between devices, body(): lax.all_to_all(summed.reshape(parts // 2, tokens // parts, -1), 'vocab',...  18.7 us
    pallas_call x8, Pallas kernels, call(): pl.pallas_call(kernel, out_shape=outs, grid_spec=pltpu.PrefetchScalarGrid...  16 us
    all_to_all x1, blocking collectives, body(): lax.all_to_all(stats, 'vocab', split_axis=0, concat_axis=0, tiled=True)  14 us
    ppermute x1, starting transfers between devices, body(): summed = pair_sum(ours, lax.ppermute(theirs, 'vocab', other))  11.4 us
    all_to_all x1, starting transfers between devices, body(): lax.all_to_all(asking, 'grp', split_axis=0, concat_axis=0, tiled=True, ax...  10.9 us
    ppermute x3, starting transfers between devices, body(): pages.append(lax.ppermute(saved_pages, 'grp', pairs))  9.33 us
    pallas_call x1, Pallas kernels, scores(): pl.pallas_call(functools.partial(score_kernel, columns, block), out_shape...  7.58 us
  transfers between devices with their start and end apart: 13, of which 7 were waited for; matrix products, arithmetic and copies ran while one was open for 4% of the time, Pallas kernels for 9%

profile of v5, /device:TPU:1, one launch (start us, length us, event | category | flops | bytes accessed | tf_op | source)
XLA Modules:
  0.0 187.3 jit_solution(9910159132049187262)
XLA Ops:
  7.2 2.0 %concatenate.15 = bf16[64,3200]{1,0:T(8,128)(2,1)} concatenate(bf16[64,1576]{1,0:T(8,128)(2,1)} %param.37, bf16[64,1576]{1,0:T(8,128)(2,1)} %param.36, bf16[64,48]{1,0:T(8,128)(2,1)S(1)} %broadcast_in_dim.60), dimensions={1} | concatenate | bytes 819200 | tf_op jit(solution)/shard_map/concatenate | solution.py:571
  10.0 2.7 %send_rows.1._ = bf16[8,144,128]{2,1,0:T(8,128)(2,1)} custom-call(s32[32,16]{1,0:T(8,128)S(1)} %copy.28.own_ref, s32[1,16]{1,0:T(1,128)} %len_ref.7, s32[1,16]{1,0:T(1,128)} %res_ref.4, s32[1]{0:T(128)} %bitcast.2.group_ref, s32[1]{0:T(128)S(6)} %and.23.core_ref, bf16[256,128]{1,0:T(8,128)(2,1)} %c_ref.5), custom_call_target="tpu_custom_call" | custom-call | flops 100000 | bytes 700000 | tf_op jit(solution)/shard_map/send_rows/pallas_call | solution.py:36
  12.7 10.9 %all-to-all-start = ((bf16[8,144,128]{2,1,0:T(8,128)(2,1)}), bf16[8,144,128]{2,1,0:T(8,128)(2,1)S(1)}, u32[]{:S(2)}, u32[]{:S(2)}) async-start(bf16[8,144,128]{2,1,0:T(8,128)(2,1)} %send_rows.1._), calls=%async_computation | async-start | bytes 589824 | tf_op jit(solution)/shard_map/all_to_all | solution.py:577
  24.6 4.4 %collective-permute-start.4 = (bf16[4,256,128]{2,1,0:T(8,128)(2,1)S(1)}, bf16[4,256,128]{2,1,0:T(8,128)(2,1)S(1)}, u32[]{:S(2)}, u32[]{:S(2)}) collective-permute-start(bf16[4,256,128]{2,1,0:T(8,128)(2,1)S(1)} %after.1.refs_0_), channel_id=1, source_target_pairs={{0,384},{16,400},{32,416},{48,432},{64,448},{80,464},{96,480},{112... | collective-permute-start | bytes 786440 | tf_op jit(solution)/shard_map/ppermute | solution.py:584
  29.0 2.4 %collective-permute-start.3 = (bf16[4,256,128]{2,1,0:T(8,128)(2,1)S(1)}, bf16[4,256,128]{2,1,0:T(8,128)(2,1)S(1)}, u32[]{:S(2)}, u32[]{:S(2)}) collective-permute-start(bf16[4,256,128]{2,1,0:T(8,128)(2,1)S(1)} %after.1.refs_0_), channel_id=1, source_target_pairs={{0,256},{16,272},{32,288},{48,304},{64,320},{80,336},{96,352},{112... | collective-permute-start | bytes 786440 | tf_op jit(solution)/shard_map/ppermute | solution.py:584
  31.4 2.5 %collective-permute-start.2 = (bf16[4,256,128]{2,1,0:T(8,128)(2,1)S(1)}, bf16[4,256,128]{2,1,0:T(8,128)(2,1)S(1)}, u32[]{:S(2)}, u32[]{:S(2)}) collective-permute-start(bf16[4,256,128]{2,1,0:T(8,128)(2,1)S(1)} %after.1.refs_0_), channel_id=1, source_target_pairs={{0,128},{16,144},{32,160},{48,176},{64,192},{80,208},{96,224},{112... | collective-permute-start | bytes 786440 | tf_op jit(solution)/shard_map/ppermute | solution.py:584
  40.5 3.7 %collective-permute-start.1 = (bf16[8,144,128]{2,1,0:T(8,128)(2,1)S(1)}, bf16[8,144,128]{2,1,0:T(8,128)(2,1)S(1)}, u32[]{:S(2)}, u32[]{:S(2)}) collective-permute-start(bf16[8,144,128]{2,1,0:T(8,128)(2,1)S(1)} %all-to-all-done.own_ref), channel_id=1, source_target_pairs={{0,1},{1,0},{2,3},{3,2},{4,5},{5,4},{6,7},{7,6},{8,9},{9,8},{10,11... | collective-permute-start | bytes 884744 | tf_op jit(solution)/shard_map/ppermute | solution.py:580
  44.3 6.0 %collective-permute-done.2.refs_1_ = bf16[4,256,128]{2,1,0:T(8,128)(2,1)S(1)} collective-permute-done((bf16[4,256,128]{2,1,0:T(8,128)(2,1)S(1)}, bf16[4,256,128]{2,1,0:T(8,128)(2,1)S(1)}, u32[]{:S(2)}, u32[]{:S(2)}) %collective-permute-start.2) | collective-permute-done | bytes 262176 | tf_op jit(solution)/shard_map/ppermute | solution.py:584
  50.3 1.9 %page_reads.1 = (bf16[4,256,256]{2,1,0:T(8,128)(2,1)S(1)}, bf16[4,256,128]{2,1,0:T(8,128)(2,1)S(1)}, bf16[4,256,128]{2,1,0:T(8,128)(2,1)S(1)}) custom-call(s32[8,5]{1,0:T(8,128)S(1)} %pad_add_fusion.table_ref, s32[1]{0:T(128)S(6)} %and.23.core_ref, s32[1]{0:T(128)} %bitcast.11.side_ref, bf16[8,144,128]{2,1,0:T(8,128)(2,1)S(1)} %all-to-all-done.own_ref, ...), custom_call_target="tpu_custom_call" | custom-call | flops 700000000 | bytes 3000000 | tf_op jit(solution)/shard_map/page_reads/pallas_call | solution.py:36
  52.2 4.8 %collective-permute-start.5 = (bf16[4,256,128]{2,1,0:T(8,128)(2,1)S(1)}, bf16[4,256,128]{2,1,0:T(8,128)(2,1)S(1)}, u32[]{:S(2)}, u32[]{:S(2)}) collective-permute-start(bf16[4,256,128]{2,1,0:T(8,128)(2,1)S(1)} %get-tuple-element.18), channel_id=1, source_target_pairs={{0,16},{16,0},{32,48},{48,32},{64,80},{80,64},{96,112},{112,96},{1... | collective-permute-start | bytes 786440 | tf_op jit(solution)/shard_map/ppermute | solution.py:618
  56.9 4.2 %collective-permute-start.6 = (bf16[4,256,128]{2,1,0:T(8,128)(2,1)S(1)}, bf16[4,256,128]{2,1,0:T(8,128)(2,1)S(1)}, u32[]{:S(2)}, u32[]{:S(2)}) collective-permute-start(bf16[4,256,128]{2,1,0:T(8,128)(2,1)S(1)} %get-tuple-element.19), channel_id=1, source_target_pairs={{0,112},{16,32},{32,16},{48,64},{64,48},{80,96},{96,80},{112,0},{1... | collective-permute-start | bytes 786440 | tf_op jit(solution)/shard_map/ppermute | solution.py:618
  61.1 6.0 %collective-permute-done.5.low_ref = bf16[4,256,128]{2,1,0:T(8,128)(2,1)S(1)} collective-permute-done((bf16[4,256,128]{2,1,0:T(8,128)(2,1)S(1)}, bf16[4,256,128]{2,1,0:T(8,128)(2,1)S(1)}, u32[]{:S(2)}, u32[]{:S(2)}) %collective-permute-start.5) | collective-permute-done | bytes 262176 | tf_op jit(solution)/shard_map/ppermute | solution.py:618
  69.4 4.4 %all-to-all-start.1 = ((bf16[4,256,256]{2,1,0:T(8,128)(2,1)}), bf16[4,256,256]{2,1,0:T(8,128)(2,1)S(1)}, u32[]{:S(2)}, u32[]{:S(2)}) async-start(bf16[4,256,256]{2,1,0:T(8,128)(2,1)} %join.1), calls=%async_computation.1 | async-start | bytes 1048576 | tf_op jit(solution)/shard_map/all_to_all | solution.py:620
  74.7 3.4 %scan_parts.1 = (f32[256,256]{1,0:T(8,128)S(1)}, f32[256,256]{1,0:T(8,128)S(1)}, f32[264,128]{1,0:T(8,128)S(1)}) custom-call(s32[1,16]{1,0:T(1,128)} %len_ref.7, s32[1,16]{1,0:T(1,128)} %res_ref.4, bf16[256,256]{1,0:T(8,128)(2,1)} %x_ref.3, bf16[256,256]{1,0:T(8,128)(2,1)} %z_ref.1, bf16[256,128]{1,0:T(8,128)(2,1)} %b_ref.1, bf16[256,128]{1,0:T(8,128)(2,1)} %c_ref.5, ...), custom_call_target="tpu_custom_call" | custom-call | flops 400000000 | bytes 2000000 | tf_op jit(solution)/shard_map/scan_parts/pallas_call | solution.py:36
  78.0 2.4 %collective-permute-start = (f32[264,128]{1,0:T(8,128)S(1)}, f32[264,128]{1,0:T(8,128)S(1)}, u32[]{:S(2)}, u32[]{:S(2)}) collective-permute-start(f32[264,128]{1,0:T(8,128)S(1)} %get-tuple-element.13), channel_id=1, source_target_pairs={{0,16},{16,32},{32,48},{48,64},{64,80},{80,96},{96,112},{112,128},... | collective-permute-start | bytes 405512 | tf_op jit(solution)/shard_map/ppermute | solution.py:523
  80.5 7.0 %collective-permute-done.carry_ref = f32[264,128]{1,0:T(8,128)S(1)} collective-permute-done((f32[264,128]{1,0:T(8,128)S(1)}, f32[264,128]{1,0:T(8,128)S(1)}, u32[]{:S(2)}, u32[]{:S(2)}) %collective-permute-start) | collective-permute-done | bytes 135200 | tf_op jit(solution)/shard_map/ppermute | solution.py:523
  88.8 2.7 %project.1 = (bf16[128,2176]{1,0:T(8,128)(2,1)S(1)}, bf16[128,2176]{1,0:T(8,128)(2,1)S(1)}) custom-call(s32[1,16]{1,0:T(1,128)} %len_ref.7, s32[1]{0:T(128)} %bitcast.2.group_ref, s32[1]{0:T(128)S(6)} %and.23.core_ref, bf16[256,128]{1,0:T(8,128)(2,1)} %c_ref.5, f32[264,128]{1,0:T(8,128)S(1)} %collective-permute-done.carry_ref, ...), custom_call_target="tpu_custom_call" | custom-call | flops 300000000 | bytes 3500000 | tf_op jit(solution)/shard_map/project/pallas_call | solution.py:36
  91.6 11.4 %collective-permute-start.7 = (bf16[128,2176]{1,0:T(8,128)(2,1)S(1)}, bf16[128,2176]{1,0:T(8,128)(2,1)S(1)}, u32[]{:S(2)}, u32[]{:S(2)}) collective-permute-start(bf16[128,2176]{1,0:T(8,128)(2,1)S(1)} %get-tuple-element.23), channel_id=1, source_target_pairs={{0,1},{1,0},{2,3},{3,2},{4,5},{5,4},{6,7},{7,6},{8,9},{9,8},{10,11... | collective-permute-start | bytes 1671176 | tf_op jit(solution)/shard_map/ppermute | solution.py:627
  105.7 7.3 %all-to-all-start.2 = ((bf16[8,16,2176]{2,1,0:T(8,128)(2,1)}), bf16[8,16,2176]{2,1,0:T(8,128)(2,1)S(1)}, u32[]{:S(2)}, u32[]{:S(2)}) async-start(bf16[8,16,2176]{2,1,0:T(8,128)(2,1)} %bitcast.13), calls=%async_computation.2 | async-start | bytes 1114112 | tf_op jit(solution)/shard_map/all_to_all | solution.py:628
  113.0 18.7 %all-to-all-done.2.recv_ref = bf16[8,16,2176]{2,1,0:T(8,128)(2,1)S(1)} async-done(((bf16[8,16,2176]{2,1,0:T(8,128)(2,1)}), bf16[8,16,2176]{2,1,0:T(8,128)(2,1)S(1)}, u32[]{:S(2)}, u32[]{:S(2)}) %all-to-all-start.2) | async-done | bytes 557088 | tf_op jit(solution)/shard_map/all_to_all | solution.py:628
  132.8 20.1 %all_to_all.25 = bf16[8,16,2048]{2,1,0:T(8,128)(2,1)S(1)} all-to-all(bf16[8,16,2048]{2,1,0:T(8,128)(2,1)S(1)} %norm_rows.1), channel_id=1, replica_groups={{0,2,4,6,8,10,12,14},{1,3,5,7,9,11,13,15},{16,18,20,22,24,26,28,30},{17..., dimensions={0} | all-to-all | bytes 1048576 | tf_op jit(solution)/shard_map/all_to_all | solution.py:633
  153.0 2.6 %collective-permute-start.8 = (bf16[128,2048]{1,0:T(8,128)(2,1)S(1)}, bf16[128,2048]{1,0:T(8,128)(2,1)S(1)}, u32[]{:S(2)}, u32[]{:S(2)}) collective-permute-start(bf16[128,2048]{1,0:T(8,128)(2,1)S(1)} %bitcast.19), channel_id=1, source_target_pairs={{0,1},{1,0},{2,3},{3,2},{4,5},{5,4},{6,7},{7,6},{8,9},{9,8},{10,11... | collective-permute-start | bytes 1572872 | tf_op jit(solution)/shard_map/ppermute | solution.py:637
  157.4 7.6 %scores.1 = f32[16,8,256]{2,1,0:T(8,128)S(1)} custom-call(s32[1]{0:T(128)} %bitcast.place_ref, s32[1]{0:T(128)S(6)} %and.23.core_ref, bf16[256,2048]{1,0:T(8,128)(2,1)S(1)} %ref_norm.1.ref_ref, bf16[128,2048]{1,0:T(8,128)(2,1)S(1)} %bitcast.20, bf16[128,2048]{1,0:T(8,128)(2,1)S(1)} %collective-permute-done.8.far_ref, ...), custom_call_target="tpu_custom_call" | custom-call | flops 3400000000 | bytes 15000000 | tf_op jit(solution)/shard_map/scores/pallas_call | solution.py:454
  165.0 14.0 %all_to_all.26.recv_ref = f32[16,8,256]{2,1,0:T(8,128)S(1)} all-to-all(f32[16,8,256]{2,1,0:T(8,128)S(1)} %scores.1), channel_id=1, replica_groups=mesh['grp'=32,'vocab'=16] {'vocab'}, dimensions={0} | all-to-all | bytes 262144 | tf_op jit(solution)/shard_map/all_to_all | solution.py:639
  (40 shorter events, 19.9 us)
Async XLA Ops:
  7.2 150.1 %copy-start = (s32[256]{0:T(256)S(1)}, s32[256]{0:T(256)}, u32[]{:S(2)}) copy-start(s32[256]{0:T(256)} %param.43) | copy-start | bytes 3076
  7.2 150.1 %all-gather.2.cloned.1.call-start = ((), (), s32[]{:S(2)}) async-start(), calls=%async_computation.5 | async-start | bytes 13516800 | tf_op jit(solution)/shard_map/all_gather | solution.py:570
  12.7 27.7 %all-to-all-start = ((bf16[8,144,128]{2,1,0:T(8,128)(2,1)}), bf16[8,144,128]{2,1,0:T(8,128)(2,1)S(1)}, u32[]{:S(2)}, u32[]{:S(2)}) async-start(bf16[8,144,128]{2,1,0:T(8,128)(2,1)} %send_rows.1._), calls=%async_computation | async-start | bytes 589824 | tf_op jit(solution)/shard_map/all_to_all | solution.py:577
  24.6 19.7 %collective-permute-start.4 = (bf16[4,256,128]{2,1,0:T(8,128)(2,1)S(1)}, bf16[4,256,128]{2,1,0:T(8,128)(2,1)S(1)}, u32[]{:S(2)}, u32[]{:S(2)}) collective-permute-start(bf16[4,256,128]{2,1,0:T(8,128)(2,1)S(1)} %after.1.refs_0_), channel_id=1, source_target_pairs={{0,384},{16,400},{32,416},{48,432},{64,448},{80,464},{96,480},{112... | collective-permute-start | bytes 786440 | tf_op jit(solution)/shard_map/ppermute | solution.py:584
  29.0 15.3 %collective-permute-start.3 = (bf16[4,256,128]{2,1,0:T(8,128)(2,1)S(1)}, bf16[4,256,128]{2,1,0:T(8,128)(2,1)S(1)}, u32[]{:S(2)}, u32[]{:S(2)}) collective-permute-start(bf16[4,256,128]{2,1,0:T(8,128)(2,1)S(1)} %after.1.refs_0_), channel_id=1, source_target_pairs={{0,256},{16,272},{32,288},{48,304},{64,320},{80,336},{96,352},{112... | collective-permute-start | bytes 786440 | tf_op jit(solution)/shard_map/ppermute | solution.py:584
  31.4 18.9 %collective-permute-start.2 = (bf16[4,256,128]{2,1,0:T(8,128)(2,1)S(1)}, bf16[4,256,128]{2,1,0:T(8,128)(2,1)S(1)}, u32[]{:S(2)}, u32[]{:S(2)}) collective-permute-start(bf16[4,256,128]{2,1,0:T(8,128)(2,1)S(1)} %after.1.refs_0_), channel_id=1, source_target_pairs={{0,128},{16,144},{32,160},{48,176},{64,192},{80,208},{96,224},{112... | collective-permute-start | bytes 786440 | tf_op jit(solution)/shard_map/ppermute | solution.py:584
  40.5 9.8 %collective-permute-start.1 = (bf16[8,144,128]{2,1,0:T(8,128)(2,1)S(1)}, bf16[8,144,128]{2,1,0:T(8,128)(2,1)S(1)}, u32[]{:S(2)}, u32[]{:S(2)}) collective-permute-start(bf16[8,144,128]{2,1,0:T(8,128)(2,1)S(1)} %all-to-all-done.own_ref), channel_id=1, source_target_pairs={{0,1},{1,0},{2,3},{3,2},{4,5},{5,4},{6,7},{7,6},{8,9},{9,8},{10,11... | collective-permute-start | bytes 884744 | tf_op jit(solution)/shard_map/ppermute | solution.py:580
  52.2 14.9 %collective-permute-start.5 = (bf16[4,256,128]{2,1,0:T(8,128)(2,1)S(1)}, bf16[4,256,128]{2,1,0:T(8,128)(2,1)S(1)}, u32[]{:S(2)}, u32[]{:S(2)}) collective-permute-start(bf16[4,256,128]{2,1,0:T(8,128)(2,1)S(1)} %get-tuple-element.18), channel_id=1, source_target_pairs={{0,16},{16,0},{32,48},{48,32},{64,80},{80,64},{96,112},{112,96},{1... | collective-permute-start | bytes 786440 | tf_op jit(solution)/shard_map/ppermute | solution.py:618
  56.9 11.5 %collective-permute-start.6 = (bf16[4,256,128]{2,1,0:T(8,128)(2,1)S(1)}, bf16[4,256,128]{2,1,0:T(8,128)(2,1)S(1)}, u32[]{:S(2)}, u32[]{:S(2)}) collective-permute-start(bf16[4,256,128]{2,1,0:T(8,128)(2,1)S(1)} %get-tuple-element.19), channel_id=1, source_target_pairs={{0,112},{16,32},{32,16},{48,64},{64,48},{80,96},{96,80},{112,0},{1... | collective-permute-start | bytes 786440 | tf_op jit(solution)/shard_map/ppermute | solution.py:618
  69.4 19.4 %all-to-all-start.1 = ((bf16[4,256,256]{2,1,0:T(8,128)(2,1)}), bf16[4,256,256]{2,1,0:T(8,128)(2,1)S(1)}, u32[]{:S(2)}, u32[]{:S(2)}) async-start(bf16[4,256,256]{2,1,0:T(8,128)(2,1)} %join.1), calls=%async_computation.1 | async-start | bytes 1048576 | tf_op jit(solution)/shard_map/all_to_all | solution.py:620
  78.0 9.5 %collective-permute-start = (f32[264,128]{1,0:T(8,128)S(1)}, f32[264,128]{1,0:T(8,128)S(1)}, u32[]{:S(2)}, u32[]{:S(2)}) collective-permute-start(f32[264,128]{1,0:T(8,128)S(1)} %get-tuple-element.13), channel_id=1, source_target_pairs={{0,16},{16,32},{32,48},{48,64},{64,80},{80,96},{96,112},{112,128},... | collective-permute-start | bytes 405512 | tf_op jit(solution)/shard_map/ppermute | solution.py:523
  91.6 13.0 %collective-permute-start.7 = (bf16[128,2176]{1,0:T(8,128)(2,1)S(1)}, bf16[128,2176]{1,0:T(8,128)(2,1)S(1)}, u32[]{:S(2)}, u32[]{:S(2)}) collective-permute-start(bf16[128,2176]{1,0:T(8,128)(2,1)S(1)} %get-tuple-element.23), channel_id=1, source_target_pairs={{0,1},{1,0},{2,3},{3,2},{4,5},{5,4},{6,7},{7,6},{8,9},{9,8},{10,11... | collective-permute-start | bytes 1671176 | tf_op jit(solution)/shard_map/ppermute | solution.py:627
  105.7 26.0 %all-to-all-start.2 = ((bf16[8,16,2176]{2,1,0:T(8,128)(2,1)}), bf16[8,16,2176]{2,1,0:T(8,128)(2,1)S(1)}, u32[]{:S(2)}, u32[]{:S(2)}) async-start(bf16[8,16,2176]{2,1,0:T(8,128)(2,1)} %bitcast.13), calls=%async_computation.2 | async-start | bytes 1114112 | tf_op jit(solution)/shard_map/all_to_all | solution.py:628
  153.0 4.3 %collective-permute-start.8 = (bf16[128,2048]{1,0:T(8,128)(2,1)S(1)}, bf16[128,2048]{1,0:T(8,128)(2,1)S(1)}, u32[]{:S(2)}, u32[]{:S(2)}) collective-permute-start(bf16[128,2048]{1,0:T(8,128)(2,1)S(1)} %bitcast.19), channel_id=1, source_target_pairs={{0,1},{1,0},{2,3},{3,2},{4,5},{5,4},{6,7},{7,6},{8,9},{9,8},{10,11... | collective-permute-start | bytes 1572872 | tf_op jit(solution)/shard_map/ppermute | solution.py:637
Sparse Core Ops, SparseCore 0:
  11.2 143.3 all-gather.1

commit v6 on v4

--- a/solution.py
+++ b/solution.py
@@ -354,7 +354,8 @@
 ):
     wide = head.shape[1]
     low = float(jnp.finfo(F32).min)
-    cuts = [(c, min(c + block, wide)) for c in range(0, wide, block)]
+    ends = [0, *range(block // 2, wide, block), wide]
+    cuts = list(zip(ends[:-1], ends[1:]))
     copies = []
     for k, (c, d) in enumerate(cuts):
         copies.append(pltpu.make_async_copy(head_ref.at[:, c:d], head.at[:, c:d], sems.at[k]))
@@ -368,9 +369,11 @@
     jobs = []
     for model in range(2):
         first, stop = model * columns, (model + 1) * columns
+        found = []
         for k, (c, d) in enumerate(cuts):
             if c < stop and d > first:
-                jobs.append((model, k, c, min(d, (stop + 127) // 128 * 128)))
+                found.append((model, k, max(c, first // 128 * 128), min(d, (stop + 127) // 128 * 128)))
+        jobs += found if model == 0 else found[1:] + found[:1]
     lane = lax.broadcasted_iota(jnp.int32, target_ref.shape, 1)
     local = target_ref[...] - place_ref[0] * columns
     local = jnp.where(jnp.logical_and(local >= 0, local < columns), local, -2 * wide)
@@ -444,7 +447,7 @@
                 state,
                 state,
                 state,
-                pltpu.SemaphoreType.DMA((pl.cdiv(wide, block),)),
+                pltpu.SemaphoreType.DMA((pl.cdiv(wide, block) + 1,)),
             ],
         ),
         compiler_params=params(),

time: 187 us -> 188 us (level)
  no operation moved by 1% of the time
where the time goes in v6:
time: 188 us; the launch traced here: 186 us
  waiting for transfers between devices  50.7 us (27%)
  starting transfers between devices  48.2 us (26%)
  blocking collectives  36.9 us (20%)
  Pallas kernels  26.1 us (14%)
  between operations  14.2 us (8%)
  local copies, waits for them, and re-layouts  8 us (4%)
  other arithmetic  2.3 us (1%)
    ppermute x1, waiting for transfers between devices, from_behind(): return lax.ppermute(x, axis, pairs)  21 us
    all_to_all x1, blocking collectives, body(): lax.all_to_all(mine, 'vocab', split_axis=0, concat_axis=0, tiled=True, ax...  20.1 us
    all_to_all x1, waiting for transfers between devices, body(): lax.all_to_all(summed.reshape(parts // 2, tokens // parts, -1), 'vocab',...  18.7 us
    all_to_all x1, blocking collectives, body(): lax.all_to_all(stats, 'vocab', split_axis=0, concat_axis=0, tiled=True)  16.8 us
    pallas_call x7, Pallas kernels, call(): pl.pallas_call(kernel, out_shape=outs, grid_spec=pltpu.PrefetchScalarGrid...  16 us
    ppermute x3, starting transfers between devices, body(): pages.append(lax.ppermute(saved_pages, 'grp', pairs))  11.4 us
    all_to_all x1, starting transfers between devices, body(): lax.all_to_all(asking, 'grp', split_axis=0, concat_axis=0, tiled=True, ax...  10 us
    pallas_call x1, Pallas kernels, scores(): pl.pallas_call(functools.partial(score_kernel, columns, block), out_shape...  7.95 us
  transfers between devices with their start and end apart: 11, of which 6 were waited for; matrix products, arithmetic and copies ran while one was open for 4% of the time, Pallas kernels for 9%

profile of v6, /device:TPU:1, one launch (start us, length us, event | category | flops | bytes accessed | tf_op | source)
XLA Modules:
  0.0 186.4 jit_solution(7446014822819055017)
XLA Ops:
  7.2 2.0 %concatenate.15 = bf16[64,3200]{1,0:T(8,128)(2,1)} concatenate(bf16[64,1576]{1,0:T(8,128)(2,1)} %param.37, bf16[64,1576]{1,0:T(8,128)(2,1)} %param.36, bf16[64,48]{1,0:T(8,128)(2,1)S(1)} %broadcast_in_dim.59), dimensions={1} | concatenate | bytes 819200 | tf_op jit(solution)/shard_map/concatenate | solution.py:550
  10.0 2.7 %send_rows.1._ = bf16[8,144,128]{2,1,0:T(8,128)(2,1)} custom-call(s32[32,16]{1,0:T(8,128)S(1)} %copy.28.own_ref, s32[1,16]{1,0:T(1,128)} %len_ref.7, s32[1,16]{1,0:T(1,128)} %res_ref.4, s32[1]{0:T(128)} %bitcast.2.group_ref, s32[1]{0:T(128)S(6)} %and.18.core_ref, bf16[256,128]{1,0:T(8,128)(2,1)} %c_ref.5), custom_call_target="tpu_custom_call" | custom-call | flops 100000 | bytes 700000 | tf_op jit(solution)/shard_map/send_rows/pallas_call | solution.py:36
  13.7 3.9 %collective-permute-start.2 = (bf16[4,256,128]{2,1,0:T(8,128)(2,1)S(1)}, bf16[4,256,128]{2,1,0:T(8,128)(2,1)S(1)}, u32[]{:S(2)}, u32[]{:S(2)}) collective-permute-start(bf16[4,256,128]{2,1,0:T(8,128)(2,1)S(1)} %after.1.refs_0_), channel_id=1, source_target_pairs={{0,128},{16,144},{32,160},{48,176},{64,192},{80,208},{96,224},{112... | collective-permute-start | bytes 786440 | tf_op jit(solution)/shard_map/ppermute | solution.py:563
  17.6 4.4 %collective-permute-start.3 = (bf16[4,256,128]{2,1,0:T(8,128)(2,1)S(1)}, bf16[4,256,128]{2,1,0:T(8,128)(2,1)S(1)}, u32[]{:S(2)}, u32[]{:S(2)}) collective-permute-start(bf16[4,256,128]{2,1,0:T(8,128)(2,1)S(1)} %after.1.refs_0_), channel_id=1, source_target_pairs={{0,256},{16,272},{32,288},{48,304},{64,320},{80,336},{96,352},{112... | collective-permute-start | bytes 786440 | tf_op jit(solution)/shard_map/ppermute | solution.py:563
  22.0 3.1 %collective-permute-start.4 = (bf16[4,256,128]{2,1,0:T(8,128)(2,1)S(1)}, bf16[4,256,128]{2,1,0:T(8,128)(2,1)S(1)}, u32[]{:S(2)}, u32[]{:S(2)}) collective-permute-start(bf16[4,256,128]{2,1,0:T(8,128)(2,1)S(1)} %after.1.refs_0_), channel_id=1, source_target_pairs={{0,384},{16,400},{32,416},{48,432},{64,448},{80,464},{96,480},{112... | collective-permute-start | bytes 786440 | tf_op jit(solution)/shard_map/ppermute | solution.py:563
  25.1 10.0 %all-to-all-start = ((bf16[8,144,128]{2,1,0:T(8,128)(2,1)}), bf16[8,144,128]{2,1,0:T(8,128)(2,1)S(1)}, u32[]{:S(2)}, u32[]{:S(2)}) async-start(bf16[8,144,128]{2,1,0:T(8,128)(2,1)} %send_rows.1._), calls=%async_computation | async-start | bytes 589824 | tf_op jit(solution)/shard_map/all_to_all | solution.py:556
  41.7 5.2 %all-to-all-done.own_ref = bf16[8,144,128]{2,1,0:T(8,128)(2,1)S(1)} async-done(((bf16[8,144,128]{2,1,0:T(8,128)(2,1)}), bf16[8,144,128]{2,1,0:T(8,128)(2,1)S(1)}, u32[]{:S(2)}, u32[]{:S(2)}) %all-to-all-start) | async-done | bytes 294944 | tf_op jit(solution)/shard_map/all_to_all | solution.py:556
  46.9 6.8 %collective-permute-start.1 = (bf16[8,144,128]{2,1,0:T(8,128)(2,1)S(1)}, bf16[8,144,128]{2,1,0:T(8,128)(2,1)S(1)}, u32[]{:S(2)}, u32[]{:S(2)}) collective-permute-start(bf16[8,144,128]{2,1,0:T(8,128)(2,1)S(1)} %all-to-all-done.own_ref), channel_id=1, source_target_pairs={{0,1},{1,0},{2,3},{3,2},{4,5},{5,4},{6,7},{7,6},{8,9},{9,8},{10,11... | collective-permute-start | bytes 884744 | tf_op jit(solution)/shard_map/ppermute | solution.py:559
  54.9 2.9 %page_reads.1 = bf16[8,256,256]{2,1,0:T(8,128)(2,1)} custom-call(s32[8,5]{1,0:T(8,128)S(1)} %pad_add_fusion.table_ref, s32[1]{0:T(128)S(6)} %and.18.core_ref, bf16[8,144,128]{2,1,0:T(8,128)(2,1)S(1)} %all-to-all-done.own_ref, bf16[8,144,128]{2,1,0:T(8,128)(2,1)S(1)} %collective-permute-done.1.far_ref, bf16[4,256,128]{2,1,0:T(8,128)(2,1)S(1)} %after.1.refs_0_, ...), custom_call_target="tpu_custom_call" | custom-call | flops 700000000 | bytes 3000000 | tf_op jit(solution)/shard_map/page_reads/pallas_call | solution.py:36
  57.8 3.6 %all-to-all-start.1 = ((bf16[8,256,256]{2,1,0:T(8,128)(2,1)}), bf16[8,256,256]{2,1,0:T(8,128)(2,1)S(1)}, u32[]{:S(2)}, u32[]{:S(2)}) async-start(bf16[8,256,256]{2,1,0:T(8,128)(2,1)} %page_reads.1), calls=%async_computation.1 | async-start | bytes 2097152 | tf_op jit(solution)/shard_map/all_to_all | solution.py:591
  62.2 3.4 %scan_parts.1 = (f32[256,256]{1,0:T(8,128)S(1)}, f32[256,256]{1,0:T(8,128)S(1)}, f32[264,128]{1,0:T(8,128)S(1)}) custom-call(s32[1,16]{1,0:T(1,128)} %len_ref.7, s32[1,16]{1,0:T(1,128)} %res_ref.4, bf16[256,256]{1,0:T(8,128)(2,1)} %x_ref.3, bf16[256,256]{1,0:T(8,128)(2,1)} %z_ref.1, bf16[256,128]{1,0:T(8,128)(2,1)} %b_ref.1, bf16[256,128]{1,0:T(8,128)(2,1)} %c_ref.5, ...), custom_call_target="tpu_custom_call" | custom-call | flops 400000000 | bytes 2000000 | tf_op jit(solution)/shard_map/scan_parts/pallas_call | solution.py:36
  65.5 3.3 %collective-permute-start = (f32[264,128]{1,0:T(8,128)S(1)}, f32[264,128]{1,0:T(8,128)S(1)}, u32[]{:S(2)}, u32[]{:S(2)}) collective-permute-start(f32[264,128]{1,0:T(8,128)S(1)} %get-tuple-element.10), channel_id=1, source_target_pairs={{0,16},{16,32},{32,48},{48,64},{64,80},{80,96},{96,112},{112,128},... | collective-permute-start | bytes 405512 | tf_op jit(solution)/shard_map/ppermute | solution.py:502
  68.8 21.0 %collective-permute-done.carry_ref = f32[264,128]{1,0:T(8,128)S(1)} collective-permute-done((f32[264,128]{1,0:T(8,128)S(1)}, f32[264,128]{1,0:T(8,128)S(1)}, u32[]{:S(2)}, u32[]{:S(2)}) %collective-permute-start) | collective-permute-done | bytes 135200 | tf_op jit(solution)/shard_map/ppermute | solution.py:502
  89.8 2.8 %project.1 = (bf16[128,2176]{1,0:T(8,128)(2,1)S(1)}, bf16[128,2176]{1,0:T(8,128)(2,1)S(1)}) custom-call(s32[1,16]{1,0:T(1,128)} %len_ref.7, s32[1]{0:T(128)} %bitcast.2.group_ref, s32[1]{0:T(128)S(6)} %and.18.core_ref, bf16[256,128]{1,0:T(8,128)(2,1)} %c_ref.5, f32[264,128]{1,0:T(8,128)S(1)} %collective-permute-done.carry_ref, ...), custom_call_target="tpu_custom_call" | custom-call | flops 300000000 | bytes 3500000 | tf_op jit(solution)/shard_map/project/pallas_call | solution.py:36
  92.7 3.6 %collective-permute-start.5 = (bf16[128,2176]{1,0:T(8,128)(2,1)S(1)}, bf16[128,2176]{1,0:T(8,128)(2,1)S(1)}, u32[]{:S(2)}, u32[]{:S(2)}) collective-permute-start(bf16[128,2176]{1,0:T(8,128)(2,1)S(1)} %get-tuple-element.17), channel_id=1, source_target_pairs={{0,1},{1,0},{2,3},{3,2},{4,5},{5,4},{6,7},{7,6},{8,9},{9,8},{10,11... | collective-permute-start | bytes 1671176 | tf_op jit(solution)/shard_map/ppermute | solution.py:598
  96.3 1.6 collective-permute-done.5.b_ref
  99.0 6.9 %all-to-all-start.2 = ((bf16[8,16,2176]{2,1,0:T(8,128)(2,1)}), bf16[8,16,2176]{2,1,0:T(8,128)(2,1)S(1)}, u32[]{:S(2)}, u32[]{:S(2)}) async-start(bf16[8,16,2176]{2,1,0:T(8,128)(2,1)} %bitcast.12), calls=%async_computation.2 | async-start | bytes 1114112 | tf_op jit(solution)/shard_map/all_to_all | solution.py:599
  105.9 18.7 %all-to-all-done.2.recv_ref = bf16[8,16,2176]{2,1,0:T(8,128)(2,1)S(1)} async-done(((bf16[8,16,2176]{2,1,0:T(8,128)(2,1)}), bf16[8,16,2176]{2,1,0:T(8,128)(2,1)S(1)}, u32[]{:S(2)}, u32[]{:S(2)}) %all-to-all-start.2) | async-done | bytes 557088 | tf_op jit(solution)/shard_map/all_to_all | solution.py:599
  125.7 20.1 %all_to_all.25 = bf16[8,16,2048]{2,1,0:T(8,128)(2,1)S(1)} all-to-all(bf16[8,16,2048]{2,1,0:T(8,128)(2,1)S(1)} %norm_rows.1), channel_id=1, replica_groups={{0,2,4,6,8,10,12,14},{1,3,5,7,9,11,13,15},{16,18,20,22,24,26,28,30},{17..., dimensions={0} | all-to-all | bytes 1048576 | tf_op jit(solution)/shard_map/all_to_all | solution.py:604
  145.9 2.6 %collective-permute-start.6 = (bf16[128,2048]{1,0:T(8,128)(2,1)S(1)}, bf16[128,2048]{1,0:T(8,128)(2,1)S(1)}, u32[]{:S(2)}, u32[]{:S(2)}) collective-permute-start(bf16[128,2048]{1,0:T(8,128)(2,1)S(1)} %bitcast.18), channel_id=1, source_target_pairs={{0,1},{1,0},{2,3},{3,2},{4,5},{5,4},{6,7},{7,6},{8,9},{9,8},{10,11... | collective-permute-start | bytes 1572872 | tf_op jit(solution)/shard_map/ppermute | solution.py:608
  148.5 1.6 ref_norm.1.ref_ref
  150.2 3.2 %all-gather.2.cloned.1.call-done.head_ref = bf16[2048,3200]{1,0:T(8,128)(2,1)} async-done(((bf16[64,3200]{1,0:T(8,128)(2,1)}), bf16[2048,3200]{1,0:T(8,128)(2,1)}) %all-gather.2.cloned.1.call-update) | async-done | bytes 13107216 | tf_op jit(solution)/shard_map/all_gather | solution.py:549
  153.4 8.0 %scores.1 = f32[16,8,256]{2,1,0:T(8,128)S(1)} custom-call(s32[1]{0:T(128)} %bitcast.place_ref, s32[1]{0:T(128)S(6)} %and.18.core_ref, bf16[256,2048]{1,0:T(8,128)(2,1)S(1)} %ref_norm.1.ref_ref, bf16[128,2048]{1,0:T(8,128)(2,1)S(1)} %bitcast.19, bf16[128,2048]{1,0:T(8,128)(2,1)S(1)} %collective-permute-done.6.far_ref, ...), custom_call_target="tpu_custom_call" | custom-call | flops 3400000000 | bytes 15000000 | tf_op jit(solution)/shard_map/scores/pallas_call | solution.py:433
  161.4 16.8 %all_to_all.26.recv_ref = f32[16,8,256]{2,1,0:T(8,128)S(1)} all-to-all(f32[16,8,256]{2,1,0:T(8,128)S(1)} %scores.1), channel_id=1, replica_groups=mesh['grp'=32,'vocab'=16] {'vocab'}, dimensions={0} | all-to-all | bytes 262144 | tf_op jit(solution)/shard_map/all_to_all | solution.py:610
  (35 shorter events, 14.2 us)
Async XLA Ops:
  7.2 146.1 %copy-start = (s32[256]{0:T(256)S(1)}, s32[256]{0:T(256)}, u32[]{:S(2)}) copy-start(s32[256]{0:T(256)} %param.43) | copy-start | bytes 3076
  7.2 146.1 %all-gather.2.cloned.1.call-start = ((), (), s32[]{:S(2)}) async-start(), calls=%async_computation.5 | async-start | bytes 13516800 | tf_op jit(solution)/shard_map/all_gather | solution.py:549
  13.7 40.1 %collective-permute-start.2 = (bf16[4,256,128]{2,1,0:T(8,128)(2,1)S(1)}, bf16[4,256,128]{2,1,0:T(8,128)(2,1)S(1)}, u32[]{:S(2)}, u32[]{:S(2)}) collective-permute-start(bf16[4,256,128]{2,1,0:T(8,128)(2,1)S(1)} %after.1.refs_0_), channel_id=1, source_target_pairs={{0,128},{16,144},{32,160},{48,176},{64,192},{80,208},{96,224},{112... | collective-permute-start | bytes 786440 | tf_op jit(solution)/shard_map/ppermute | solution.py:563
  17.6 36.2 %collective-permute-start.3 = (bf16[4,256,128]{2,1,0:T(8,128)(2,1)S(1)}, bf16[4,256,128]{2,1,0:T(8,128)(2,1)S(1)}, u32[]{:S(2)}, u32[]{:S(2)}) collective-permute-start(bf16[4,256,128]{2,1,0:T(8,128)(2,1)S(1)} %after.1.refs_0_), channel_id=1, source_target_pairs={{0,256},{16,272},{32,288},{48,304},{64,320},{80,336},{96,352},{112... | collective-permute-start | bytes 786440 | tf_op jit(solution)/shard_map/ppermute | solution.py:563
  22.0 31.8 %collective-permute-start.4 = (bf16[4,256,128]{2,1,0:T(8,128)(2,1)S(1)}, bf16[4,256,128]{2,1,0:T(8,128)(2,1)S(1)}, u32[]{:S(2)}, u32[]{:S(2)}) collective-permute-start(bf16[4,256,128]{2,1,0:T(8,128)(2,1)S(1)} %after.1.refs_0_), channel_id=1, source_target_pairs={{0,384},{16,400},{32,416},{48,432},{64,448},{80,464},{96,480},{112... | collective-permute-start | bytes 786440 | tf_op jit(solution)/shard_map/ppermute | solution.py:563
  25.1 21.9 %all-to-all-start = ((bf16[8,144,128]{2,1,0:T(8,128)(2,1)}), bf16[8,144,128]{2,1,0:T(8,128)(2,1)S(1)}, u32[]{:S(2)}, u32[]{:S(2)}) async-start(bf16[8,144,128]{2,1,0:T(8,128)(2,1)} %send_rows.1._), calls=%async_computation | async-start | bytes 589824 | tf_op jit(solution)/shard_map/all_to_all | solution.py:556
  46.9 8.0 %collective-permute-start.1 = (bf16[8,144,128]{2,1,0:T(8,128)(2,1)S(1)}, bf16[8,144,128]{2,1,0:T(8,128)(2,1)S(1)}, u32[]{:S(2)}, u32[]{:S(2)}) collective-permute-start(bf16[8,144,128]{2,1,0:T(8,128)(2,1)S(1)} %all-to-all-done.own_ref), channel_id=1, source_target_pairs={{0,1},{1,0},{2,3},{3,2},{4,5},{5,4},{6,7},{7,6},{8,9},{9,8},{10,11... | collective-permute-start | bytes 884744 | tf_op jit(solution)/shard_map/ppermute | solution.py:559
  57.8 32.0 %all-to-all-start.1 = ((bf16[8,256,256]{2,1,0:T(8,128)(2,1)}), bf16[8,256,256]{2,1,0:T(8,128)(2,1)S(1)}, u32[]{:S(2)}, u32[]{:S(2)}) async-start(bf16[8,256,256]{2,1,0:T(8,128)(2,1)} %page_reads.1), calls=%async_computation.1 | async-start | bytes 2097152 | tf_op jit(solution)/shard_map/all_to_all | solution.py:591
  65.5 24.3 %collective-permute-start = (f32[264,128]{1,0:T(8,128)S(1)}, f32[264,128]{1,0:T(8,128)S(1)}, u32[]{:S(2)}, u32[]{:S(2)}) collective-permute-start(f32[264,128]{1,0:T(8,128)S(1)} %get-tuple-element.10), channel_id=1, source_target_pairs={{0,16},{16,32},{32,48},{48,64},{64,80},{80,96},{96,112},{112,128},... | collective-permute-start | bytes 405512 | tf_op jit(solution)/shard_map/ppermute | solution.py:502
  92.7 5.2 %collective-permute-start.5 = (bf16[128,2176]{1,0:T(8,128)(2,1)S(1)}, bf16[128,2176]{1,0:T(8,128)(2,1)S(1)}, u32[]{:S(2)}, u32[]{:S(2)}) collective-permute-start(bf16[128,2176]{1,0:T(8,128)(2,1)S(1)} %get-tuple-element.17), channel_id=1, source_target_pairs={{0,1},{1,0},{2,3},{3,2},{4,5},{5,4},{6,7},{7,6},{8,9},{9,8},{10,11... | collective-permute-start | bytes 1671176 | tf_op jit(solution)/shard_map/ppermute | solution.py:598
  99.0 25.6 %all-to-all-start.2 = ((bf16[8,16,2176]{2,1,0:T(8,128)(2,1)}), bf16[8,16,2176]{2,1,0:T(8,128)(2,1)S(1)}, u32[]{:S(2)}, u32[]{:S(2)}) async-start(bf16[8,16,2176]{2,1,0:T(8,128)(2,1)} %bitcast.12), calls=%async_computation.2 | async-start | bytes 1114112 | tf_op jit(solution)/shard_map/all_to_all | solution.py:599
  145.9 4.3 %collective-permute-start.6 = (bf16[128,2048]{1,0:T(8,128)(2,1)S(1)}, bf16[128,2048]{1,0:T(8,128)(2,1)S(1)}, u32[]{:S(2)}, u32[]{:S(2)}) collective-permute-start(bf16[128,2048]{1,0:T(8,128)(2,1)S(1)} %bitcast.18), channel_id=1, source_target_pairs={{0,1},{1,0},{2,3},{3,2},{4,5},{5,4},{6,7},{7,6},{8,9},{9,8},{10,11... | collective-permute-start | bytes 1572872 | tf_op jit(solution)/shard_map/ppermute | solution.py:608
Sparse Core Ops, SparseCore 0:
  11.2 142.0 all-gather.1

commit v7 on v4

--- a/solution.py
+++ b/solution.py
@@ -549,7 +549,7 @@
 
     asking = send_rows(page_owner, lengths, resumed, my_group, core, state_c, ring)
     asking, page_owner, page_slot = lax.optimization_barrier((asking, page_owner, page_slot))
-    saved_pages = after(asking, settled(saved_pages))
+    saved_pages = settled(saved_pages)
     asking = lax.all_to_all(
         asking, "grp", split_axis=0, concat_axis=0, tiled=True, axis_index_groups=lines
     )

time: 187 us -> 187 us (level)
  waiting for transfers between devices: 50.7 us -> 53.4 us
  starting transfers between devices: 48.2 us -> 45.9 us
    all_to_all x1, waiting for transfers between devices: 5.21 us -> 8.03 us  [body(): lax.all_to_all(asking, 'grp', split_axis=0, concat_axis=0, tiled=True, ax...]
    ppermute x1, starting transfers between devices: 6.78 us -> 4.72 us  [body(): far_asking = lax.ppermute(asking, 'vocab', other)]
    all_gather x1, waiting for transfers between devices: 3.15 us -> 1.25 us  [body(): lax.all_gather(jnp.concatenate([ref_head, policy_head, spare], axis=1), '...]
where the time goes in v7:
time: 187 us; the launch traced here: 186 us
  waiting for transfers between devices  53.4 us (29%)
  starting transfers between devices  45.9 us (25%)
  blocking collectives  36.5 us (20%)
  Pallas kernels  26 us (14%)
  between operations  14.2 us (8%)
  local copies, waits for them, and re-layouts  7.98 us (4%)
  other arithmetic  2.26 us (1%)
    ppermute x1, waiting for transfers between devices, from_behind(): return lax.ppermute(x, axis, pairs)  22.8 us
    all_to_all x1, blocking collectives, body(): lax.all_to_all(mine, 'vocab', split_axis=0, concat_axis=0, tiled=True, ax...  20.1 us
    all_to_all x1, waiting for transfers between devices, body(): lax.all_to_all(summed.reshape(parts // 2, tokens // parts, -1), 'vocab',...  18.7 us
    pallas_call x7, Pallas kernels, call(): pl.pallas_call(kernel, out_shape=outs, grid_spec=pltpu.PrefetchScalarGrid...  17.2 us
    all_to_all x1, blocking collectives, body(): lax.all_to_all(stats, 'vocab', split_axis=0, concat_axis=0, tiled=True)  16.4 us
    ppermute x3, starting transfers between devices, body(): pages.append(lax.ppermute(saved_pages, 'grp', pairs))  11.4 us
    all_to_all x1, starting transfers between devices, body(): lax.all_to_all(asking, 'grp', split_axis=0, concat_axis=0, tiled=True, ax...  10 us
    all_to_all x1, waiting for transfers between devices, body(): lax.all_to_all(asking, 'grp', split_axis=0, concat_axis=0, tiled=True, ax...  8.03 us
  transfers between devices with their start and end apart: 11, of which 6 were waited for; matrix products, arithmetic and copies ran while one was open for 4% of the time, Pallas kernels for 9%

profile of v7, /device:TPU:1, one launch (start us, length us, event | category | flops | bytes accessed | tf_op | source)
XLA Modules:
  0.0 186.3 jit_solution(22168425537779893)
XLA Ops:
  7.2 2.0 %concatenate.15 = bf16[64,3200]{1,0:T(8,128)(2,1)} concatenate(bf16[64,1576]{1,0:T(8,128)(2,1)} %param.37, bf16[64,1576]{1,0:T(8,128)(2,1)} %param.36, bf16[64,48]{1,0:T(8,128)(2,1)S(1)} %broadcast_in_dim.59), dimensions={1} | concatenate | bytes 819200 | tf_op jit(solution)/shard_map/concatenate | solution.py:547
  9.2 4.0 %collective-permute-start.2 = (bf16[4,256,128]{2,1,0:T(8,128)(2,1)}, bf16[4,256,128]{2,1,0:T(8,128)(2,1)S(1)}, u32[]{:S(2)}, u32[]{:S(2)}) collective-permute-start(bf16[4,256,128]{2,1,0:T(8,128)(2,1)} %refs_0_.1), channel_id=1, source_target_pairs={{0,128},{16,144},{32,160},{48,176},{64,192},{80,208},{96,224},{112... | collective-permute-start | bytes 786440 | tf_op jit(solution)/shard_map/ppermute | solution.py:560
  13.2 4.4 %collective-permute-start.3 = (bf16[4,256,128]{2,1,0:T(8,128)(2,1)}, bf16[4,256,128]{2,1,0:T(8,128)(2,1)S(1)}, u32[]{:S(2)}, u32[]{:S(2)}) collective-permute-start(bf16[4,256,128]{2,1,0:T(8,128)(2,1)} %refs_0_.1), channel_id=1, source_target_pairs={{0,256},{16,272},{32,288},{48,304},{64,320},{80,336},{96,352},{112... | collective-permute-start | bytes 786440 | tf_op jit(solution)/shard_map/ppermute | solution.py:560
  17.6 3.1 %collective-permute-start.4 = (bf16[4,256,128]{2,1,0:T(8,128)(2,1)}, bf16[4,256,128]{2,1,0:T(8,128)(2,1)S(1)}, u32[]{:S(2)}, u32[]{:S(2)}) collective-permute-start(bf16[4,256,128]{2,1,0:T(8,128)(2,1)} %refs_0_.1), channel_id=1, source_target_pairs={{0,384},{16,400},{32,416},{48,432},{64,448},{80,464},{96,480},{112... | collective-permute-start | bytes 786440 | tf_op jit(solution)/shard_map/ppermute | solution.py:560
  21.4 2.7 %send_rows.1 = bf16[8,144,128]{2,1,0:T(8,128)(2,1)} custom-call(s32[32,16]{1,0:T(8,128)S(1)} %copy.28.own_ref, s32[1,16]{1,0:T(1,128)} %len_ref.7, s32[1,16]{1,0:T(1,128)} %res_ref.4, s32[1]{0:T(128)} %bitcast.2.group_ref, s32[1]{0:T(128)S(6)} %and.18.core_ref, bf16[256,128]{1,0:T(8,128)(2,1)} %c_ref.5), custom_call_target="tpu_custom_call" | custom-call | flops 100000 | bytes 700000 | tf_op jit(solution)/shard_map/send_rows/pallas_call | solution.py:36
  24.1 10.0 %all-to-all-start = ((bf16[8,144,128]{2,1,0:T(8,128)(2,1)}), bf16[8,144,128]{2,1,0:T(8,128)(2,1)S(1)}, u32[]{:S(2)}, u32[]{:S(2)}) async-start(bf16[8,144,128]{2,1,0:T(8,128)(2,1)} %send_rows.1), calls=%async_computation | async-start | bytes 589824 | tf_op jit(solution)/shard_map/all_to_all | solution.py:553
  40.7 8.0 %all-to-all-done.own_ref = bf16[8,144,128]{2,1,0:T(8,128)(2,1)S(1)} async-done(((bf16[8,144,128]{2,1,0:T(8,128)(2,1)}), bf16[8,144,128]{2,1,0:T(8,128)(2,1)S(1)}, u32[]{:S(2)}, u32[]{:S(2)}) %all-to-all-start) | async-done | bytes 294944 | tf_op jit(solution)/shard_map/all_to_all | solution.py:553
  48.7 4.7 %collective-permute-start.1 = (bf16[8,144,128]{2,1,0:T(8,128)(2,1)S(1)}, bf16[8,144,128]{2,1,0:T(8,128)(2,1)S(1)}, u32[]{:S(2)}, u32[]{:S(2)}) collective-permute-start(bf16[8,144,128]{2,1,0:T(8,128)(2,1)S(1)} %all-to-all-done.own_ref), channel_id=1, source_target_pairs={{0,1},{1,0},{2,3},{3,2},{4,5},{5,4},{6,7},{7,6},{8,9},{9,8},{10,11... | collective-permute-start | bytes 884744 | tf_op jit(solution)/shard_map/ppermute | solution.py:556
  54.6 4.1 %page_reads.1 = bf16[8,256,256]{2,1,0:T(8,128)(2,1)} custom-call(s32[8,5]{1,0:T(8,128)S(1)} %pad_add_fusion.table_ref, s32[1]{0:T(128)S(6)} %and.18.core_ref, bf16[8,144,128]{2,1,0:T(8,128)(2,1)S(1)} %all-to-all-done.own_ref, bf16[8,144,128]{2,1,0:T(8,128)(2,1)S(1)} %collective-permute-done.1.far_ref, bf16[4,256,128]{2,1,0:T(8,128)(2,1)} %refs_0_.1, ...), custom_call_target="tpu_custom_call" | custom-call | flops 700000000 | bytes 3000000 | tf_op jit(solution)/shard_map/page_reads/pallas_call | solution.py:36
  58.7 3.6 %all-to-all-start.1 = ((bf16[8,256,256]{2,1,0:T(8,128)(2,1)}), bf16[8,256,256]{2,1,0:T(8,128)(2,1)S(1)}, u32[]{:S(2)}, u32[]{:S(2)}) async-start(bf16[8,256,256]{2,1,0:T(8,128)(2,1)} %page_reads.1), calls=%async_computation.1 | async-start | bytes 2097152 | tf_op jit(solution)/shard_map/all_to_all | solution.py:588
  63.1 3.4 %scan_parts.1 = (f32[256,256]{1,0:T(8,128)S(1)}, f32[256,256]{1,0:T(8,128)S(1)}, f32[264,128]{1,0:T(8,128)S(1)}) custom-call(s32[1,16]{1,0:T(1,128)} %len_ref.7, s32[1,16]{1,0:T(1,128)} %res_ref.4, bf16[256,256]{1,0:T(8,128)(2,1)} %x_ref.3, bf16[256,256]{1,0:T(8,128)(2,1)} %z_ref.1, bf16[256,128]{1,0:T(8,128)(2,1)} %b_ref.1, bf16[256,128]{1,0:T(8,128)(2,1)} %c_ref.5, ...), custom_call_target="tpu_custom_call" | custom-call | flops 400000000 | bytes 2000000 | tf_op jit(solution)/shard_map/scan_parts/pallas_call | solution.py:36
  66.5 3.3 %collective-permute-start = (f32[264,128]{1,0:T(8,128)S(1)}, f32[264,128]{1,0:T(8,128)S(1)}, u32[]{:S(2)}, u32[]{:S(2)}) collective-permute-start(f32[264,128]{1,0:T(8,128)S(1)} %get-tuple-element.10), channel_id=1, source_target_pairs={{0,16},{16,32},{32,48},{48,64},{64,80},{80,96},{96,112},{112,128},... | collective-permute-start | bytes 405512 | tf_op jit(solution)/shard_map/ppermute | solution.py:499
  69.7 22.8 %collective-permute-done.carry_ref = f32[264,128]{1,0:T(8,128)S(1)} collective-permute-done((f32[264,128]{1,0:T(8,128)S(1)}, f32[264,128]{1,0:T(8,128)S(1)}, u32[]{:S(2)}, u32[]{:S(2)}) %collective-permute-start) | collective-permute-done | bytes 135200 | tf_op jit(solution)/shard_map/ppermute | solution.py:499
  92.6 2.8 %project.1 = (bf16[128,2176]{1,0:T(8,128)(2,1)S(1)}, bf16[128,2176]{1,0:T(8,128)(2,1)S(1)}) custom-call(s32[1,16]{1,0:T(1,128)} %len_ref.7, s32[1]{0:T(128)} %bitcast.2.group_ref, s32[1]{0:T(128)S(6)} %and.18.core_ref, bf16[256,128]{1,0:T(8,128)(2,1)} %c_ref.5, f32[264,128]{1,0:T(8,128)S(1)} %collective-permute-done.carry_ref, ...), custom_call_target="tpu_custom_call" | custom-call | flops 300000000 | bytes 3500000 | tf_op jit(solution)/shard_map/project/pallas_call | solution.py:36
  95.4 2.8 %collective-permute-start.5 = (bf16[128,2176]{1,0:T(8,128)(2,1)S(1)}, bf16[128,2176]{1,0:T(8,128)(2,1)S(1)}, u32[]{:S(2)}, u32[]{:S(2)}) collective-permute-start(bf16[128,2176]{1,0:T(8,128)(2,1)S(1)} %get-tuple-element.17), channel_id=1, source_target_pairs={{0,1},{1,0},{2,3},{3,2},{4,5},{5,4},{6,7},{7,6},{8,9},{9,8},{10,11... | collective-permute-start | bytes 1671176 | tf_op jit(solution)/shard_map/ppermute | solution.py:595
  98.2 1.6 collective-permute-done.5.b_ref
  101.0 7.5 %all-to-all-start.2 = ((bf16[8,16,2176]{2,1,0:T(8,128)(2,1)}), bf16[8,16,2176]{2,1,0:T(8,128)(2,1)S(1)}, u32[]{:S(2)}, u32[]{:S(2)}) async-start(bf16[8,16,2176]{2,1,0:T(8,128)(2,1)} %bitcast.12), calls=%async_computation.2 | async-start | bytes 1114112 | tf_op jit(solution)/shard_map/all_to_all | solution.py:596
  108.5 18.7 %all-to-all-done.2.recv_ref = bf16[8,16,2176]{2,1,0:T(8,128)(2,1)S(1)} async-done(((bf16[8,16,2176]{2,1,0:T(8,128)(2,1)}), bf16[8,16,2176]{2,1,0:T(8,128)(2,1)S(1)}, u32[]{:S(2)}, u32[]{:S(2)}) %all-to-all-start.2) | async-done | bytes 557088 | tf_op jit(solution)/shard_map/all_to_all | solution.py:596
  128.3 20.1 %all_to_all.25 = bf16[8,16,2048]{2,1,0:T(8,128)(2,1)S(1)} all-to-all(bf16[8,16,2048]{2,1,0:T(8,128)(2,1)S(1)} %norm_rows.1), channel_id=1, replica_groups={{0,2,4,6,8,10,12,14},{1,3,5,7,9,11,13,15},{16,18,20,22,24,26,28,30},{17..., dimensions={0} | all-to-all | bytes 1048576 | tf_op jit(solution)/shard_map/all_to_all | solution.py:601
  148.4 2.6 %collective-permute-start.6 = (bf16[128,2048]{1,0:T(8,128)(2,1)S(1)}, bf16[128,2048]{1,0:T(8,128)(2,1)S(1)}, u32[]{:S(2)}, u32[]{:S(2)}) collective-permute-start(bf16[128,2048]{1,0:T(8,128)(2,1)S(1)} %bitcast.18), channel_id=1, source_target_pairs={{0,1},{1,0},{2,3},{3,2},{4,5},{5,4},{6,7},{7,6},{8,9},{9,8},{10,11... | collective-permute-start | bytes 1572872 | tf_op jit(solution)/shard_map/ppermute | solution.py:605
  151.0 1.6 ref_norm.1.ref_ref
  154.0 7.6 %scores.1 = f32[16,8,256]{2,1,0:T(8,128)S(1)} custom-call(s32[1]{0:T(128)} %bitcast.place_ref, s32[1]{0:T(128)S(6)} %and.18.core_ref, bf16[256,2048]{1,0:T(8,128)(2,1)S(1)} %ref_norm.1.ref_ref, bf16[128,2048]{1,0:T(8,128)(2,1)S(1)} %bitcast.19, bf16[128,2048]{1,0:T(8,128)(2,1)S(1)} %collective-permute-done.6.far_ref, ...), custom_call_target="tpu_custom_call" | custom-call | flops 3400000000 | bytes 15000000 | tf_op jit(solution)/shard_map/scores/pallas_call | solution.py:430
  161.6 16.4 %all_to_all.26.recv_ref = f32[16,8,256]{2,1,0:T(8,128)S(1)} all-to-all(f32[16,8,256]{2,1,0:T(8,128)S(1)} %scores.1), channel_id=1, replica_groups=mesh['grp'=32,'vocab'=16] {'vocab'}, dimensions={0} | all-to-all | bytes 262144 | tf_op jit(solution)/shard_map/all_to_all | solution.py:607
  178.0 1.4 finish.1
  (40 shorter events, 13.0 us)
Async XLA Ops:
  7.2 146.8 %copy-start.3 = (s32[256]{0:T(256)S(1)}, s32[256]{0:T(256)}, u32[]{:S(2)}) copy-start(s32[256]{0:T(256)} %param.43) | copy-start | bytes 3076
  7.2 146.7 %all-gather.2.cloned.1.call-start = ((), (), s32[]{:S(2)}) async-start(), calls=%async_computation.5 | async-start | bytes 13516800 | tf_op jit(solution)/shard_map/all_gather | solution.py:546
  9.2 44.3 %collective-permute-start.2 = (bf16[4,256,128]{2,1,0:T(8,128)(2,1)}, bf16[4,256,128]{2,1,0:T(8,128)(2,1)S(1)}, u32[]{:S(2)}, u32[]{:S(2)}) collective-permute-start(bf16[4,256,128]{2,1,0:T(8,128)(2,1)} %refs_0_.1), channel_id=1, source_target_pairs={{0,128},{16,144},{32,160},{48,176},{64,192},{80,208},{96,224},{112... | collective-permute-start | bytes 786440 | tf_op jit(solution)/shard_map/ppermute | solution.py:560
  13.2 40.3 %collective-permute-start.3 = (bf16[4,256,128]{2,1,0:T(8,128)(2,1)}, bf16[4,256,128]{2,1,0:T(8,128)(2,1)S(1)}, u32[]{:S(2)}, u32[]{:S(2)}) collective-permute-start(bf16[4,256,128]{2,1,0:T(8,128)(2,1)} %refs_0_.1), channel_id=1, source_target_pairs={{0,256},{16,272},{32,288},{48,304},{64,320},{80,336},{96,352},{112... | collective-permute-start | bytes 786440 | tf_op jit(solution)/shard_map/ppermute | solution.py:560
  17.6 36.0 %collective-permute-start.4 = (bf16[4,256,128]{2,1,0:T(8,128)(2,1)}, bf16[4,256,128]{2,1,0:T(8,128)(2,1)S(1)}, u32[]{:S(2)}, u32[]{:S(2)}) collective-permute-start(bf16[4,256,128]{2,1,0:T(8,128)(2,1)} %refs_0_.1), channel_id=1, source_target_pairs={{0,384},{16,400},{32,416},{48,432},{64,448},{80,464},{96,480},{112... | collective-permute-start | bytes 786440 | tf_op jit(solution)/shard_map/ppermute | solution.py:560
  24.1 24.6 %all-to-all-start = ((bf16[8,144,128]{2,1,0:T(8,128)(2,1)}), bf16[8,144,128]{2,1,0:T(8,128)(2,1)S(1)}, u32[]{:S(2)}, u32[]{:S(2)}) async-start(bf16[8,144,128]{2,1,0:T(8,128)(2,1)} %send_rows.1), calls=%async_computation | async-start | bytes 589824 | tf_op jit(solution)/shard_map/all_to_all | solution.py:553
  48.7 5.9 %collective-permute-start.1 = (bf16[8,144,128]{2,1,0:T(8,128)(2,1)S(1)}, bf16[8,144,128]{2,1,0:T(8,128)(2,1)S(1)}, u32[]{:S(2)}, u32[]{:S(2)}) collective-permute-start(bf16[8,144,128]{2,1,0:T(8,128)(2,1)S(1)} %all-to-all-done.own_ref), channel_id=1, source_target_pairs={{0,1},{1,0},{2,3},{3,2},{4,5},{5,4},{6,7},{7,6},{8,9},{9,8},{10,11... | collective-permute-start | bytes 884744 | tf_op jit(solution)/shard_map/ppermute | solution.py:556
  53.5 1.1 copy-start
  53.5 1.1 copy-start.1
  53.6 1.1 copy-start.2
  58.7 33.9 %all-to-all-start.1 = ((bf16[8,256,256]{2,1,0:T(8,128)(2,1)}), bf16[8,256,256]{2,1,0:T(8,128)(2,1)S(1)}, u32[]{:S(2)}, u32[]{:S(2)}) async-start(bf16[8,256,256]{2,1,0:T(8,128)(2,1)} %page_reads.1), calls=%async_computation.1 | async-start | bytes 2097152 | tf_op jit(solution)/shard_map/all_to_all | solution.py:588
  66.5 26.1 %collective-permute-start = (f32[264,128]{1,0:T(8,128)S(1)}, f32[264,128]{1,0:T(8,128)S(1)}, u32[]{:S(2)}, u32[]{:S(2)}) collective-permute-start(f32[264,128]{1,0:T(8,128)S(1)} %get-tuple-element.10), channel_id=1, source_target_pairs={{0,16},{16,32},{32,48},{48,64},{64,80},{80,96},{96,112},{112,128},... | collective-permute-start | bytes 405512 | tf_op jit(solution)/shard_map/ppermute | solution.py:499
  95.4 4.4 %collective-permute-start.5 = (bf16[128,2176]{1,0:T(8,128)(2,1)S(1)}, bf16[128,2176]{1,0:T(8,128)(2,1)S(1)}, u32[]{:S(2)}, u32[]{:S(2)}) collective-permute-start(bf16[128,2176]{1,0:T(8,128)(2,1)S(1)} %get-tuple-element.17), channel_id=1, source_target_pairs={{0,1},{1,0},{2,3},{3,2},{4,5},{5,4},{6,7},{7,6},{8,9},{9,8},{10,11... | collective-permute-start | bytes 1671176 | tf_op jit(solution)/shard_map/ppermute | solution.py:595
  101.0 26.2 %all-to-all-start.2 = ((bf16[8,16,2176]{2,1,0:T(8,128)(2,1)}), bf16[8,16,2176]{2,1,0:T(8,128)(2,1)S(1)}, u32[]{:S(2)}, u32[]{:S(2)}) async-start(bf16[8,16,2176]{2,1,0:T(8,128)(2,1)} %bitcast.12), calls=%async_computation.2 | async-start | bytes 1114112 | tf_op jit(solution)/shard_map/all_to_all | solution.py:596
  148.4 4.3 %collective-permute-start.6 = (bf16[128,2048]{1,0:T(8,128)(2,1)S(1)}, bf16[128,2048]{1,0:T(8,128)(2,1)S(1)}, u32[]{:S(2)}, u32[]{:S(2)}) collective-permute-start(bf16[128,2048]{1,0:T(8,128)(2,1)S(1)} %bitcast.18), channel_id=1, source_target_pairs={{0,1},{1,0},{2,3},{3,2},{4,5},{5,4},{6,7},{7,6},{8,9},{9,8},{10,11... | collective-permute-start | bytes 1572872 | tf_op jit(solution)/shard_map/ppermute | solution.py:605
Sparse Core Ops, SparseCore 0:
  11.2 142.6 all-gather.1
